TPU v7x, 256 devices: a whole 4x4x8 slice. The times are simulated.
256 devices in a mesh: px: 16 (over z, y_hi), py: 16 (over x, y_lo, core).
Axes of the slice: x: 4, y: 4 (y_hi: 2, y_lo: 2; y = y_hi * 2 + y_lo), z: 8, core: 2. Of those that a mesh axis runs over, the one named last changes fastest.
Arguments:
- estimate: float32 [512, 512, 128], P('px', 'py'), may hold values from 0.2 to 5
- observed: float32 [512, 512, 128], P('px', 'py'), may hold values from 0.2 to 5
- psf: float32 [32, 32, 32], replicated, as said below
Outputs:
- updated: float32 [512, 512, 128], P('px', 'py')
Inputs may be any that keep to these rules, and one draw needn't show every extreme that they name: `psf`: every entry is positive.
All inputs are finite; a program needn't handle non-finite values.
Results may differ from a plain program's by a relative error of at most 0.00009.
Values sent between devices are 32-bit elements; how exact they have to be, the bound alone decides.
No kernel may reach another device: no remote copies, remote signals or barrier semaphores. Data moves between devices by JAX's collectives and lax.ppermute only.
A program may use at most 128 MiB of HBM per device.

v0:
```python
import math

import jax
import jax.numpy as jnp
from jax import lax
from jax.sharding import PartitionSpec as P

NX = 512
NY = 512


penalty_weight = 0.1
smoothing = 0.1


def with_halo(block, sides, width):
    for axis, dim in sides:
        count = lax.axis_size(axis)
        forward = [(i, i + 1) for i in range(count - 1)]
        backward = [(target, source) for source, target in forward]
        low = lax.ppermute(
            lax.slice_in_dim(block, block.shape[dim] - width, None, axis=dim), axis, forward
        )
        high = lax.ppermute(lax.slice_in_dim(block, 0, width, axis=dim), axis, backward)
        block = jnp.concatenate([low, block, high], axis=dim)
    return block


def product(pattern, left, right):
    return jnp.einsum(pattern, left, right, precision=lax.Precision.HIGHEST)


def tables(length):
    indices = jnp.arange(length)
    turns = jnp.remainder(indices[:, None] * indices[None, :], length).astype(jnp.float32) * (
        2.0 * math.pi / length
    )
    return (jnp.cos(turns), jnp.sin(turns))


def offset_tables(offsets, frequency, length):
    turns = jnp.remainder(offsets[:, None] * frequency[None, :], length).astype(jnp.float32) * (
        2.0 * math.pi / length
    )
    return (jnp.cos(turns), jnp.sin(turns))


def complex_apply(real_part, imag_part, cosine, sines, pattern, forward):
    real_cos = product(pattern, real_part, cosine)
    real_sin = product(pattern, real_part, sines)
    imag_cos = product(pattern, imag_part, cosine)
    imag_sin = product(pattern, imag_part, sines)
    if forward:
        return (real_cos + imag_sin, imag_cos - real_sin)
    return (real_cos - imag_sin, imag_cos + real_sin)


def transfer_function(
    kernel, first_index, second_index, depth_share, first_share, second_whole, first_whole, depth
):
    length = kernel.shape[0]
    offsets = jnp.arange(length) - length // 2
    depth_freq = first_index * depth_share + jnp.arange(depth_share)
    first_freq = second_index * first_share + jnp.arange(first_share)
    second_freq = jnp.arange(second_whole)
    cosine, sines = offset_tables(offsets, depth_freq, depth)
    real_part = product("baz,zk->bak", kernel, cosine)
    imag_part = -product("baz,zk->bak", kernel, sines)
    cosine, sines = offset_tables(offsets, first_freq, first_whole)
    real_part, imag_part = complex_apply(real_part, imag_part, cosine, sines, "baz,aj->bzj", True)
    cosine, sines = offset_tables(offsets, second_freq, second_whole)
    real_part, imag_part = complex_apply(real_part, imag_part, cosine, sines, "bzj,bm->zjm", True)
    factor = 1.0 / (first_whole * second_whole * depth)
    return (real_part * factor, imag_part * factor)


def outward_one(spectrum, handler):
    result = handler(lax.all_to_all(spectrum, "py", split_axis=2, concat_axis=3, tiled=True))
    return result


def outward_two(spectrum):
    result = lax.all_to_all(spectrum, "px", split_axis=2, concat_axis=3, tiled=True)
    return result


def homeward_two(spectrum, handler):
    result = handler(lax.all_to_all(spectrum, "px", split_axis=3, concat_axis=2, tiled=True))
    return result


def homeward_one(spectrum, handler):
    result = handler(lax.all_to_all(spectrum, "py", split_axis=3, concat_axis=2, tiled=True))
    return result


def along_first(segment):
    cosine, sines = tables(segment.shape[3])
    real_part, imag_part = complex_apply(segment[0], segment[1], cosine, sines, "bza,ak->zkb", True)
    return jnp.stack([real_part, imag_part])


def inverse_first(segment):
    cosine, sines = tables(segment.shape[2])
    real_part, imag_part = complex_apply(
        segment[0], segment[1], cosine, sines, "zab,ak->bzk", False
    )
    return jnp.stack([real_part, imag_part])


def to_real(segment):
    cosine, sines = tables(segment.shape[2])
    return product("bza,zk->bak", segment[0], cosine) - product("bza,zk->bak", segment[1], sines)


def convolve(volume, transfer_real, transfer_imag, adjoint):
    cosine, sines = tables(volume.shape[2])
    spectrum = jnp.stack(
        [product("baz,zk->bka", volume, cosine), -product("baz,zk->bka", volume, sines)]
    )
    spectrum = outward_one(spectrum, along_first)
    spectrum = outward_two(spectrum)
    cosine_second, sines_second = tables(spectrum.shape[3])
    real_part, imag_part = complex_apply(
        spectrum[0], spectrum[1], cosine_second, sines_second, "zab,bk->zak", True
    )
    signed_imag = -transfer_imag if adjoint else transfer_imag
    weighted_real = real_part * transfer_real - imag_part * signed_imag
    weighted_imag = real_part * signed_imag + imag_part * transfer_real
    real_part, imag_part = complex_apply(
        weighted_real, weighted_imag, cosine_second, sines_second, "zab,bk->zak", False
    )
    spectrum = homeward_two(jnp.stack([real_part, imag_part]), inverse_first)
    return homeward_one(spectrum, to_real)


def backward_depth(flux):
    return flux - jnp.concatenate([jnp.zeros_like(flux[:, :, :1]), flux[:, :, :-1]], 2)


def normalized(slope_rows, slope_cols, slope_depth):
    factor = lax.rsqrt(
        slope_rows * slope_rows
        + slope_cols * slope_cols
        + slope_depth * slope_depth
        + smoothing * smoothing
    )
    return (slope_rows * factor, slope_cols * factor, slope_depth * factor)


def variation(volume):
    row_count = volume.shape[0]
    col_count = volume.shape[1]
    padded = with_halo(volume, (("px", 0), ("py", 1)), 1)
    region = padded[:-1, :-1]
    slope_rows = padded[1:, :-1] - region
    slope_cols = padded[:-1, 1:] - region
    row_global = lax.axis_index("px") * row_count - 1 + jnp.arange(row_count + 1)
    col_global = lax.axis_index("py") * col_count - 1 + jnp.arange(col_count + 1)
    row_valid = ((row_global >= 0) & (row_global <= NX - 2))[:, None, None]
    col_valid = ((col_global >= 0) & (col_global <= NY - 2))[None, :, None]
    slope_rows = jnp.where(row_valid, slope_rows, 0.0)
    slope_cols = jnp.where(col_valid, slope_cols, 0.0)
    slope_depth = jnp.concatenate(
        [region[:, :, 1:] - region[:, :, :-1], jnp.zeros_like(region[:, :, :1])], 2
    )
    flux_rows, flux_cols, flux_depth = normalized(slope_rows, slope_cols, slope_depth)
    divergence = (
        flux_rows[1:, 1:]
        - flux_rows[:-1, 1:]
        + (flux_cols[1:, 1:] - flux_cols[1:, :-1])
        + backward_depth(flux_depth[1:, 1:])
    )
    return divergence


def shards(estimate, observed, psf):
    first_index = lax.axis_index("py")
    second_index = lax.axis_index("px")
    first_size = lax.axis_size("py")
    second_size = lax.axis_size("px")
    second_local, first_local, depth = estimate.shape
    first_whole = first_local * first_size
    second_whole = second_local * second_size
    transfer_real, transfer_imag = transfer_function(
        psf,
        first_index,
        second_index,
        depth // first_size,
        first_whole // second_size,
        second_whole,
        first_whole,
        depth,
    )
    blurred = convolve(estimate, transfer_real, transfer_imag, False)
    quotient = observed / blurred
    correction = convolve(quotient, transfer_real, transfer_imag, True)
    divergence = variation(estimate)
    return estimate * correction / (1.0 - penalty_weight * divergence)


def solution(mesh):
    placed = (P("px", "py", None), P("px", "py", None), P())
    return jax.shard_map(
        shards, mesh=mesh, in_specs=placed, out_specs=P("px", "py", None), check_vma=False
    )
```

profile of v0, /device:TPU:1, one launch (start us, length us, event | category | flops | bytes accessed | tf_op | source)
XLA Modules:
  0.0 613.1 jit_solution(9039552779921789667)
XLA Ops:
  13.1 7.1 %all-to-all-start = ((f32[16,1,16384]{2,1,0:T(1,128)}), f32[16,1,16384]{2,1,0:T(1,128)S(1)}, u32[]{:S(2)}, u32[]{:S(2)}) async-start(f32[16,1,16384]{2,1,0:T(1,128)} %reshape.84), calls=%async_computation | async-start | bytes 2097152 | tf_op jit(solution)/shard_map/all_to_all | solution.py:78
  22.4 13.4 %all-to-all-done = f32[16,1,16384]{2,1,0:T(1,128)S(1)} async-done(((f32[16,1,16384]{2,1,0:T(1,128)}), f32[16,1,16384]{2,1,0:T(1,128)S(1)}, u32[]{:S(2)}, u32[]{:S(2)}) %all-to-all-start) | async-done | bytes 1048608 | tf_op jit(solution)/shard_map/all_to_all | solution.py:78
  49.8 6.0 fusion.59
  57.9 6.5 %fusion.57 = f32[512,32,8]{0,1,2:T(8,128)S(1)} fusion(f32[32,8,512]{2,0,1:T(8,128)} %squeeze.49), kind=kOutput, calls=%fused_computation.103 | convolution fusion | flops 808976384 | bytes 1048576 | tf_op jit(solution)/shard_map/bza,ak->zkb/dot_general | solution.py:30
  83.7 11.0 %all-to-all-start.1 = ((f32[16,1,16384]{2,1,0:T(1,128)}), f32[16,1,16384]{2,1,0:T(1,128)S(1)}, u32[]{:S(2)}, u32[]{:S(2)}) async-start(f32[16,1,16384]{2,1,0:T(1,128)} %reshape.86), calls=%async_computation.1 | async-start | bytes 2097152 | tf_op jit(solution)/shard_map/all_to_all | solution.py:83
  103.6 17.6 %all-to-all-done.1 = f32[16,1,16384]{2,1,0:T(1,128)S(1)} async-done(((f32[16,1,16384]{2,1,0:T(1,128)}), f32[16,1,16384]{2,1,0:T(1,128)S(1)}, u32[]{:S(2)}, u32[]{:S(2)}) %all-to-all-start.1) | async-done | bytes 1048608 | tf_op jit(solution)/shard_map/all_to_all | solution.py:83
  136.0 5.8 fusion.55
  153.3 5.7 multiply_subtract_fusion.1
  175.0 5.8 fusion.8
  188.5 35.0 %all_to_all.120 = f32[16,1,16384]{2,1,0:T(1,128)S(1)} all-to-all(f32[16,1,16384]{2,1,0:T(1,128)S(1)} %reshape.88), channel_id=1, replica_groups=mesh['px'=16,'py'=16] {'px'}, dimensions={0} | all-to-all | bytes 2097152 | tf_op jit(solution)/shard_map/all_to_all | solution.py:88
  238.0 5.9 fusion.109
  268.8 21.3 %all_to_all.121 = f32[16,1,16384]{2,1,0:T(1,128)S(1)} all-to-all(f32[16,1,16384]{2,1,0:T(1,128)S(1)} %reshape.90), channel_id=1, replica_groups=mesh['px'=16,'py'=16] {'py'}, dimensions={0} | all-to-all | bytes 2097152 | tf_op jit(solution)/shard_map/all_to_all | solution.py:93
  296.1 6.2 %copy.73 = f32[2,32,8,16,32]{4,2,3,1,0:T(8,128)} copy(f32[2,32,8,16,32]{1,2,0,4,3:T(8,128)} %bitcast.349) | data formatting | bytes 2097152 | tf_op jit(solution)/shard_map/all_to_all | solution.py:93
  322.5 19.2 %all_to_all.122 = f32[16,1,16384]{2,1,0:T(1,128)S(1)} all-to-all(f32[16,1,16384]{2,1,0:T(1,128)S(1)} %reshape.92), channel_id=1, replica_groups=mesh['px'=16,'py'=16] {'py'}, dimensions={0} | all-to-all | bytes 2097152 | tf_op jit(solution)/shard_map/all_to_all | solution.py:78
  355.2 5.9 fusion.47
  362.3 5.6 fusion.45
  386.4 31.2 %all_to_all.123 = f32[16,1,16384]{2,1,0:T(1,128)S(1)} all-to-all(f32[16,1,16384]{2,1,0:T(1,128)S(1)} %reshape.94), channel_id=1, replica_groups=mesh['px'=16,'py'=16] {'px'}, dimensions={0} | all-to-all | bytes 2097152 | tf_op jit(solution)/shard_map/all_to_all | solution.py:83
  432.1 5.8 fusion.43
  501.3 13.7 %all-to-all-done.6 = f32[16,1,16384]{2,1,0:T(1,128)S(1)} async-done(((f32[16,1,16384]{2,1,0:T(1,128)}), f32[16,1,16384]{2,1,0:T(1,128)S(1)}, u32[]{:S(2)}, u32[]{:S(2)}) %all-to-all-start.6) | async-done | bytes 1048608 | tf_op jit(solution)/shard_map/all_to_all | solution.py:88
  530.0 5.9 fusion.113
  535.9 5.8 fusion.95
  562.2 9.9 %all-to-all-start.7 = ((f32[16,1,16384]{2,1,0:T(1,128)}), f32[16,1,16384]{2,1,0:T(1,128)}, u32[]{:S(2)}, u32[]{:S(2)}) async-start(f32[16,1,16384]{2,1,0:T(1,128)} %reshape.98), calls=%async_computation.7 | async-start | bytes 2097152 | tf_op jit(solution)/shard_map/all_to_all | solution.py:93
  595.5 6.1 copy.85
  606.7 6.2 %fusion.19 = f32[32,32,128]{2,1,0:T(8,128)} fusion(f32[32,32,128]{2,1,0:T(8,128)S(1)} %copy-done.2, f32[32,32,128]{2,1,0:T(8,128)S(1)} %fusion, f32[2,32,16,8,32]{4,3,2,1,0:T(8,128)} %bitcast.355, f32[33,33,128]{2,1,0:T(8,128)S(1)} %get-tuple-element.25, f32[33,33,128]{2,1,0:T(8,128)S(1)} %get-tuple-element.24, f32[33,33,128]{2,1,0:T(8,128)S(1)} %copy-done.7, ...), kind=kOutput, calls=%fused_computation.53 | convolution fusion | flops 202866688 | bytes 6815744 | tf_op jit(solution)/shard_map/bza,zk->bak/dot_general | solution.py:30
  (175 shorter events, 349.5 us)
Async XLA Ops:
  0.0 20.2 %copy-start = (f32[32,32,32]{2,1,0:T(8,128)S(1)}, f32[32,32,32]{2,1,0:T(8,128)}, u32[]{:S(2)}) copy-start(f32[32,32,32]{2,1,0:T(8,128)} %param.5) | copy-start | bytes 393220
  13.1 22.7 %all-to-all-start = ((f32[16,1,16384]{2,1,0:T(1,128)}), f32[16,1,16384]{2,1,0:T(1,128)S(1)}, u32[]{:S(2)}, u32[]{:S(2)}) async-start(f32[16,1,16384]{2,1,0:T(1,128)} %reshape.84), calls=%async_computation | async-start | bytes 2097152 | tf_op jit(solution)/shard_map/all_to_all | solution.py:78
  49.8 6.1 copy-start.3
  57.9 6.5 %copy-start.12 = (f32[32,8,512]{2,0,1:T(8,128)S(1)}, f32[32,8,512]{2,0,1:T(8,128)}, u32[]{:S(2)}) copy-start(f32[32,8,512]{2,0,1:T(8,128)} %squeeze.49) | copy-start | bytes 1572868
  57.9 6.5 %copy-start.17 = (f32[512,32,8]{0,1,2:T(8,128)S(1)}, f32[512,32,8]{0,1,2:T(8,128)}, u32[]{:S(2)}) copy-start(f32[512,32,8]{0,1,2:T(8,128)} %fusion.59) | copy-start | bytes 1572868
  83.7 37.6 %all-to-all-start.1 = ((f32[16,1,16384]{2,1,0:T(1,128)}), f32[16,1,16384]{2,1,0:T(1,128)S(1)}, u32[]{:S(2)}, u32[]{:S(2)}) async-start(f32[16,1,16384]{2,1,0:T(1,128)} %reshape.86), calls=%async_computation.1 | async-start | bytes 2097152 | tf_op jit(solution)/shard_map/all_to_all | solution.py:83
  142.6 10.7 %copy-start.13 = (f32[8,32,512]{2,1,0:T(8,128)S(1)}, f32[8,32,512]{2,1,0:T(8,128)}, u32[]{:S(2)}) copy-start(f32[8,32,512]{2,1,0:T(8,128)} %fusion.16) | copy-start | bytes 1572868
  142.6 10.7 %copy-start.15 = (f32[8,32,512]{2,1,0:T(8,128)S(1)}, f32[8,32,512]{2,1,0:T(8,128)}, u32[]{:S(2)}) copy-start(f32[8,32,512]{2,1,0:T(8,128)} %fusion.17) | copy-start | bytes 1572868
  250.2 10.8 %copy-start.10 = (f32[512,256]{0,1:S(1)}, f32[512,256]{0,1}, u32[]{:S(2)}) copy-start(f32[512,256]{0,1} %fusion.109) | copy-start | bytes 1572868
  296.1 11.2 %copy-start.8 = (f32[32,32,128]{2,1,0:T(8,128)S(1)}, f32[32,32,128]{2,1,0:T(8,128)}, u32[]{:S(2)}) copy-start(f32[32,32,128]{2,1,0:T(8,128)} %param.4) | copy-start | bytes 1572868
  355.2 5.9 copy-start.4
  438.7 10.9 %copy-start.14 = (f32[8,32,512]{2,1,0:T(8,128)S(1)}, f32[8,32,512]{2,1,0:T(8,128)}, u32[]{:S(2)}) copy-start(f32[8,32,512]{2,1,0:T(8,128)} %fusion.16) | copy-start | bytes 1572868
  438.7 10.9 %copy-start.16 = (f32[8,32,512]{2,1,0:T(8,128)S(1)}, f32[8,32,512]{2,1,0:T(8,128)}, u32[]{:S(2)}) copy-start(f32[8,32,512]{2,1,0:T(8,128)} %fusion.17) | copy-start | bytes 1572868
  480.4 9.0 %copy-start.2 = (f32[32,32,128]{2,1,0:T(8,128)S(1)}, f32[32,32,128]{2,1,0:T(8,128)}, u32[]{:S(2)}) copy-start(f32[32,32,128]{2,1,0:T(8,128)} %param.3) | copy-start | bytes 1572868
  485.2 29.8 %all-to-all-start.6 = ((f32[16,1,16384]{2,1,0:T(1,128)}), f32[16,1,16384]{2,1,0:T(1,128)S(1)}, u32[]{:S(2)}, u32[]{:S(2)}) async-start(f32[16,1,16384]{2,1,0:T(1,128)} %reshape.96), calls=%async_computation.6 | async-start | bytes 2097152 | tf_op jit(solution)/shard_map/all_to_all | solution.py:88
  489.4 6.1 collective-permute-start
  494.2 6.3 %collective-permute-start.1 = (f32[1,32,128]{2,1,0:T(8,128)S(1)}, f32[1,32,128]{2,1,0:T(8,128)S(1)}, u32[]{:S(2)}, u32[]{:S(2)}) collective-permute-start(f32[1,32,128]{2,1,0:T(8,128)S(1)} %get-tuple-element.28), channel_id=1, source_target_pairs={{16,0},{32,16},{48,32},{64,48},{80,64},{96,80},{112,96},{128,112},... | collective-permute-start | bytes 49160 | tf_op jit(solution)/shard_map/ppermute | solution.py:24
  542.5 11.0 %copy-start.11 = (f32[512,256]{0,1:S(1)}, f32[512,256]{0,1}, u32[]{:S(2)}) copy-start(f32[512,256]{0,1} %fusion.113) | copy-start | bytes 1572868
  557.5 14.7 %copy-start.6 = (f32[34,32,128]{2,1,0:T(8,128)S(1)}, f32[34,32,128]{2,1,0:T(8,128)}, u32[]{:S(2)}) copy-start(f32[34,32,128]{2,1,0:T(8,128)} %copy-done.5) | copy-start | bytes 1671172
  562.2 25.7 %all-to-all-start.7 = ((f32[16,1,16384]{2,1,0:T(1,128)}), f32[16,1,16384]{2,1,0:T(1,128)}, u32[]{:S(2)}, u32[]{:S(2)}) async-start(f32[16,1,16384]{2,1,0:T(1,128)} %reshape.98), calls=%async_computation.7 | async-start | bytes 2097152 | tf_op jit(solution)/shard_map/all_to_all | solution.py:93
  572.2 5.5 collective-permute-start.2
  575.8 6.1 collective-permute-start.3
  595.5 11.2 %copy-start.7 = (f32[33,33,128]{2,1,0:T(8,128)S(1)}, f32[33,33,128]{2,1,0:T(8,128)}, u32[]{:S(2)}) copy-start(f32[33,33,128]{2,1,0:T(8,128)} %get-tuple-element.5) | copy-start | bytes 1672708
  601.6 11.3 %copy-start.1 = (f32[32,32,32]{2,1,0:T(8,128)S(1)}, f32[32,32,32]{2,1,0:T(8,128)}, u32[]{:S(2)}) copy-start(f32[32,32,32]{2,1,0:T(8,128)} %param.5) | copy-start | bytes 393220
  (5 other events, 22.8 us)
where the time goes:
time: 619 us; the launch traced here: 613 us
  matrix products  216 us (35%)
  local copies, waits for them, and re-layouts  159 us (26%)
  blocking collectives  107 us (17%)
  waiting for transfers between devices  57 us (9%)
  starting transfers between devices  43.8 us (7%)
  other arithmetic  29.9 us (5%)
    dot_general x42, matrix products, product(): return jnp.einsum(pattern, left, right, precision=lax.Precision.HIGHEST)  171 us
    unnamed x60, local copies, waits for them, and re-layouts  57.8 us
    unnamed x8, matrix products  44.8 us
    all_to_all x1, blocking collectives, homeward_two(): lax.all_to_all(spectrum, 'px', split_axis=3, concat_axis=2, tiled=True)  35 us
    all_to_all x1, blocking collectives, outward_two(): lax.all_to_all(spectrum, 'px', split_axis=2, concat_axis=3, tiled=True)  31.2 us
    all_to_all x1, blocking collectives, homeward_one(): lax.all_to_all(spectrum, 'py', split_axis=3, concat_axis=2, tiled=True)  21.3 us
    all_to_all x1, blocking collectives, outward_one(): lax.all_to_all(spectrum, 'py', split_axis=2, concat_axis=3, tiled=True)  19.2 us
    all_to_all x1, waiting for transfers between devices, outward_two(): lax.all_to_all(spectrum, 'px', split_axis=2, concat_axis=3, tiled=True)  17.6 us
  transfers between devices with their start and end apart: 8, of which 6 were waited for; matrix products, arithmetic and copies ran while one was open for 2% of the time, Pallas kernels for 0%

commit v1 on v0

v1 whole, which is shorter than its diff:
```python
import functools
import math

import jax
import jax.numpy as jnp
import ml_dtypes
import numpy as np
from jax import lax
from jax.experimental import pallas as pl
from jax.experimental.pallas import tpu as pltpu
from jax.sharding import PartitionSpec as P

penalty_weight = 0.1
smoothing = 0.1

WINDOW = 64
PLANES = 34
ROOT = math.sqrt(0.5)


def two_part(matrix):
    high = matrix.astype(ml_dtypes.bfloat16)
    low = (matrix - high.astype(np.float64)).astype(ml_dtypes.bfloat16)
    return high, low


def right_operand(matrix):
    high, low = two_part(matrix)
    return np.block([[high, low], [high, np.zeros_like(high)]])


def left_operand(matrix):
    high, low = two_part(matrix)
    return np.block([[high, high], [low, np.zeros_like(high)]])


def depth_forward(positions, depth):
    half = depth // 2
    turns = 2.0 * np.pi / depth
    real = np.cos(turns * np.outer(positions, np.arange(half + 1)))
    imag = -np.sin(turns * np.outer(positions, np.arange(1, half)))
    return np.concatenate([real, imag], 1)


def depth_inverse(depth):
    half = depth // 2
    turns = 2.0 * np.pi / depth
    positions = np.arange(depth)
    weight = np.full(half + 1, 2.0)
    weight[0] = weight[half] = 1.0
    real = weight[:, None] * np.cos(turns * np.outer(np.arange(half + 1), positions))
    imag = -2.0 * np.sin(turns * np.outer(np.arange(1, half), positions))
    return np.concatenate([real, imag], 0)


def column_forward(positions):
    angles = 2.0 * np.pi / WINDOW * np.outer(np.arange(WINDOW), positions)
    cosine, sine = np.cos(angles), np.sin(angles)
    return np.block([[cosine, sine], [-sine, cosine]])


def column_inverse(positions):
    angles = 2.0 * np.pi / WINDOW * np.outer(positions, np.arange(WINDOW))
    cosine, sine = np.cos(angles), np.sin(angles)
    return np.block([[cosine, -sine], [sine, cosine]])


def add(a, b):
    return (a[0] + b[0], a[1] + b[1])


def sub(a, b):
    return (a[0] - b[0], a[1] - b[1])


def turn(a, eighths):
    real, imag = a
    eighths %= 8
    if eighths == 0:
        return a
    if eighths == 2:
        return (-imag, real)
    if eighths == 4:
        return (-real, -imag)
    if eighths == 6:
        return (imag, -real)
    total, gap = (real + imag) * ROOT, (real - imag) * ROOT
    if eighths == 1:
        return (gap, total)
    if eighths == 3:
        return (-total, gap)
    if eighths == 5:
        return (-gap, -total)
    return (total, -gap)


def twiddle(a, power, sign):
    angle = sign * 2.0 * math.pi * power / WINDOW
    cosine, sine = math.cos(angle), math.sin(angle)
    if power == 0:
        return a
    real, imag = a
    return (real * cosine - imag * sine, real * sine + imag * cosine)


def complex_eight(values, sign):
    if len(values) == 1:
        return values
    count = len(values)
    even = complex_eight(values[0::2], sign)
    odd = complex_eight(values[1::2], sign)
    odd = [turn(value, sign * k * (8 // count)) for k, value in enumerate(odd)]
    return [add(e, o) for e, o in zip(even, odd)] + [sub(e, o) for e, o in zip(even, odd)]


def real_eight(a):
    s04, d04, s26, d26 = a[0] + a[4], a[0] - a[4], a[2] + a[6], a[2] - a[6]
    s15, d15, s37, d37 = a[1] + a[5], a[1] - a[5], a[3] + a[7], a[3] - a[7]
    even, odd = s04 + s26, s15 + s37
    gap, total = (d15 - d37) * ROOT, (d15 + d37) * ROOT
    return (
        even + odd,
        (d04 + gap, -d26 - total),
        (s04 - s26, s37 - s15),
        (d04 - gap, d26 - total),
        even - odd,
    )


def rows_forward(load, store, zero):
    first = [real_eight([load(8 * x1 + x0) for x1 in range(8)]) for x0 in range(8)]
    ends = real_eight([f[0] for f in first])
    store(0, ends[0], zero)
    for k0 in (1, 2, 3):
        store(k0, *ends[k0])
    store(4, ends[4], zero)
    plane = 5
    for k1 in (1, 2, 3):
        out = complex_eight([twiddle(first[x0][k1], k1 * x0, -1) for x0 in range(8)], -1)
        for value in out:
            store(plane, *value)
            plane += 1
    middle = []
    for x0 in range(8):
        angle = 2.0 * math.pi * 4 * x0 / WINDOW
        middle.append((first[x0][4] * math.cos(angle), first[x0][4] * -math.sin(angle)))
    middle = complex_eight(middle, -1)
    for k0 in range(4):
        store(plane, *middle[k0])
        plane += 1


def rows_inverse(load, store):
    ends = [load(p) for p in range(5)]
    x0r, x4r = ends[0][0], ends[4][0]
    spectrum = [(x0r, jnp.zeros_like(x0r))] + [ends[k] for k in (1, 2, 3)]
    parts = [[None] * 8 for _ in range(5)]
    (r1, i1), (r2, i2), (r3, i3) = [(2.0 * e[0], 2.0 * e[1]) for e in ends[1:4]]
    del spectrum
    base, flip = x0r + x4r, x0r - x4r
    g13, t13 = r1 - r3, r1 + r3
    h13, u13 = i1 - i3, i1 + i3
    parts[0][0] = base + t13 + r2
    parts[0][4] = base - t13 + r2
    parts[0][2] = base - r2 - h13
    parts[0][6] = base - r2 + h13
    odd_a, odd_b = g13 * ROOT, u13 * ROOT
    parts[0][1] = flip + odd_a - odd_b - i2
    parts[0][5] = flip - odd_a + odd_b - i2
    parts[0][3] = flip - odd_a - odd_b + i2
    parts[0][7] = flip + odd_a + odd_b + i2
    plane = 5
    for k1 in (1, 2, 3):
        values = complex_eight([load(plane + k0) for k0 in range(8)], 1)
        plane += 8
        parts[k1] = [twiddle(values[x0], k1 * x0, 1) for x0 in range(8)]
    half = [load(plane + k0) for k0 in range(4)]
    middle = complex_eight(half + [(half[3 - k][0], -half[3 - k][1]) for k in range(4)], 1)
    for x0 in range(8):
        angle = 2.0 * math.pi * 4 * x0 / WINDOW
        parts[4][x0] = middle[x0][0] * math.cos(angle) - middle[x0][1] * math.sin(angle)
    for x0 in range(8):
        v0, v4 = parts[0][x0], parts[4][x0]
        (a, b), (c, d), (e, f) = parts[1][x0], parts[2][x0], parts[3][x0]
        plus, minus = v0 + v4, v0 - v4
        store(16 + x0, plus + 2.0 * (f - b - c))
        store(24 + x0, minus + 2.0 * (d + ROOT * ((e - f) - (a + b))))
        store(32 + x0, plus + 2.0 * (c - a - e))
        store(40 + x0, minus + 2.0 * (ROOT * ((b - a) + (e + f)) - d))


def parts_of(value):
    high = value.astype(jnp.bfloat16)
    low = (value - high.astype(jnp.float32)).astype(jnp.bfloat16)
    return high, low


def along_depth(rows, matrix):
    high, low = parts_of(rows)
    out = jnp.dot(
        jnp.concatenate([high, low], 1), matrix, preferred_element_type=jnp.float32
    )
    return out[:, :128] + out[:, 128:]


def along_columns(matrix, value):
    high, low = parts_of(value)
    out = jnp.dot(
        matrix, jnp.concatenate([high, low], 0), preferred_element_type=jnp.float32
    )
    half = out.shape[0] // 2
    return out[:half] + out[half:]


def transfer_kernel(psf_ref, depth_ref, column_ref, out_ref, field, rows):
    size = psf_ref.shape[0]
    for x in range(0, size, 8):
        values = psf_ref[x : x + 8].reshape(8 * size, size)
        field[x : x + 8] = jnp.dot(
            values,
            depth_ref[...],
            precision=lax.Precision.HIGHEST,
            preferred_element_type=jnp.float32,
        ).reshape(8, size, 128)
    zero = jnp.zeros((8, 128), jnp.float32)

    def chunk(c, carry):
        here = pl.ds(pl.multiple_of(c * 8, 8), 8)
        there = pl.ds(pl.multiple_of(c * 8 + size, 8), 8)

        def load(x):
            tap = (x + size // 2) % WINDOW
            return field[tap, here, :] if tap < size else zero

        def store(plane, real, imag):
            rows[plane, here, :] = real
            rows[plane, there, :] = imag

        rows_forward(load, store, zero)
        return carry

    lax.fori_loop(0, size // 8, chunk, 0)
    lane = lax.broadcasted_iota(jnp.int32, (1, 128), 1)
    real_lane = lane <= 64
    first_half = lane < 64
    alone = (lane == 0) | (lane == 64)

    def plane_of(p, carry):
        spectrum = jnp.dot(
            column_ref[...],
            rows[p],
            precision=lax.Precision.HIGHEST,
            preferred_element_type=jnp.float32,
        )
        other = pltpu.roll(spectrum, 64, 1)
        own = jnp.where(real_lane, spectrum, other)
        partner = jnp.where(alone, 0.0, jnp.where(first_half, -other, spectrum))
        out_ref[p, :128, :] = own
        out_ref[p, 128:, :] = partner
        return carry

    lax.fori_loop(0, PLANES - 1, plane_of, 0)
    out_ref[PLANES - 1] = jnp.zeros_like(out_ref[0])


def convolve_kernel(
    adjoint,
    own_ref,
    top_ref,
    bottom_ref,
    left_ref,
    right_ref,
    transfer_ref,
    other_ref,
    depth_ref,
    column_ref,
    column_back_ref,
    depth_back_ref,
    out_ref,
    field,
    rows,
    back,
):
    depth_matrix = depth_ref[...]

    def depth_piece(ref, x_from, y_from, step):
        count, width, lanes = ref.shape
        for x in range(0, count, step):
            values = ref[x : x + step].reshape(step * width, lanes)
            field[x_from + x : x_from + x + step, y_from : y_from + width, :] = along_depth(
                values, depth_matrix
            ).reshape(step, width, lanes)

    depth_piece(own_ref, 16, 16, 8)
    depth_piece(top_ref, 0, 16, 8)
    depth_piece(bottom_ref, 48, 16, 8)
    depth_piece(left_ref, 0, 0, 16)
    depth_piece(right_ref, 0, 48, 16)

    zero = jnp.zeros((8, 128), jnp.float32)
    rows[PLANES - 1] = jnp.zeros_like(rows[0])

    def chunk(c, carry):
        here = pl.ds(pl.multiple_of(c * 8, 8), 8)
        there = pl.ds(pl.multiple_of(c * 8 + WINDOW, 8), 8)

        def load(x):
            return field[x, here, :]

        def store(plane, real, imag):
            rows[plane, here, :] = real
            rows[plane, there, :] = imag

        rows_forward(load, store, zero)
        return carry

    lax.fori_loop(0, WINDOW // 8, chunk, 0)

    def pair(i, carry):
        p = i * 2
        spectrum = along_columns(
            column_ref[...], jnp.concatenate([rows[p], rows[p + 1]], 1)
        )
        weighted = []
        for k in range(2):
            own = spectrum[:, 128 * k : 128 * (k + 1)]
            partner = pltpu.roll(own, 64, 1)
            a, b = own[:64], own[64:]
            c, d = partner[:64], partner[64:]
            fr, fi = transfer_ref[p + k, 0:64, :], transfer_ref[p + k, 64:128, :]
            gr, gi = transfer_ref[p + k, 128:192, :], transfer_ref[p + k, 192:256, :]
            if adjoint:
                real = (a * fr + b * fi) - (c * gr + d * gi)
                imag = (b * fr - a * fi) - (d * gr - c * gi)
            else:
                real = (a * fr - b * fi) + (c * gr - d * gi)
                imag = (b * fr + a * fi) + (d * gr + c * gi)
            weighted.append(jnp.concatenate([real, imag], 0))
        result = along_columns(column_back_ref[...], jnp.concatenate(weighted, 1))
        back[p] = result[:, :128]
        back[p + 1] = result[:, 128:]
        return carry

    lax.fori_loop(0, PLANES // 2, pair, 0, unroll=PLANES // 2)

    def chunk_back(c, carry):
        here = pl.ds(pl.multiple_of(c * 8, 8), 8)
        there = pl.ds(pl.multiple_of(c * 8 + 32, 8), 8)

        def load(plane):
            return back[plane, here, :], back[plane, there, :]

        def store(x, value):
            field[x, here, :] = value

        rows_inverse(load, store)
        return carry

    lax.fori_loop(0, 4, chunk_back, 0)

    matrix = depth_back_ref[...]
    for x in range(0, 32, 8):
        values = field[16 + x : 24 + x, 0:32, :].reshape(256, 128)
        result = along_depth(values, matrix).reshape(8, 32, 128)
        if adjoint:
            out_ref[x : x + 8] = other_ref[x : x + 8] * result
        else:
            out_ref[x : x + 8] = other_ref[x : x + 8] / result


def vmem(count):
    return [pl.BlockSpec(memory_space=pltpu.VMEM)] * count


def transfer_function(psf, depth):
    size = psf.shape[0]
    offsets = np.arange(size) - size // 2
    return pl.pallas_call(
        transfer_kernel,
        out_shape=jax.ShapeDtypeStruct((PLANES, 256, 128), jnp.float32),
        in_specs=vmem(3),
        out_specs=pl.BlockSpec(memory_space=pltpu.VMEM),
        scratch_shapes=[
            pltpu.VMEM((size, size, 128), jnp.float32),
            pltpu.VMEM((PLANES - 1, 2 * size, 128), jnp.float32),
        ],
        compiler_params=pltpu.CompilerParams(vmem_limit_bytes=32 * 2**20),
        name="transfer",
    )(
        psf,
        jnp.asarray(depth_forward(offsets, depth), jnp.float32),
        jnp.asarray(column_forward(offsets), jnp.float32),
    )


def convolve(pieces, transfer, other, adjoint):
    depth = other.shape[2]
    positions = np.arange(WINDOW)
    scale = 1.0 / (WINDOW * WINDOW * depth)
    return pl.pallas_call(
        functools.partial(convolve_kernel, adjoint),
        out_shape=jax.ShapeDtypeStruct(other.shape, jnp.float32),
        in_specs=vmem(11),
        out_specs=pl.BlockSpec(memory_space=pltpu.VMEM),
        scratch_shapes=[
            pltpu.VMEM((WINDOW, WINDOW, depth), jnp.float32),
            pltpu.VMEM((PLANES, 2 * WINDOW, depth), jnp.float32),
            pltpu.VMEM((PLANES, WINDOW, depth), jnp.float32),
        ],
        compiler_params=pltpu.CompilerParams(vmem_limit_bytes=48 * 2**20),
        name="correlate" if adjoint else "convolve",
    )(
        *pieces,
        transfer,
        other,
        right_operand(depth_forward(np.arange(depth), depth)),
        left_operand(column_forward(positions)),
        left_operand(column_inverse(positions[16:48])),
        right_operand(depth_inverse(depth) * scale),
    )


def halos(block):
    def ring(axis, step):
        count = lax.axis_size(axis)
        return [(i, (i + step) % count) for i in range(count)]

    top = lax.ppermute(block[16:], "px", ring("px", 1))
    bottom = lax.ppermute(block[:16], "px", ring("px", -1))
    ends = jnp.concatenate([top[:, 16:], block[:, 16:], bottom[:, 16:]], 0)
    starts = jnp.concatenate([top[:, :16], block[:, :16], bottom[:, :16]], 0)
    left = lax.ppermute(ends, "py", ring("py", 1))
    right = lax.ppermute(starts, "py", ring("py", -1))
    return block, top, bottom, left, right


def variation(pieces):
    volume, top, bottom, left, right = pieces
    row_count, col_count, _ = volume.shape
    row_whole = row_count * lax.axis_size("px")
    col_whole = col_count * lax.axis_size("py")
    padded = jnp.concatenate(
        [
            left[15:49, 15:],
            jnp.concatenate([top[15:], volume, bottom[:1]], 0),
            right[15:49, :1],
        ],
        1,
    )
    region = padded[:-1, :-1]
    slope_rows = padded[1:, :-1] - region
    slope_cols = padded[:-1, 1:] - region
    row_global = lax.axis_index("px") * row_count - 1 + jnp.arange(row_count + 1)
    col_global = lax.axis_index("py") * col_count - 1 + jnp.arange(col_count + 1)
    row_valid = ((row_global >= 0) & (row_global <= row_whole - 2))[:, None, None]
    col_valid = ((col_global >= 0) & (col_global <= col_whole - 2))[None, :, None]
    slope_rows = jnp.where(row_valid, slope_rows, 0.0)
    slope_cols = jnp.where(col_valid, slope_cols, 0.0)
    slope_depth = jnp.concatenate(
        [region[:, :, 1:] - region[:, :, :-1], jnp.zeros_like(region[:, :, :1])], 2
    )
    factor = lax.rsqrt(
        slope_rows * slope_rows
        + slope_cols * slope_cols
        + slope_depth * slope_depth
        + smoothing * smoothing
    )
    flux_rows, flux_cols = slope_rows * factor, slope_cols * factor
    flux_depth = (slope_depth * factor)[1:, 1:]
    flux_depth = flux_depth - jnp.concatenate(
        [jnp.zeros_like(flux_depth[:, :, :1]), flux_depth[:, :, :-1]], 2
    )
    return (
        flux_rows[1:, 1:]
        - flux_rows[:-1, 1:]
        + (flux_cols[1:, 1:] - flux_cols[1:, :-1])
        + flux_depth
    )


def shards(estimate, observed, psf):
    transfer = transfer_function(psf, estimate.shape[2])
    pieces = halos(estimate)
    quotient = convolve(pieces, transfer, observed, False)
    scaled = estimate / (1.0 - penalty_weight * variation(pieces))
    return convolve(halos(quotient), transfer, scaled, True)


def solution(mesh):
    placed = (P("px", "py", None), P("px", "py", None), P())
    return jax.shard_map(
        shards, mesh=mesh, in_specs=placed, out_specs=P("px", "py", None), check_vma=False
    )
```

time: 619 us -> 91.8 us (0.15)
  matrix products: 216 us -> 0 us
  local copies, waits for them, and re-layouts: 159 us -> 5.53 us
  blocking collectives: 107 us -> 0 us
  Pallas kernels: 0 us -> 30.9 us
  other arithmetic: 29.9 us -> 3.11 us
  starting transfers between devices: 43.8 us -> 19.1 us
  waiting for transfers between devices: 57 us -> 32.8 us
    dot_general x42 -> x0, matrix products: 171 us -> none  [product(): return jnp.einsum(pattern, left, right, precision=lax.Precision.HIGHEST)]
    all_to_all x4 -> x0, blocking collectives: 107 us -> none  [the longest x1 35 us: homeward_two(): lax.all_to_all(spectrum, 'px', split_axis=3, concat_axis=2, tiled=True)]
    unnamed x60 -> x20, local copies, waits for them, and re-layouts: 57.8 us -> 3.05 us
    all_to_all x4 -> x0, waiting for transfers between devices: 48.2 us -> none  [the longest x1 17.6 us: outward_two(): lax.all_to_all(spectrum, 'px', split_axis=2, concat_axis=3, tiled=True)]
    unnamed x8 -> x0, matrix products: 44.8 us -> none
    all_to_all x9 -> x0, local copies, waits for them, and re-layouts: 40.5 us -> none  [the longest x2 12.2 us: homeward_one(): lax.all_to_all(spectrum, 'py', split_axis=3, concat_axis=2, tiled=True)]
    all_to_all x4 -> x0, starting transfers between devices: 32.3 us -> none  [the longest x1 11 us: outward_two(): lax.all_to_all(spectrum, 'px', split_axis=2, concat_axis=3, tiled=True)]
    another operation x8 -> x0, local copies, waits for them, and re-layouts: 30.9 us -> none  [the longest x2 8.93 us: convolve(): jnp.stack([product('baz,zk->bka', volume, cosine), -product('baz,zk->bka'...]
  transfers between devices with their start and end apart: 8 -> 8, of which waited for: 6 -> 7; matrix products, arithmetic and copies ran while one was open for 2% -> 4% of each run, Pallas kernels for 0% -> 11%
where the time goes in v1:
time: 91.8 us; the launch traced here: 91.6 us
  waiting for transfers between devices  32.8 us (36%)
  Pallas kernels  30.9 us (34%)
  starting transfers between devices  19.1 us (21%)
  local copies, waits for them, and re-layouts  5.53 us (6%)
  other arithmetic  3.11 us (3%)
    pallas_call x2, Pallas kernels, convolve(): pl.pallas_call(functools.partial(convolve_kernel, adjoint), out_shape=jax...  21.2 us
    ppermute x2, starting transfers between devices, halos(): bottom = lax.ppermute(block[:16], 'px', ring('px', -1))  13.4 us
    ppermute x2, waiting for transfers between devices, halos(): top = lax.ppermute(block[16:], 'px', ring('px', 1))  10.9 us
    ppermute x2, waiting for transfers between devices, halos(): left = lax.ppermute(ends, 'py', ring('py', 1))  10.7 us
    pallas_call x1, Pallas kernels, transfer_function(): pl.pallas_call(transfer_kernel, out_shape=jax.ShapeDtypeStruct((PLANES, 2...  9.7 us
    ppermute x2, waiting for transfers between devices, halos(): bottom = lax.ppermute(block[:16], 'px', ring('px', -1))  7.14 us
    ppermute x2, starting transfers between devices, halos(): left = lax.ppermute(ends, 'py', ring('py', 1))  5.38 us
    ppermute x2, waiting for transfers between devices, halos(): right = lax.ppermute(starts, 'py', ring('py', -1))  4.04 us
  transfers between devices with their start and end apart: 8, of which 7 were waited for; matrix products, arithmetic and copies ran while one was open for 4% of the time, Pallas kernels for 11%

profile of v1, /device:TPU:1, one launch (start us, length us, event | category | flops | bytes accessed | tf_op | source)
XLA Modules:
  0.0 91.6 jit_solution(10361444439167823354)
XLA Ops:
  0.0 1.1 %fusion.13 = (f32[16,32,128]{2,1,0:T(8,128)S(1)}, f32[16,32,128]{2,1,0:T(8,128)S(1)}) fusion(f32[32,32,128]{2,1,0:T(8,128)} %own_ref.1), kind=kLoop, calls=%fused_computation.30 | loop fusion | bytes 1048576 | tf_op jit(solution)/shard_map/slice | solution.py:429
  1.1 9.1 %collective-permute-start.1 = (f32[16,32,128]{2,1,0:T(8,128)S(1)}, f32[16,32,128]{2,1,0:T(8,128)S(1)}, u32[]{:S(2)}, u32[]{:S(2)}) collective-permute-start(f32[16,32,128]{2,1,0:T(8,128)S(1)} %get-tuple-element.15), channel_id=1, source_target_pairs={{0,240},{16,0},{32,16},{48,32},{64,48},{80,64},{96,80},{112,96},{1... | collective-permute-start | bytes 786440 | tf_op jit(solution)/shard_map/ppermute | solution.py:429
  10.2 1.1 %fusion.12 = (f32[32,16,128]{2,1,0:T(8,128)S(1)}, f32[32,16,128]{2,1,0:T(8,128)S(1)}) fusion(f32[32,32,128]{2,1,0:T(8,128)} %own_ref.1), kind=kLoop, calls=%fused_computation.29 | loop fusion | bytes 1048576 | tf_op jit(solution)/shard_map/slice | solution.py:431
  11.4 3.9 %collective-permute-done.1.bottom_ref = f32[16,32,128]{2,1,0:T(8,128)S(1)} collective-permute-done((f32[16,32,128]{2,1,0:T(8,128)S(1)}, f32[16,32,128]{2,1,0:T(8,128)S(1)}, u32[]{:S(2)}, u32[]{:S(2)}) %collective-permute-start.1) | collective-permute-done | bytes 262176 | tf_op jit(solution)/shard_map/ppermute | solution.py:429
  15.3 5.4 %collective-permute-done.top_ref = f32[16,32,128]{2,1,0:T(8,128)S(1)} collective-permute-done((f32[16,32,128]{2,1,0:T(8,128)S(1)}, f32[16,32,128]{2,1,0:T(8,128)S(1)}, u32[]{:S(2)}, u32[]{:S(2)}) %collective-permute-start) | collective-permute-done | bytes 262176 | tf_op jit(solution)/shard_map/ppermute | solution.py:428
  20.7 0.8 pad_maximum_fusion.3
  21.6 2.1 %collective-permute-start.2 = (f32[64,16,128]{2,1,0:T(8,128)}, f32[64,16,128]{2,1,0:T(8,128)S(1)}, u32[]{:S(2)}, u32[]{:S(2)}) collective-permute-start(f32[64,16,128]{2,1,0:T(8,128)} %pad_maximum_fusion.3), channel_id=1, source_target_pairs={{0,1},{1,2},{2,3},{3,4},{4,5},{5,6},{6,7},{7,8},{8,9},{9,10},{10,1... | collective-permute-start | bytes 1572872 | tf_op jit(solution)/shard_map/ppermute | solution.py:432
  23.7 0.8 pad_maximum_fusion.4
  24.7 1.0 %copy-done.8 = f32[128,64]{1,0:T(8,128)S(1)} copy-done((f32[128,64]{1,0:T(8,128)S(1)}, f32[128,64]{1,0:T(8,128)}, u32[]{:S(2)}) %copy-start.8) | copy-done | bytes 32792
  25.7 9.7 %transfer.1.transfer_ref = f32[34,256,128]{2,1,0:T(8,128)S(1)} custom-call(f32[32,32,32]{2,1,0:T(8,128)S(1)} %copy-done.5, f32[32,128]{1,0:T(8,128)S(1)} %copy-done.9, f32[128,64]{1,0:T(8,128)S(1)} %copy-done.8), custom_call_target="tpu_custom_call" | custom-call | tf_op jit(solution)/shard_map/transfer/pallas_call | solution.py:378
  35.4 2.0 %copy-done = f32[34,256,128]{2,1,0:T(8,128)} copy-done((f32[34,256,128]{2,1,0:T(8,128)}, f32[34,256,128]{2,1,0:T(8,128)S(1)}, u32[]{:S(2)}) %copy-start) | copy-done | bytes 4456472
  37.6 0.2 slice_subtract_fusion
  37.8 1.3 %collective-permute-done.3.right_ref = f32[64,16,128]{2,1,0:T(8,128)S(1)} collective-permute-done((f32[64,16,128]{2,1,0:T(8,128)}, f32[64,16,128]{2,1,0:T(8,128)S(1)}, u32[]{:S(2)}, u32[]{:S(2)}) %collective-permute-start.3) | collective-permute-done | bytes 524320 | tf_op jit(solution)/shard_map/ppermute | solution.py:433
  39.1 10.2 %convolve.1.own_ref = f32[32,32,128]{2,1,0:T(8,128)S(1)} custom-call(f32[32,32,128]{2,1,0:T(8,128)S(1)} %copy-done.1, f32[16,32,128]{2,1,0:T(8,128)S(1)} %collective-permute-done.top_ref, f32[16,32,128]{2,1,0:T(8,128)S(1)} %collective-permute-done.1.bottom_ref, f32[64,16,128]{2,1,0:T(8,128)S(1)} %collective-permute-done.2.left_ref, ...), custom_call_target="tpu_custom_call" | custom-call | tf_op jit(solution)/shard_map/convolve/pallas_call | solution.py:400
  49.4 4.2 %collective-permute-start.5 = (f32[16,32,128]{2,1,0:T(8,128)S(1)}, f32[16,32,128]{2,1,0:T(8,128)S(1)}, u32[]{:S(2)}, u32[]{:S(2)}) collective-permute-start(f32[16,32,128]{2,1,0:T(8,128)S(1)} %get-tuple-element.11), channel_id=1, source_target_pairs={{0,240},{16,0},{32,16},{48,32},{64,48},{80,64},{96,80},{112,96},{1... | collective-permute-start | bytes 786440 | tf_op jit(solution)/shard_map/ppermute | solution.py:429
  53.6 0.4 fusion.8
  54.1 3.3 %collective-permute-done.5.bottom_ref = f32[16,32,128]{2,1,0:T(8,128)S(1)} collective-permute-done((f32[16,32,128]{2,1,0:T(8,128)S(1)}, f32[16,32,128]{2,1,0:T(8,128)S(1)}, u32[]{:S(2)}, u32[]{:S(2)}) %collective-permute-start.5) | collective-permute-done | bytes 262176 | tf_op jit(solution)/shard_map/ppermute | solution.py:429
  57.4 5.4 %collective-permute-done.4.top_ref = f32[16,32,128]{2,1,0:T(8,128)S(1)} collective-permute-done((f32[16,32,128]{2,1,0:T(8,128)S(1)}, f32[16,32,128]{2,1,0:T(8,128)S(1)}, u32[]{:S(2)}, u32[]{:S(2)}) %collective-permute-start.4) | collective-permute-done | bytes 262176 | tf_op jit(solution)/shard_map/ppermute | solution.py:428
  62.9 3.2 %collective-permute-start.6 = (f32[64,16,128]{2,1,0:T(8,128)S(1)}, f32[64,16,128]{2,1,0:T(8,128)S(1)}, u32[]{:S(2)}, u32[]{:S(2)}) collective-permute-start(f32[64,16,128]{2,1,0:T(8,128)S(1)} %pad_maximum_fusion.5), channel_id=1, source_target_pairs={{0,1},{1,2},{2,3},{3,4},{4,5},{5,6},{6,7},{7,8},{8,9},{9,10},{10,1... | collective-permute-start | bytes 1572872 | tf_op jit(solution)/shard_map/ppermute | solution.py:432
  66.1 0.3 collective-permute-start.7
  66.7 0.4 fusion.6.other_ref
  67.1 10.7 %collective-permute-done.6.left_ref = f32[64,16,128]{2,1,0:T(8,128)S(1)} collective-permute-done((f32[64,16,128]{2,1,0:T(8,128)S(1)}, f32[64,16,128]{2,1,0:T(8,128)S(1)}, u32[]{:S(2)}, u32[]{:S(2)}) %collective-permute-start.6) | collective-permute-done | bytes 524320 | tf_op jit(solution)/shard_map/ppermute | solution.py:432
  77.8 2.8 %collective-permute-done.7.right_ref = f32[64,16,128]{2,1,0:T(8,128)S(1)} collective-permute-done((f32[64,16,128]{2,1,0:T(8,128)S(1)}, f32[64,16,128]{2,1,0:T(8,128)S(1)}, u32[]{:S(2)}, u32[]{:S(2)}) %collective-permute-start.7) | collective-permute-done | bytes 524320 | tf_op jit(solution)/shard_map/ppermute | solution.py:433
  80.6 11.0 %correlate.1 = f32[32,32,128]{2,1,0:T(8,128)} custom-call(f32[32,32,128]{2,1,0:T(8,128)S(1)} %convolve.1.own_ref, f32[16,32,128]{2,1,0:T(8,128)S(1)} %collective-permute-done.4.top_ref, f32[16,32,128]{2,1,0:T(8,128)S(1)} %collective-permute-done.5.bottom_ref, f32[64,16,128]{2,1,0:T(8,128)S(1)} %collective-permute-done.6.left_ref, ...), custom_call_target="tpu_custom_call" | custom-call | tf_op jit(solution)/shard_map/correlate/pallas_call | solution.py:400
  (38 shorter events, 0.8 us)
Async XLA Ops:
  0.0 24.7 %copy-start.9 = (f32[32,128]{1,0:T(8,128)S(1)}, f32[32,128]{1,0:T(8,128)}, u32[]{:S(2)}) copy-start(f32[32,128]{1,0:T(8,128)} %constant.39.clone.depth_ref) | copy-start | bytes 49156
  0.0 24.7 %copy-start.5 = (f32[32,32,32]{2,1,0:T(8,128)S(1)}, f32[32,32,32]{2,1,0:T(8,128)}, u32[]{:S(2)}) copy-start(f32[32,32,32]{2,1,0:T(8,128)} %psf_ref.1) | copy-start | bytes 393220
  1.1 14.1 %collective-permute-start.1 = (f32[16,32,128]{2,1,0:T(8,128)S(1)}, f32[16,32,128]{2,1,0:T(8,128)S(1)}, u32[]{:S(2)}, u32[]{:S(2)}) collective-permute-start(f32[16,32,128]{2,1,0:T(8,128)S(1)} %get-tuple-element.15), channel_id=1, source_target_pairs={{0,240},{16,0},{32,16},{48,32},{64,48},{80,64},{96,80},{112,96},{1... | collective-permute-start | bytes 786440 | tf_op jit(solution)/shard_map/ppermute | solution.py:429
  10.2 27.2 %copy-start.1 = (f32[32,32,128]{2,1,0:T(8,128)S(1)}, f32[32,32,128]{2,1,0:T(8,128)}, u32[]{:S(2)}) copy-start(f32[32,32,128]{2,1,0:T(8,128)} %own_ref.1) | copy-start | bytes 1572868
  10.2 10.5 %collective-permute-start = (f32[16,32,128]{2,1,0:T(8,128)S(1)}, f32[16,32,128]{2,1,0:T(8,128)S(1)}, u32[]{:S(2)}, u32[]{:S(2)}) collective-permute-start(f32[16,32,128]{2,1,0:T(8,128)S(1)} %get-tuple-element.16), channel_id=1, source_target_pairs={{0,16},{16,32},{32,48},{48,64},{64,80},{80,96},{96,112},{112,128},... | collective-permute-start | bytes 786440 | tf_op jit(solution)/shard_map/ppermute | solution.py:428
  21.6 15.9 %collective-permute-start.2 = (f32[64,16,128]{2,1,0:T(8,128)}, f32[64,16,128]{2,1,0:T(8,128)S(1)}, u32[]{:S(2)}, u32[]{:S(2)}) collective-permute-start(f32[64,16,128]{2,1,0:T(8,128)} %pad_maximum_fusion.3), channel_id=1, source_target_pairs={{0,1},{1,2},{2,3},{3,4},{4,5},{5,6},{6,7},{7,8},{8,9},{9,10},{10,1... | collective-permute-start | bytes 1572872 | tf_op jit(solution)/shard_map/ppermute | solution.py:432
  24.5 14.5 %copy-start.2 = (bf16[256,256]{1,0:T(8,128)(2,1)S(1)}, bf16[256,256]{1,0:T(8,128)(2,1)}, u32[]{:S(2)}) copy-start(bf16[256,256]{1,0:T(8,128)(2,1)} %constant.44.clone.depth_back_ref) | copy-start | bytes 393220
  24.5 14.5 %copy-start.3 = (bf16[256,256]{1,0:T(8,128)(2,1)S(1)}, bf16[256,256]{1,0:T(8,128)(2,1)}, u32[]{:S(2)}) copy-start(bf16[256,256]{1,0:T(8,128)(2,1)} %constant.42.clone.column_ref) | copy-start | bytes 393220
  24.5 14.5 %copy-start.4 = (bf16[256,256]{1,0:T(8,128)(2,1)S(1)}, bf16[256,256]{1,0:T(8,128)(2,1)}, u32[]{:S(2)}) copy-start(bf16[256,256]{1,0:T(8,128)(2,1)} %constant.41.clone.depth_ref) | copy-start | bytes 393220
  24.6 14.5 %copy-start.6 = (f32[32,32,128]{2,1,0:T(8,128)S(1)}, f32[32,32,128]{2,1,0:T(8,128)}, u32[]{:S(2)}) copy-start(f32[32,32,128]{2,1,0:T(8,128)} %other_ref.1) | copy-start | bytes 1572868
  24.6 14.5 %collective-permute-start.3 = (f32[64,16,128]{2,1,0:T(8,128)}, f32[64,16,128]{2,1,0:T(8,128)S(1)}, u32[]{:S(2)}, u32[]{:S(2)}) collective-permute-start(f32[64,16,128]{2,1,0:T(8,128)} %pad_maximum_fusion.4), channel_id=1, source_target_pairs={{0,15},{1,0},{2,1},{3,2},{4,3},{5,4},{6,5},{7,6},{8,7},{9,8},{10,9... | collective-permute-start | bytes 1572872 | tf_op jit(solution)/shard_map/ppermute | solution.py:433
  24.7 1.0 %copy-start.8 = (f32[128,64]{1,0:T(8,128)S(1)}, f32[128,64]{1,0:T(8,128)}, u32[]{:S(2)}) copy-start(f32[128,64]{1,0:T(8,128)} %constant.40.clone.column_ref) | copy-start | bytes 98308
  25.7 13.4 %copy-start.7 = (bf16[128,256]{1,0:T(8,128)(2,1)S(1)}, bf16[128,256]{1,0:T(8,128)(2,1)}, u32[]{:S(2)}) copy-start(bf16[128,256]{1,0:T(8,128)(2,1)} %constant.43.clone.column_back_ref) | copy-start | bytes 196612
  35.4 2.1 %copy-start = (f32[34,256,128]{2,1,0:T(8,128)}, f32[34,256,128]{2,1,0:T(8,128)S(1)}, u32[]{:S(2)}) copy-start(f32[34,256,128]{2,1,0:T(8,128)S(1)} %transfer.1.transfer_ref) | copy-start | bytes 13369348
  49.4 8.0 %collective-permute-start.5 = (f32[16,32,128]{2,1,0:T(8,128)S(1)}, f32[16,32,128]{2,1,0:T(8,128)S(1)}, u32[]{:S(2)}, u32[]{:S(2)}) collective-permute-start(f32[16,32,128]{2,1,0:T(8,128)S(1)} %get-tuple-element.11), channel_id=1, source_target_pairs={{0,240},{16,0},{32,16},{48,32},{64,48},{80,64},{96,80},{112,96},{1... | collective-permute-start | bytes 786440 | tf_op jit(solution)/shard_map/ppermute | solution.py:429
  53.6 9.2 %collective-permute-start.4 = (f32[16,32,128]{2,1,0:T(8,128)S(1)}, f32[16,32,128]{2,1,0:T(8,128)S(1)}, u32[]{:S(2)}, u32[]{:S(2)}) collective-permute-start(f32[16,32,128]{2,1,0:T(8,128)S(1)} %get-tuple-element.12), channel_id=1, source_target_pairs={{0,16},{16,32},{32,48},{48,64},{64,80},{80,96},{96,112},{112,128},... | collective-permute-start | bytes 786440 | tf_op jit(solution)/shard_map/ppermute | solution.py:428
  62.9 15.0 %collective-permute-start.6 = (f32[64,16,128]{2,1,0:T(8,128)S(1)}, f32[64,16,128]{2,1,0:T(8,128)S(1)}, u32[]{:S(2)}, u32[]{:S(2)}) collective-permute-start(f32[64,16,128]{2,1,0:T(8,128)S(1)} %pad_maximum_fusion.5), channel_id=1, source_target_pairs={{0,1},{1,2},{2,3},{3,4},{4,5},{5,6},{6,7},{7,8},{8,9},{9,10},{10,1... | collective-permute-start | bytes 1572872 | tf_op jit(solution)/shard_map/ppermute | solution.py:432
  66.1 14.5 %collective-permute-start.7 = (f32[64,16,128]{2,1,0:T(8,128)S(1)}, f32[64,16,128]{2,1,0:T(8,128)S(1)}, u32[]{:S(2)}, u32[]{:S(2)}) collective-permute-start(f32[64,16,128]{2,1,0:T(8,128)S(1)} %pad_maximum_fusion.6), channel_id=1, source_target_pairs={{0,15},{1,0},{2,1},{3,2},{4,3},{5,4},{6,5},{7,6},{8,7},{9,8},{10,9... | collective-permute-start | bytes 1572872 | tf_op jit(solution)/shard_map/ppermute | solution.py:433

commit v2 on v1

--- a/solution.py
+++ b/solution.py
@@ -212,7 +212,7 @@
     return out[:half] + out[half:]
 
 
-def transfer_kernel(psf_ref, depth_ref, column_ref, out_ref, field, rows):
+def transfer_kernel(psf_ref, depth_ref, column_ref, out_ref, field, rows, factors, done):
     size = psf_ref.shape[0]
     for x in range(0, size, 8):
         values = psf_ref[x : x + 8].reshape(8 * size, size)
@@ -223,6 +223,7 @@
             preferred_element_type=jnp.float32,
         ).reshape(8, size, 128)
     zero = jnp.zeros((8, 128), jnp.float32)
+    rows[PLANES - 1] = jnp.zeros_like(rows[0])
 
     def chunk(c, carry):
         here = pl.ds(pl.multiple_of(c * 8, 8), 8)
@@ -244,23 +245,26 @@
     real_lane = lane <= 64
     first_half = lane < 64
     alone = (lane == 0) | (lane == 64)
-
-    def plane_of(p, carry):
-        spectrum = jnp.dot(
-            column_ref[...],
-            rows[p],
-            precision=lax.Precision.HIGHEST,
-            preferred_element_type=jnp.float32,
-        )
-        other = pltpu.roll(spectrum, 64, 1)
-        own = jnp.where(real_lane, spectrum, other)
-        partner = jnp.where(alone, 0.0, jnp.where(first_half, -other, spectrum))
-        out_ref[p, :128, :] = own
-        out_ref[p, 128:, :] = partner
-        return carry
-
-    lax.fori_loop(0, PLANES - 1, plane_of, 0)
-    out_ref[PLANES - 1] = jnp.zeros_like(out_ref[0])
+    copies = []
+    for p in range(0, PLANES, 2):
+        both = along_columns(column_ref[...], jnp.concatenate([rows[p], rows[p + 1]], 1))
+        for k in range(2):
+            spectrum = both[:, 128 * k : 128 * (k + 1)]
+            other = pltpu.roll(spectrum, 64, 1)
+            factors[p + k, :128, :] = jnp.where(real_lane, spectrum, other)
+            factors[p + k, 128:, :] = jnp.where(
+                alone, 0.0, jnp.where(first_half, -other, spectrum)
+            )
+        if p + 2 in (PLANES // 2 + 1, PLANES):
+            part = pl.ds(0, p + 2) if not copies else pl.ds(PLANES // 2 + 1, PLANES // 2 - 1)
+            copies.append(
+                pltpu.make_async_copy(
+                    factors.at[part], out_ref.at[part], done.at[len(copies)]
+                )
+            )
+            copies[-1].start()
+    for copy in copies:
+        copy.wait()
 
 
 def convolve_kernel(
@@ -280,7 +284,11 @@
     field,
     rows,
     back,
+    factors,
+    arrived,
 ):
+    fetch = pltpu.make_async_copy(transfer_ref, factors, arrived)
+    fetch.start()
     depth_matrix = depth_ref[...]
 
     def depth_piece(ref, x_from, y_from, step):
@@ -291,11 +299,11 @@
                 values, depth_matrix
             ).reshape(step, width, lanes)
 
-    depth_piece(own_ref, 16, 16, 8)
-    depth_piece(top_ref, 0, 16, 8)
-    depth_piece(bottom_ref, 48, 16, 8)
-    depth_piece(left_ref, 0, 0, 16)
-    depth_piece(right_ref, 0, 48, 16)
+    depth_piece(own_ref, 16, 16, 16)
+    depth_piece(top_ref, 0, 16, 16)
+    depth_piece(bottom_ref, 48, 16, 16)
+    depth_piece(left_ref, 0, 0, 32)
+    depth_piece(right_ref, 0, 48, 32)
 
     zero = jnp.zeros((8, 128), jnp.float32)
     rows[PLANES - 1] = jnp.zeros_like(rows[0])
@@ -316,19 +324,23 @@
 
     lax.fori_loop(0, WINDOW // 8, chunk, 0)
 
-    def pair(i, carry):
-        p = i * 2
+    for p in range(0, PLANES, 2):
         spectrum = along_columns(
             column_ref[...], jnp.concatenate([rows[p], rows[p + 1]], 1)
         )
+        rows[p] = spectrum[:, :128]
+        rows[p + 1] = spectrum[:, 128:]
+
+    fetch.wait()
+    for p in range(0, PLANES, 2):
         weighted = []
         for k in range(2):
-            own = spectrum[:, 128 * k : 128 * (k + 1)]
+            own = rows[p + k]
             partner = pltpu.roll(own, 64, 1)
             a, b = own[:64], own[64:]
             c, d = partner[:64], partner[64:]
-            fr, fi = transfer_ref[p + k, 0:64, :], transfer_ref[p + k, 64:128, :]
-            gr, gi = transfer_ref[p + k, 128:192, :], transfer_ref[p + k, 192:256, :]
+            fr, fi = factors[p + k, 0:64, :], factors[p + k, 64:128, :]
+            gr, gi = factors[p + k, 128:192, :], factors[p + k, 192:256, :]
             if adjoint:
                 real = (a * fr + b * fi) - (c * gr + d * gi)
                 imag = (b * fr - a * fi) - (d * gr - c * gi)
@@ -339,9 +351,6 @@
         result = along_columns(column_back_ref[...], jnp.concatenate(weighted, 1))
         back[p] = result[:, :128]
         back[p + 1] = result[:, 128:]
-        return carry
-
-    lax.fori_loop(0, PLANES // 2, pair, 0, unroll=PLANES // 2)
 
     def chunk_back(c, carry):
         here = pl.ds(pl.multiple_of(c * 8, 8), 8)
@@ -359,13 +368,13 @@
     lax.fori_loop(0, 4, chunk_back, 0)
 
     matrix = depth_back_ref[...]
-    for x in range(0, 32, 8):
-        values = field[16 + x : 24 + x, 0:32, :].reshape(256, 128)
-        result = along_depth(values, matrix).reshape(8, 32, 128)
+    for x in range(0, 32, 16):
+        values = field[16 + x : 32 + x, 0:32, :].reshape(512, 128)
+        result = along_depth(values, matrix).reshape(16, 32, 128)
         if adjoint:
-            out_ref[x : x + 8] = other_ref[x : x + 8] * result
+            out_ref[x : x + 16] = other_ref[x : x + 16] * result
         else:
-            out_ref[x : x + 8] = other_ref[x : x + 8] / result
+            out_ref[x : x + 16] = other_ref[x : x + 16] / result
 
 
 def vmem(count):
@@ -377,19 +386,20 @@
     offsets = np.arange(size) - size // 2
     return pl.pallas_call(
         transfer_kernel,
-        out_shape=jax.ShapeDtypeStruct((PLANES, 256, 128), jnp.float32),
-        in_specs=vmem(3),
-        out_specs=pl.BlockSpec(memory_space=pltpu.VMEM),
+        out_shape=jax.ShapeDtypeStruct((PLANES, 256, depth), jnp.float32),
+        out_specs=pl.BlockSpec(memory_space=pltpu.HBM),
         scratch_shapes=[
-            pltpu.VMEM((size, size, 128), jnp.float32),
-            pltpu.VMEM((PLANES - 1, 2 * size, 128), jnp.float32),
+            pltpu.VMEM((size, size, depth), jnp.float32),
+            pltpu.VMEM((PLANES, 2 * size, depth), jnp.float32),
+            pltpu.VMEM((PLANES, 256, depth), jnp.float32),
+            pltpu.SemaphoreType.DMA((2,)),
         ],
-        compiler_params=pltpu.CompilerParams(vmem_limit_bytes=32 * 2**20),
+        compiler_params=pltpu.CompilerParams(vmem_limit_bytes=16 * 2**20),
         name="transfer",
     )(
         psf,
         jnp.asarray(depth_forward(offsets, depth), jnp.float32),
-        jnp.asarray(column_forward(offsets), jnp.float32),
+        left_operand(column_forward(offsets)),
     )
 
 
@@ -400,14 +410,16 @@
     return pl.pallas_call(
         functools.partial(convolve_kernel, adjoint),
         out_shape=jax.ShapeDtypeStruct(other.shape, jnp.float32),
-        in_specs=vmem(11),
+        in_specs=vmem(5) + [pl.BlockSpec(memory_space=pltpu.HBM)] + vmem(5),
         out_specs=pl.BlockSpec(memory_space=pltpu.VMEM),
         scratch_shapes=[
             pltpu.VMEM((WINDOW, WINDOW, depth), jnp.float32),
             pltpu.VMEM((PLANES, 2 * WINDOW, depth), jnp.float32),
             pltpu.VMEM((PLANES, WINDOW, depth), jnp.float32),
+            pltpu.VMEM((PLANES, 256, depth), jnp.float32),
+            pltpu.SemaphoreType.DMA,
         ],
-        compiler_params=pltpu.CompilerParams(vmem_limit_bytes=48 * 2**20),
+        compiler_params=pltpu.CompilerParams(vmem_limit_bytes=20 * 2**20),
         name="correlate" if adjoint else "convolve",
     )(
         *pieces,
@@ -420,18 +432,21 @@
     )
 
 
-def halos(block):
+def halos(block, beside=None):
     def ring(axis, step):
         count = lax.axis_size(axis)
         return [(i, (i + step) % count) for i in range(count)]
 
     top = lax.ppermute(block[16:], "px", ring("px", 1))
     bottom = lax.ppermute(block[:16], "px", ring("px", -1))
-    ends = jnp.concatenate([top[:, 16:], block[:, 16:], bottom[:, 16:]], 0)
-    starts = jnp.concatenate([top[:, :16], block[:, :16], bottom[:, :16]], 0)
+    sent = block
+    if beside is not None:
+        sent, beside = lax.optimization_barrier((block, beside))
+    ends = jnp.concatenate([top[:, 16:], sent[:, 16:], bottom[:, 16:]], 0)
+    starts = jnp.concatenate([top[:, :16], sent[:, :16], bottom[:, :16]], 0)
     left = lax.ppermute(ends, "py", ring("py", 1))
     right = lax.ppermute(starts, "py", ring("py", -1))
-    return block, top, bottom, left, right
+    return (block, top, bottom, left, right), beside
 
 
 def variation(pieces):
@@ -480,10 +495,10 @@
 
 def shards(estimate, observed, psf):
     transfer = transfer_function(psf, estimate.shape[2])
-    pieces = halos(estimate)
+    pieces, transfer = halos(estimate, transfer)
     quotient = convolve(pieces, transfer, observed, False)
     scaled = estimate / (1.0 - penalty_weight * variation(pieces))
-    return convolve(halos(quotient), transfer, scaled, True)
+    return convolve(halos(quotient)[0], transfer, scaled, True)
 
 
 def solution(mesh):

time: 91.8 us -> 76.6 us (0.83)
  Pallas kernels: 30.9 us -> 12.5 us
  local copies, waits for them, and re-layouts: 5.53 us -> 8.32 us
    pallas_call x2, Pallas kernels: 21.2 us -> 10.1 us  [convolve(): pl.pallas_call(functools.partial(convolve_kernel, adjoint), out_shape=jax...]
    ppermute x2, waiting for transfers between devices: 4.04 us -> 14.4 us  [halos(): right = lax.ppermute(starts, 'py', ring('py', -1))]
    ppermute x2, waiting for transfers between devices: 10.9 us -> 3.28 us  [halos(): top = lax.ppermute(block[16:], 'px', ring('px', 1))]
    pallas_call x1, Pallas kernels: 9.7 us -> 2.42 us  [transfer_function(): pl.pallas_call(transfer_kernel, out_shape=jax.ShapeDtypeStruct((PLANES, 2...]
    ppermute x2, starting transfers between devices: 0.01 us -> 4.25 us  [halos(): top = lax.ppermute(block[16:], 'px', ring('px', 1))]
    unnamed x20 -> x22, local copies, waits for them, and re-layouts: 3.05 us -> 6.92 us
    ppermute x2, waiting for transfers between devices: 7.14 us -> 4 us  [halos(): bottom = lax.ppermute(block[:16], 'px', ring('px', -1))]
    ppermute x2, starting transfers between devices: 13.4 us -> 10.8 us  [halos(): bottom = lax.ppermute(block[:16], 'px', ring('px', -1))]
  transfers between devices with their start and end apart: 8 -> 8, of which waited for: 7 -> 6; matrix products, arithmetic and copies ran while one was open for 4% -> 3% of each run, Pallas kernels for 11% -> 3%
where the time goes in v2:
time: 76.6 us; the launch traced here: 76.4 us
  waiting for transfers between devices  32.9 us (43%)
  starting transfers between devices  19.2 us (25%)
  Pallas kernels  12.5 us (16%)
  local copies, waits for them, and re-layouts  8.32 us (11%)
  other arithmetic  3.07 us (4%)
    ppermute x2, waiting for transfers between devices, halos(): right = lax.ppermute(starts, 'py', ring('py', -1))  14.4 us
    ppermute x2, waiting for transfers between devices, halos(): left = lax.ppermute(ends, 'py', ring('py', 1))  11.2 us
    ppermute x2, starting transfers between devices, halos(): bottom = lax.ppermute(block[:16], 'px', ring('px', -1))  10.8 us
    pallas_call x2, Pallas kernels, convolve(): pl.pallas_call(functools.partial(convolve_kernel, adjoint), out_shape=jax...  10.1 us
    unnamed x22, local copies, waits for them, and re-layouts  6.92 us
    ppermute x2, starting transfers between devices, halos(): top = lax.ppermute(block[16:], 'px', ring('px', 1))  4.25 us
    ppermute x2, starting transfers between devices, halos(): left = lax.ppermute(ends, 'py', ring('py', 1))  4.13 us
    ppermute x2, waiting for transfers between devices, halos(): bottom = lax.ppermute(block[:16], 'px', ring('px', -1))  4 us
  transfers between devices with their start and end apart: 8, of which 6 were waited for; matrix products, arithmetic and copies ran while one was open for 3% of the time, Pallas kernels for 3%

profile of v2, /device:TPU:1, one launch (start us, length us, event | category | flops | bytes accessed | tf_op | source)
XLA Modules:
  0.0 76.4 jit_solution(9380912646337368333)
XLA Ops:
  0.0 1.1 %fusion.13 = (f32[16,32,128]{2,1,0:T(8,128)S(1)}, f32[16,32,128]{2,1,0:T(8,128)S(1)}) fusion(f32[32,32,128]{2,1,0:T(8,128)} %own_ref.1), kind=kLoop, calls=%fused_computation.30 | loop fusion | bytes 1048576 | tf_op jit(solution)/shard_map/slice | solution.py:441
  1.1 3.8 %collective-permute-start = (f32[16,32,128]{2,1,0:T(8,128)S(1)}, f32[16,32,128]{2,1,0:T(8,128)S(1)}, u32[]{:S(2)}, u32[]{:S(2)}) collective-permute-start(f32[16,32,128]{2,1,0:T(8,128)S(1)} %get-tuple-element.20), channel_id=1, source_target_pairs={{0,16},{16,32},{32,48},{48,64},{64,80},{80,96},{96,112},{112,128},... | collective-permute-start | bytes 786440 | tf_op jit(solution)/shard_map/ppermute | solution.py:440
  4.9 5.4 %collective-permute-start.1 = (f32[16,32,128]{2,1,0:T(8,128)S(1)}, f32[16,32,128]{2,1,0:T(8,128)S(1)}, u32[]{:S(2)}, u32[]{:S(2)}) collective-permute-start(f32[16,32,128]{2,1,0:T(8,128)S(1)} %get-tuple-element.19), channel_id=1, source_target_pairs={{0,240},{16,0},{32,16},{48,32},{64,48},{80,64},{96,80},{112,96},{1... | collective-permute-start | bytes 786440 | tf_op jit(solution)/shard_map/ppermute | solution.py:441
  10.3 1.0 %copy-done.6 = f32[32,32,32]{2,1,0:T(8,128)S(1)} copy-done((f32[32,32,32]{2,1,0:T(8,128)S(1)}, f32[32,32,32]{2,1,0:T(8,128)}, u32[]{:S(2)}) %copy-start.6) | copy-done | bytes 131096
  11.4 0.8 %copy-done.9 = bf16[256,128]{1,0:T(8,128)(2,1)S(1)} copy-done((bf16[256,128]{1,0:T(8,128)(2,1)S(1)}, bf16[256,128]{1,0:T(8,128)(2,1)}, u32[]{:S(2)}) %copy-start.9) | copy-done | bytes 65560
  12.2 0.7 copy-done.10
  12.9 2.4 %transfer.1.transfer_ref = f32[34,256,128]{2,1,0:T(8,128)S(1)} custom-call(f32[32,32,32]{2,1,0:T(8,128)S(1)} %copy-done.6, f32[32,128]{1,0:T(8,128)S(1)} %copy-done.10, bf16[256,128]{1,0:T(8,128)(2,1)S(1)} %copy-done.9), custom_call_target="tpu_custom_call" | custom-call | tf_op jit(solution)/shard_map/transfer/pallas_call | solution.py:387
  15.4 2.0 %copy-done = f32[34,256,128]{2,1,0:T(8,128)} copy-done((f32[34,256,128]{2,1,0:T(8,128)}, f32[34,256,128]{2,1,0:T(8,128)S(1)}, u32[]{:S(2)}) %copy-start) | copy-done | bytes 4456472
  17.5 1.4 %collective-permute-done.1.bottom_ref = f32[16,32,128]{2,1,0:T(8,128)S(1)} collective-permute-done((f32[16,32,128]{2,1,0:T(8,128)S(1)}, f32[16,32,128]{2,1,0:T(8,128)S(1)}, u32[]{:S(2)}, u32[]{:S(2)}) %collective-permute-start.1) | collective-permute-done | bytes 262176 | tf_op jit(solution)/shard_map/ppermute | solution.py:441
  18.9 0.8 %pad_maximum_fusion.3 = f32[64,16,128]{2,1,0:T(8,128)} fusion(f32[16,16,128]{2,1,0:T(8,128)S(1)} %get-tuple-element.28, f32[32,16,128]{2,1,0:T(8,128)S(1)} %get-tuple-element.18, f32[16,16,128]{2,1,0:T(8,128)S(1)} %get-tuple-element.26), kind=kLoop, calls=%fused_computation.19 | loop fusion | flops 262144 | bytes 1048576 | tf_op jit(solution)/shard_map/concatenate | solution.py:445
  19.8 2.1 %collective-permute-start.2 = (f32[64,16,128]{2,1,0:T(8,128)}, f32[64,16,128]{2,1,0:T(8,128)S(1)}, u32[]{:S(2)}, u32[]{:S(2)}) collective-permute-start(f32[64,16,128]{2,1,0:T(8,128)} %pad_maximum_fusion.3), channel_id=1, source_target_pairs={{0,1},{1,2},{2,3},{3,4},{4,5},{5,6},{6,7},{7,8},{8,9},{9,10},{10,1... | collective-permute-start | bytes 1572872 | tf_op jit(solution)/shard_map/ppermute | solution.py:447
  21.9 0.8 %pad_maximum_fusion.4 = f32[64,16,128]{2,1,0:T(8,128)} fusion(f32[16,16,128]{2,1,0:T(8,128)S(1)} %get-tuple-element.27, f32[32,16,128]{2,1,0:T(8,128)S(1)} %get-tuple-element.17, f32[16,16,128]{2,1,0:T(8,128)S(1)} %get-tuple-element.25), kind=kLoop, calls=%fused_computation.20 | loop fusion | flops 262144 | bytes 1048576 | tf_op jit(solution)/shard_map/concatenate | solution.py:446
  22.8 11.2 %collective-permute-done.2.left_ref = f32[64,16,128]{2,1,0:T(8,128)S(1)} collective-permute-done((f32[64,16,128]{2,1,0:T(8,128)}, f32[64,16,128]{2,1,0:T(8,128)S(1)}, u32[]{:S(2)}, u32[]{:S(2)}) %collective-permute-start.2) | collective-permute-done | bytes 524320 | tf_op jit(solution)/shard_map/ppermute | solution.py:447
  34.3 2.9 %collective-permute-done.3.right_ref = f32[64,16,128]{2,1,0:T(8,128)S(1)} collective-permute-done((f32[64,16,128]{2,1,0:T(8,128)}, f32[64,16,128]{2,1,0:T(8,128)S(1)}, u32[]{:S(2)}, u32[]{:S(2)}) %collective-permute-start.3) | collective-permute-done | bytes 524320 | tf_op jit(solution)/shard_map/ppermute | solution.py:448
  37.2 2.3 %copy-done.1 = f32[34,256,128]{2,1,0:T(8,128)S(1)} copy-done((f32[34,256,128]{2,1,0:T(8,128)S(1)}, f32[34,256,128]{2,1,0:T(8,128)}, u32[]{:S(2)}) %copy-start.1) | copy-done | bytes 4456472
  39.5 4.6 %convolve.1.own_ref = f32[32,32,128]{2,1,0:T(8,128)S(1)} custom-call(f32[32,32,128]{2,1,0:T(8,128)S(1)} %copy-done.2, f32[16,32,128]{2,1,0:T(8,128)S(1)} %collective-permute-done.top_ref, f32[16,32,128]{2,1,0:T(8,128)S(1)} %collective-permute-done.1.bottom_ref, f32[64,16,128]{2,1,0:T(8,128)S(1)} %collective-permute-done.2.left_ref, ...), custom_call_target="tpu_custom_call" | custom-call | tf_op jit(solution)/shard_map/convolve/pallas_call | solution.py:410
  44.2 0.4 collective-permute-start.4
  44.6 5.4 %collective-permute-start.5 = (f32[16,32,128]{2,1,0:T(8,128)S(1)}, f32[16,32,128]{2,1,0:T(8,128)S(1)}, u32[]{:S(2)}, u32[]{:S(2)}) collective-permute-start(f32[16,32,128]{2,1,0:T(8,128)S(1)} %get-tuple-element.15), channel_id=1, source_target_pairs={{0,240},{16,0},{32,16},{48,32},{64,48},{80,64},{96,80},{112,96},{1... | collective-permute-start | bytes 786440 | tf_op jit(solution)/shard_map/ppermute | solution.py:441
  50.0 0.4 fusion.8
  50.5 3.3 %collective-permute-done.4.top_ref = f32[16,32,128]{2,1,0:T(8,128)S(1)} collective-permute-done((f32[16,32,128]{2,1,0:T(8,128)S(1)}, f32[16,32,128]{2,1,0:T(8,128)S(1)}, u32[]{:S(2)}, u32[]{:S(2)}) %collective-permute-start.4) | collective-permute-done | bytes 262176 | tf_op jit(solution)/shard_map/ppermute | solution.py:440
  53.8 2.6 %collective-permute-done.5.bottom_ref = f32[16,32,128]{2,1,0:T(8,128)S(1)} collective-permute-done((f32[16,32,128]{2,1,0:T(8,128)S(1)}, f32[16,32,128]{2,1,0:T(8,128)S(1)}, u32[]{:S(2)}, u32[]{:S(2)}) %collective-permute-start.5) | collective-permute-done | bytes 262176 | tf_op jit(solution)/shard_map/ppermute | solution.py:441
  56.6 2.0 %collective-permute-start.6 = (f32[64,16,128]{2,1,0:T(8,128)S(1)}, f32[64,16,128]{2,1,0:T(8,128)S(1)}, u32[]{:S(2)}, u32[]{:S(2)}) collective-permute-start(f32[64,16,128]{2,1,0:T(8,128)S(1)} %pad_maximum_fusion.5), channel_id=1, source_target_pairs={{0,1},{1,2},{2,3},{3,4},{4,5},{5,6},{6,7},{7,8},{8,9},{9,10},{10,1... | collective-permute-start | bytes 1572872 | tf_op jit(solution)/shard_map/ppermute | solution.py:447
  59.2 11.5 %collective-permute-done.7.right_ref = f32[64,16,128]{2,1,0:T(8,128)S(1)} collective-permute-done((f32[64,16,128]{2,1,0:T(8,128)S(1)}, f32[64,16,128]{2,1,0:T(8,128)S(1)}, u32[]{:S(2)}, u32[]{:S(2)}) %collective-permute-start.7) | collective-permute-done | bytes 524320 | tf_op jit(solution)/shard_map/ppermute | solution.py:448
  70.7 5.5 %correlate.1 = f32[32,32,128]{2,1,0:T(8,128)} custom-call(f32[32,32,128]{2,1,0:T(8,128)S(1)} %convolve.1.own_ref, f32[16,32,128]{2,1,0:T(8,128)S(1)} %collective-permute-done.4.top_ref, f32[16,32,128]{2,1,0:T(8,128)S(1)} %collective-permute-done.5.bottom_ref, f32[64,16,128]{2,1,0:T(8,128)S(1)} %collective-permute-done.6.left_ref, ...), custom_call_target="tpu_custom_call" | custom-call | tf_op jit(solution)/shard_map/correlate/pallas_call | solution.py:410
  (40 shorter events, 1.4 us)
Async XLA Ops:
  0.0 17.4 %copy-start.2 = (f32[32,32,128]{2,1,0:T(8,128)S(1)}, f32[32,32,128]{2,1,0:T(8,128)}, u32[]{:S(2)}) copy-start(f32[32,32,128]{2,1,0:T(8,128)} %own_ref.1) | copy-start | bytes 1572868
  1.1 16.4 %collective-permute-start = (f32[16,32,128]{2,1,0:T(8,128)S(1)}, f32[16,32,128]{2,1,0:T(8,128)S(1)}, u32[]{:S(2)}, u32[]{:S(2)}) collective-permute-start(f32[16,32,128]{2,1,0:T(8,128)S(1)} %get-tuple-element.20), channel_id=1, source_target_pairs={{0,16},{16,32},{32,48},{48,64},{64,80},{80,96},{96,112},{112,128},... | collective-permute-start | bytes 786440 | tf_op jit(solution)/shard_map/ppermute | solution.py:440
  4.9 14.0 %collective-permute-start.1 = (f32[16,32,128]{2,1,0:T(8,128)S(1)}, f32[16,32,128]{2,1,0:T(8,128)S(1)}, u32[]{:S(2)}, u32[]{:S(2)}) collective-permute-start(f32[16,32,128]{2,1,0:T(8,128)S(1)} %get-tuple-element.19), channel_id=1, source_target_pairs={{0,240},{16,0},{32,16},{48,32},{64,48},{80,64},{96,80},{112,96},{1... | collective-permute-start | bytes 786440 | tf_op jit(solution)/shard_map/ppermute | solution.py:441
  10.3 1.0 %copy-start.6 = (f32[32,32,32]{2,1,0:T(8,128)S(1)}, f32[32,32,32]{2,1,0:T(8,128)}, u32[]{:S(2)}) copy-start(f32[32,32,32]{2,1,0:T(8,128)} %psf_ref.1) | copy-start | bytes 393220
  11.4 0.8 %copy-start.9 = (bf16[256,128]{1,0:T(8,128)(2,1)S(1)}, bf16[256,128]{1,0:T(8,128)(2,1)}, u32[]{:S(2)}) copy-start(bf16[256,128]{1,0:T(8,128)(2,1)} %constant.40.clone.column_ref) | copy-start | bytes 196612
  12.2 0.7 copy-start.10
  15.4 2.1 %copy-start = (f32[34,256,128]{2,1,0:T(8,128)}, f32[34,256,128]{2,1,0:T(8,128)S(1)}, u32[]{:S(2)}) copy-start(f32[34,256,128]{2,1,0:T(8,128)S(1)} %transfer.1.transfer_ref) | copy-start | bytes 13369348
  17.4 19.8 %copy-start.3 = (bf16[256,256]{1,0:T(8,128)(2,1)S(1)}, bf16[256,256]{1,0:T(8,128)(2,1)}, u32[]{:S(2)}) copy-start(bf16[256,256]{1,0:T(8,128)(2,1)} %constant.41.clone.depth_ref) | copy-start | bytes 393220
  17.4 19.8 %copy-start.4 = (bf16[256,256]{1,0:T(8,128)(2,1)S(1)}, bf16[256,256]{1,0:T(8,128)(2,1)}, u32[]{:S(2)}) copy-start(bf16[256,256]{1,0:T(8,128)(2,1)} %constant.42.clone.column_ref) | copy-start | bytes 393220
  17.4 19.8 %copy-start.5 = (bf16[256,256]{1,0:T(8,128)(2,1)S(1)}, bf16[256,256]{1,0:T(8,128)(2,1)}, u32[]{:S(2)}) copy-start(bf16[256,256]{1,0:T(8,128)(2,1)} %constant.44.clone.depth_back_ref) | copy-start | bytes 393220
  17.4 19.8 %copy-start.7 = (f32[32,32,128]{2,1,0:T(8,128)S(1)}, f32[32,32,128]{2,1,0:T(8,128)}, u32[]{:S(2)}) copy-start(f32[32,32,128]{2,1,0:T(8,128)} %other_ref.1) | copy-start | bytes 1572868
  17.4 19.8 %copy-start.8 = (bf16[128,256]{1,0:T(8,128)(2,1)S(1)}, bf16[128,256]{1,0:T(8,128)(2,1)}, u32[]{:S(2)}) copy-start(bf16[128,256]{1,0:T(8,128)(2,1)} %constant.43.clone.column_back_ref) | copy-start | bytes 196612
  19.8 14.2 %collective-permute-start.2 = (f32[64,16,128]{2,1,0:T(8,128)}, f32[64,16,128]{2,1,0:T(8,128)S(1)}, u32[]{:S(2)}, u32[]{:S(2)}) collective-permute-start(f32[64,16,128]{2,1,0:T(8,128)} %pad_maximum_fusion.3), channel_id=1, source_target_pairs={{0,1},{1,2},{2,3},{3,4},{4,5},{5,6},{6,7},{7,8},{8,9},{9,10},{10,1... | collective-permute-start | bytes 1572872 | tf_op jit(solution)/shard_map/ppermute | solution.py:447
  22.8 14.4 %collective-permute-start.3 = (f32[64,16,128]{2,1,0:T(8,128)}, f32[64,16,128]{2,1,0:T(8,128)S(1)}, u32[]{:S(2)}, u32[]{:S(2)}) collective-permute-start(f32[64,16,128]{2,1,0:T(8,128)} %pad_maximum_fusion.4), channel_id=1, source_target_pairs={{0,15},{1,0},{2,1},{3,2},{4,3},{5,4},{6,5},{7,6},{8,7},{9,8},{10,9... | collective-permute-start | bytes 1572872 | tf_op jit(solution)/shard_map/ppermute | solution.py:448
  37.2 2.3 %copy-start.1 = (f32[34,256,128]{2,1,0:T(8,128)S(1)}, f32[34,256,128]{2,1,0:T(8,128)}, u32[]{:S(2)}) copy-start(f32[34,256,128]{2,1,0:T(8,128)} %copy-done) | copy-start | bytes 13369348
  44.2 9.6 %collective-permute-start.4 = (f32[16,32,128]{2,1,0:T(8,128)S(1)}, f32[16,32,128]{2,1,0:T(8,128)S(1)}, u32[]{:S(2)}, u32[]{:S(2)}) collective-permute-start(f32[16,32,128]{2,1,0:T(8,128)S(1)} %get-tuple-element.16), channel_id=1, source_target_pairs={{0,16},{16,32},{32,48},{48,64},{64,80},{80,96},{96,112},{112,128},... | collective-permute-start | bytes 786440 | tf_op jit(solution)/shard_map/ppermute | solution.py:440
  44.6 11.8 %collective-permute-start.5 = (f32[16,32,128]{2,1,0:T(8,128)S(1)}, f32[16,32,128]{2,1,0:T(8,128)S(1)}, u32[]{:S(2)}, u32[]{:S(2)}) collective-permute-start(f32[16,32,128]{2,1,0:T(8,128)S(1)} %get-tuple-element.15), channel_id=1, source_target_pairs={{0,240},{16,0},{32,16},{48,32},{64,48},{80,64},{96,80},{112,96},{1... | collective-permute-start | bytes 786440 | tf_op jit(solution)/shard_map/ppermute | solution.py:441
  56.4 14.3 %collective-permute-start.7 = (f32[64,16,128]{2,1,0:T(8,128)S(1)}, f32[64,16,128]{2,1,0:T(8,128)S(1)}, u32[]{:S(2)}, u32[]{:S(2)}) collective-permute-start(f32[64,16,128]{2,1,0:T(8,128)S(1)} %pad_maximum_fusion.6), channel_id=1, source_target_pairs={{0,15},{1,0},{2,1},{3,2},{4,3},{5,4},{6,5},{7,6},{8,7},{9,8},{10,9... | collective-permute-start | bytes 1572872 | tf_op jit(solution)/shard_map/ppermute | solution.py:448
  56.6 14.2 %collective-permute-start.6 = (f32[64,16,128]{2,1,0:T(8,128)S(1)}, f32[64,16,128]{2,1,0:T(8,128)S(1)}, u32[]{:S(2)}, u32[]{:S(2)}) collective-permute-start(f32[64,16,128]{2,1,0:T(8,128)S(1)} %pad_maximum_fusion.5), channel_id=1, source_target_pairs={{0,1},{1,2},{2,3},{3,4},{4,5},{5,6},{6,7},{7,8},{8,9},{9,10},{10,1... | collective-permute-start | bytes 1572872 | tf_op jit(solution)/shard_map/ppermute | solution.py:447

commit v3 on v2

--- a/solution.py
+++ b/solution.py
@@ -212,7 +212,7 @@
     return out[:half] + out[half:]
 
 
-def transfer_kernel(psf_ref, depth_ref, column_ref, out_ref, field, rows, factors, done):
+def transfer_kernel(psf_ref, depth_ref, column_ref, factors, field, rows):
     size = psf_ref.shape[0]
     for x in range(0, size, 8):
         values = psf_ref[x : x + 8].reshape(8 * size, size)
@@ -245,7 +245,6 @@
     real_lane = lane <= 64
     first_half = lane < 64
     alone = (lane == 0) | (lane == 64)
-    copies = []
     for p in range(0, PLANES, 2):
         both = along_columns(column_ref[...], jnp.concatenate([rows[p], rows[p + 1]], 1))
         for k in range(2):
@@ -255,23 +254,57 @@
             factors[p + k, 128:, :] = jnp.where(
                 alone, 0.0, jnp.where(first_half, -other, spectrum)
             )
-        if p + 2 in (PLANES // 2 + 1, PLANES):
-            part = pl.ds(0, p + 2) if not copies else pl.ds(PLANES // 2 + 1, PLANES // 2 - 1)
-            copies.append(
-                pltpu.make_async_copy(
-                    factors.at[part], out_ref.at[part], done.at[len(copies)]
-                )
-            )
-            copies[-1].start()
-    for copy in copies:
-        copy.wait()
+
+
+def depth_piece(ref, matrix, field, x_from, y_from):
+    count, width, lanes = ref.shape
+    step = 512 // width
+    for x in range(0, count, step):
+        values = ref[x : x + step].reshape(step * width, lanes)
+        field[x_from + x : x_from + x + step, y_from : y_from + width, :] = along_depth(
+            values, matrix
+        ).reshape(step, width, lanes)
+
+
+def row_transforms(field, rows, width):
+    zero = jnp.zeros((8, 128), jnp.float32)
+    rows[PLANES - 1] = jnp.zeros_like(rows[0])
+
+    def chunk(c, carry):
+        here = pl.ds(pl.multiple_of(c * 8, 8), 8)
+        there = pl.ds(pl.multiple_of(c * 8 + width, 8), 8)
+
+        def load(x):
+            return field[x, here, :]
+
+        def store(plane, real, imag):
+            rows[plane, here, :] = real
+            rows[plane, there, :] = imag
+
+        rows_forward(load, store, zero)
+        return carry
+
+    lax.fori_loop(0, width // 8, chunk, 0)
+
+
+def edges_kernel(own_ref, above_ref, below_ref, ends_ref, starts_ref):
+    for ref, at in ((above_ref, 0), (own_ref, 16), (below_ref, 48)):
+        count = ref.shape[0]
+        ends_ref[at : at + count] = ref[:, 16:, :]
+        starts_ref[at : at + count] = ref[:, :16, :]
+
+
+def inner_kernel(own_ref, above_ref, below_ref, depth_ref, rows_ref, field):
+    matrix = depth_ref[...]
+    depth_piece(own_ref, matrix, field, 16, 0)
+    depth_piece(above_ref, matrix, field, 0, 0)
+    depth_piece(below_ref, matrix, field, 48, 0)
+    row_transforms(field, rows_ref, 32)
 
 
 def convolve_kernel(
     adjoint,
-    own_ref,
-    top_ref,
-    bottom_ref,
+    inner_ref,
     left_ref,
     right_ref,
     transfer_ref,
@@ -283,64 +316,37 @@
     out_ref,
     field,
     rows,
+    spectra,
     back,
-    factors,
-    arrived,
 ):
-    fetch = pltpu.make_async_copy(transfer_ref, factors, arrived)
-    fetch.start()
     depth_matrix = depth_ref[...]
-
-    def depth_piece(ref, x_from, y_from, step):
-        count, width, lanes = ref.shape
-        for x in range(0, count, step):
-            values = ref[x : x + step].reshape(step * width, lanes)
-            field[x_from + x : x_from + x + step, y_from : y_from + width, :] = along_depth(
-                values, depth_matrix
-            ).reshape(step, width, lanes)
-
-    depth_piece(own_ref, 16, 16, 16)
-    depth_piece(top_ref, 0, 16, 16)
-    depth_piece(bottom_ref, 48, 16, 16)
-    depth_piece(left_ref, 0, 0, 32)
-    depth_piece(right_ref, 0, 48, 32)
-
-    zero = jnp.zeros((8, 128), jnp.float32)
-    rows[PLANES - 1] = jnp.zeros_like(rows[0])
-
-    def chunk(c, carry):
-        here = pl.ds(pl.multiple_of(c * 8, 8), 8)
-        there = pl.ds(pl.multiple_of(c * 8 + WINDOW, 8), 8)
-
-        def load(x):
-            return field[x, here, :]
-
-        def store(plane, real, imag):
-            rows[plane, here, :] = real
-            rows[plane, there, :] = imag
-
-        rows_forward(load, store, zero)
-        return carry
-
-    lax.fori_loop(0, WINDOW // 8, chunk, 0)
+    depth_piece(left_ref, depth_matrix, field, 0, 0)
+    depth_piece(right_ref, depth_matrix, field, 0, 16)
+    row_transforms(field, rows, 32)
 
     for p in range(0, PLANES, 2):
         spectrum = along_columns(
-            column_ref[...], jnp.concatenate([rows[p], rows[p + 1]], 1)
+            column_ref[...],
+            jnp.concatenate(
+                [
+                    jnp.concatenate([inner_ref[p], rows[p]], 0),
+                    jnp.concatenate([inner_ref[p + 1], rows[p + 1]], 0),
+                ],
+                1,
+            ),
         )
-        rows[p] = spectrum[:, :128]
-        rows[p + 1] = spectrum[:, 128:]
-
-    fetch.wait()
+        spectra[p] = spectrum[:, :128]
+        spectra[p + 1] = spectrum[:, 128:]
+
     for p in range(0, PLANES, 2):
         weighted = []
         for k in range(2):
-            own = rows[p + k]
+            own = spectra[p + k]
             partner = pltpu.roll(own, 64, 1)
             a, b = own[:64], own[64:]
             c, d = partner[:64], partner[64:]
-            fr, fi = factors[p + k, 0:64, :], factors[p + k, 64:128, :]
-            gr, gi = factors[p + k, 128:192, :], factors[p + k, 192:256, :]
+            fr, fi = transfer_ref[p + k, 0:64, :], transfer_ref[p + k, 64:128, :]
+            gr, gi = transfer_ref[p + k, 128:192, :], transfer_ref[p + k, 192:256, :]
             if adjoint:
                 real = (a * fr + b * fi) - (c * gr + d * gi)
                 imag = (b * fr - a * fi) - (d * gr - c * gi)
@@ -369,7 +375,7 @@
 
     matrix = depth_back_ref[...]
     for x in range(0, 32, 16):
-        values = field[16 + x : 32 + x, 0:32, :].reshape(512, 128)
+        values = field[16 + x : 32 + x].reshape(512, 128)
         result = along_depth(values, matrix).reshape(16, 32, 128)
         if adjoint:
             out_ref[x : x + 16] = other_ref[x : x + 16] * result
@@ -387,12 +393,10 @@
     return pl.pallas_call(
         transfer_kernel,
         out_shape=jax.ShapeDtypeStruct((PLANES, 256, depth), jnp.float32),
-        out_specs=pl.BlockSpec(memory_space=pltpu.HBM),
+        out_specs=vmem(1)[0],
         scratch_shapes=[
             pltpu.VMEM((size, size, depth), jnp.float32),
             pltpu.VMEM((PLANES, 2 * size, depth), jnp.float32),
-            pltpu.VMEM((PLANES, 256, depth), jnp.float32),
-            pltpu.SemaphoreType.DMA((2,)),
         ],
         compiler_params=pltpu.CompilerParams(vmem_limit_bytes=16 * 2**20),
         name="transfer",
@@ -403,61 +407,89 @@
     )
 
 
+def edges(own, above, below):
+    shape = jax.ShapeDtypeStruct((WINDOW, 16, own.shape[2]), jnp.float32)
+    return pl.pallas_call(
+        edges_kernel,
+        out_shape=(shape, shape),
+        in_specs=vmem(3),
+        out_specs=tuple(vmem(2)),
+        compiler_params=pltpu.CompilerParams(vmem_limit_bytes=2 * 2**20),
+        name="edges",
+    )(own, above, below)
+
+
 def convolve(pieces, transfer, other, adjoint):
+    own, above, below, left, right = pieces
     depth = other.shape[2]
     positions = np.arange(WINDOW)
     scale = 1.0 / (WINDOW * WINDOW * depth)
+    depth_matrix = right_operand(depth_forward(np.arange(depth), depth))
+    half_rows = (PLANES, WINDOW, depth)
+    inner = pl.pallas_call(
+        inner_kernel,
+        out_shape=jax.ShapeDtypeStruct(half_rows, jnp.float32),
+        in_specs=vmem(4),
+        out_specs=vmem(1)[0],
+        scratch_shapes=[pltpu.VMEM((WINDOW, 32, depth), jnp.float32)],
+        compiler_params=pltpu.CompilerParams(vmem_limit_bytes=16 * 2**20),
+        name="inner",
+    )(own, above, below, depth_matrix)
+    forward = np.concatenate(
+        [
+            column_forward(positions[16:48]),
+            column_forward(np.concatenate([positions[:16], positions[48:]])),
+        ],
+        1,
+    )
     return pl.pallas_call(
         functools.partial(convolve_kernel, adjoint),
         out_shape=jax.ShapeDtypeStruct(other.shape, jnp.float32),
-        in_specs=vmem(5) + [pl.BlockSpec(memory_space=pltpu.HBM)] + vmem(5),
-        out_specs=pl.BlockSpec(memory_space=pltpu.VMEM),
+        in_specs=vmem(9),
+        out_specs=vmem(1)[0],
         scratch_shapes=[
-            pltpu.VMEM((WINDOW, WINDOW, depth), jnp.float32),
+            pltpu.VMEM((WINDOW, 32, depth), jnp.float32),
+            pltpu.VMEM(half_rows, jnp.float32),
             pltpu.VMEM((PLANES, 2 * WINDOW, depth), jnp.float32),
-            pltpu.VMEM((PLANES, WINDOW, depth), jnp.float32),
-            pltpu.VMEM((PLANES, 256, depth), jnp.float32),
-            pltpu.SemaphoreType.DMA,
+            pltpu.VMEM(half_rows, jnp.float32),
         ],
         compiler_params=pltpu.CompilerParams(vmem_limit_bytes=20 * 2**20),
         name="correlate" if adjoint else "convolve",
     )(
-        *pieces,
+        inner,
+        left,
+        right,
         transfer,
         other,
-        right_operand(depth_forward(np.arange(depth), depth)),
-        left_operand(column_forward(positions)),
+        depth_matrix,
+        left_operand(forward),
         left_operand(column_inverse(positions[16:48])),
         right_operand(depth_inverse(depth) * scale),
     )
 
 
-def halos(block, beside=None):
+def halos(block):
     def ring(axis, step):
         count = lax.axis_size(axis)
         return [(i, (i + step) % count) for i in range(count)]
 
-    top = lax.ppermute(block[16:], "px", ring("px", 1))
-    bottom = lax.ppermute(block[:16], "px", ring("px", -1))
-    sent = block
-    if beside is not None:
-        sent, beside = lax.optimization_barrier((block, beside))
-    ends = jnp.concatenate([top[:, 16:], sent[:, 16:], bottom[:, 16:]], 0)
-    starts = jnp.concatenate([top[:, :16], sent[:, :16], bottom[:, :16]], 0)
+    above = lax.ppermute(block[16:], "px", ring("px", 1))
+    below = lax.ppermute(block[:16], "px", ring("px", -1))
+    ends, starts = edges(block, above, below)
     left = lax.ppermute(ends, "py", ring("py", 1))
     right = lax.ppermute(starts, "py", ring("py", -1))
-    return (block, top, bottom, left, right), beside
+    return block, above, below, left, right
 
 
 def variation(pieces):
-    volume, top, bottom, left, right = pieces
+    volume, above, below, left, right = pieces
     row_count, col_count, _ = volume.shape
     row_whole = row_count * lax.axis_size("px")
     col_whole = col_count * lax.axis_size("py")
     padded = jnp.concatenate(
         [
             left[15:49, 15:],
-            jnp.concatenate([top[15:], volume, bottom[:1]], 0),
+            jnp.concatenate([above[15:], volume, below[:1]], 0),
             right[15:49, :1],
         ],
         1,
@@ -495,10 +527,10 @@
 
 def shards(estimate, observed, psf):
     transfer = transfer_function(psf, estimate.shape[2])
-    pieces, transfer = halos(estimate, transfer)
+    pieces = halos(estimate)
     quotient = convolve(pieces, transfer, observed, False)
     scaled = estimate / (1.0 - penalty_weight * variation(pieces))
-    return convolve(halos(quotient)[0], transfer, scaled, True)
+    return convolve(halos(quotient), transfer, scaled, True)
 
 
 def solution(mesh):

time: 76.6 us -> 74 us (0.966)
  waiting for transfers between devices: 32.9 us -> 40.1 us
  local copies, waits for them, and re-layouts: 8.32 us -> 1.33 us
  other arithmetic: 3.07 us -> 1.38 us
    ppermute x4, waiting for transfers between devices: 7.28 us -> 19.1 us  [the longest x2 11.2 us: halos(): above = lax.ppermute(block[16:], 'px', ring('px', 1))]
    ppermute x2, waiting for transfers between devices: 14.4 us -> 3.21 us  [halos(): right = lax.ppermute(starts, 'py', ring('py', -1))]
    unnamed x22 -> x18, local copies, waits for them, and re-layouts: 6.92 us -> 0.05 us
    ppermute x2, waiting for transfers between devices: 11.2 us -> 17.9 us  [halos(): left = lax.ppermute(ends, 'py', ring('py', 1))]
    pallas_call x0 -> x4, Pallas kernels: none -> 2.69 us  [the longest x2 1.76 us: convolve(): pl.pallas_call(inner_kernel, out_shape=jax.ShapeDtypeStruct(half_rows, jn...]
    pallas_call x2, Pallas kernels: 10.1 us -> 7.73 us  [convolve(): pl.pallas_call(functools.partial(convolve_kernel, adjoint), out_shape=jax...]
    concatenate x5 -> x1, other arithmetic: 1.8 us -> 0.07 us  [variation(): jnp.concatenate([left[15:49, 15:], jnp.concatenate([above[15:], volume, b...]
  transfers between devices with their start and end apart: 8 -> 8, of which waited for: 6 -> 8; matrix products, arithmetic and copies ran while one was open for 3% -> 2% of each run, Pallas kernels for 3% -> 5%
where the time goes in v3:
time: 74 us; the launch traced here: 73.8 us
  waiting for transfers between devices  40.1 us (54%)
  starting transfers between devices  18.6 us (25%)
  Pallas kernels  12.2 us (16%)
  other arithmetic  1.38 us (2%)
  local copies, waits for them, and re-layouts  1.33 us (2%)
    ppermute x2, waiting for transfers between devices, halos(): left = lax.ppermute(ends, 'py', ring('py', 1))  17.9 us
    ppermute x2, starting transfers between devices, halos(): below = lax.ppermute(block[:16], 'px', ring('px', -1))  14.3 us
    ppermute x2, waiting for transfers between devices, halos(): above = lax.ppermute(block[16:], 'px', ring('px', 1))  11.2 us
    ppermute x2, waiting for transfers between devices, halos(): below = lax.ppermute(block[:16], 'px', ring('px', -1))  7.88 us
    pallas_call x2, Pallas kernels, convolve(): pl.pallas_call(functools.partial(convolve_kernel, adjoint), out_shape=jax...  7.73 us
    ppermute x2, starting transfers between devices, halos(): left = lax.ppermute(ends, 'py', ring('py', 1))  4.3 us
    ppermute x2, waiting for transfers between devices, halos(): right = lax.ppermute(starts, 'py', ring('py', -1))  3.21 us
    pallas_call x1, Pallas kernels, transfer_function(): pl.pallas_call(transfer_kernel, out_shape=jax.ShapeDtypeStruct((PLANES, 2...  1.8 us
  transfers between devices with their start and end apart: 8, of which 8 were waited for; matrix products, arithmetic and copies ran while one was open for 2% of the time, Pallas kernels for 5%

profile of v3, /device:TPU:1, one launch (start us, length us, event | category | flops | bytes accessed | tf_op | source)
XLA Modules:
  0.0 73.8 jit_solution(8944585568632356484)
XLA Ops:
  0.0 1.2 %fusion.11 = (f32[16,32,128]{2,1,0:T(8,128)S(1)}, f32[16,32,128]{2,1,0:T(8,128)S(1)}) fusion(f32[32,32,128]{2,1,0:T(8,128)} %own_ref.3), kind=kLoop, calls=%fused_computation.24 | loop fusion | bytes 1048576 | tf_op jit(solution)/shard_map/slice | solution.py:477
  1.2 9.1 %collective-permute-start.1 = (f32[16,32,128]{2,1,0:T(8,128)S(1)}, f32[16,32,128]{2,1,0:T(8,128)S(1)}, u32[]{:S(2)}, u32[]{:S(2)}) collective-permute-start(f32[16,32,128]{2,1,0:T(8,128)S(1)} %get-tuple-element.19), channel_id=1, source_target_pairs={{0,240},{16,0},{32,16},{48,32},{64,48},{80,64},{96,80},{112,96},{1... | collective-permute-start | bytes 786440 | tf_op jit(solution)/shard_map/ppermute | solution.py:477
  10.3 5.0 %collective-permute-done.1.below_ref = f32[16,32,128]{2,1,0:T(8,128)S(1)} collective-permute-done((f32[16,32,128]{2,1,0:T(8,128)S(1)}, f32[16,32,128]{2,1,0:T(8,128)S(1)}, u32[]{:S(2)}, u32[]{:S(2)}) %collective-permute-start.1) | collective-permute-done | bytes 262176 | tf_op jit(solution)/shard_map/ppermute | solution.py:477
  15.3 5.5 %collective-permute-done.above_ref = f32[16,32,128]{2,1,0:T(8,128)S(1)} collective-permute-done((f32[16,32,128]{2,1,0:T(8,128)S(1)}, f32[16,32,128]{2,1,0:T(8,128)S(1)}, u32[]{:S(2)}, u32[]{:S(2)}) %collective-permute-start) | collective-permute-done | bytes 262176 | tf_op jit(solution)/shard_map/ppermute | solution.py:476
  20.8 0.9 %edges.2 = (f32[64,16,128]{2,1,0:T(8,128)}, f32[64,16,128]{2,1,0:T(8,128)S(1)}) custom-call(f32[32,32,128]{2,1,0:T(8,128)S(1)} %copy-done, f32[16,32,128]{2,1,0:T(8,128)S(1)} %collective-permute-done.above_ref, f32[16,32,128]{2,1,0:T(8,128)S(1)} %collective-permute-done.1.below_ref), custom_call_target="tpu_custom_call" | custom-call | tf_op jit(solution)/shard_map/edges/pallas_call | solution.py:412
  21.6 2.1 %collective-permute-start.2 = (f32[64,16,128]{2,1,0:T(8,128)}, f32[64,16,128]{2,1,0:T(8,128)S(1)}, u32[]{:S(2)}, u32[]{:S(2)}) collective-permute-start(f32[64,16,128]{2,1,0:T(8,128)} %get-tuple-element.9), channel_id=1, source_target_pairs={{0,1},{1,2},{2,3},{3,4},{4,5},{5,6},{6,7},{7,8},{8,9},{9,10},{10,1... | collective-permute-start | bytes 1572872 | tf_op jit(solution)/shard_map/ppermute | solution.py:479
  23.8 1.8 %transfer.1.transfer_ref = f32[34,256,128]{2,1,0:T(8,128)S(1)} custom-call(f32[32,32,32]{2,1,0:T(8,128)S(1)} %copy-done.4, f32[32,128]{1,0:T(8,128)S(1)} %copy-done.8, bf16[256,128]{1,0:T(8,128)(2,1)S(1)} %copy-done.7), custom_call_target="tpu_custom_call" | custom-call | tf_op jit(solution)/shard_map/transfer/pallas_call | solution.py:393
  25.7 0.9 %inner.2.inner_ref = f32[34,64,128]{2,1,0:T(8,128)S(1)} custom-call(f32[32,32,128]{2,1,0:T(8,128)S(1)} %copy-done, f32[16,32,128]{2,1,0:T(8,128)S(1)} %collective-permute-done.above_ref, f32[16,32,128]{2,1,0:T(8,128)S(1)} %collective-permute-done.1.below_ref, bf16[256,256]{1,0:T(8,128)(2,1)S(1)} %copy-done.1), custom_call_target="tpu_custom_call" | custom-call | tf_op jit(solution)/shard_map/inner/pallas_call | solution.py:429
  26.6 9.3 %collective-permute-done.2.left_ref = f32[64,16,128]{2,1,0:T(8,128)S(1)} collective-permute-done((f32[64,16,128]{2,1,0:T(8,128)}, f32[64,16,128]{2,1,0:T(8,128)S(1)}, u32[]{:S(2)}, u32[]{:S(2)}) %collective-permute-start.2) | collective-permute-done | bytes 524320 | tf_op jit(solution)/shard_map/ppermute | solution.py:479
  35.9 0.1 maximum_maximum_fusion
  36.0 0.2 slice_subtract_fusion
  36.2 1.8 %collective-permute-done.3.right_ref = f32[64,16,128]{2,1,0:T(8,128)S(1)} collective-permute-done((f32[64,16,128]{2,1,0:T(8,128)S(1)}, f32[64,16,128]{2,1,0:T(8,128)S(1)}, u32[]{:S(2)}, u32[]{:S(2)}) %collective-permute-start.3) | collective-permute-done | bytes 524320 | tf_op jit(solution)/shard_map/ppermute | solution.py:480
  38.0 3.5 %convolve.1.own_ref = f32[32,32,128]{2,1,0:T(8,128)S(1)} custom-call(f32[34,64,128]{2,1,0:T(8,128)S(1)} %inner.2.inner_ref, f32[64,16,128]{2,1,0:T(8,128)S(1)} %collective-permute-done.2.left_ref, f32[64,16,128]{2,1,0:T(8,128)S(1)} %collective-permute-done.3.right_ref, f32[34,256,128]{2,1,0:T(8,128)S(1)} %transfer.1.transfer_ref, ...), custom_call_target="tpu_custom_call" | custom-call | tf_op jit(solution)/shard_map/convolve/pallas_call | solution.py:445
  41.5 5.2 %collective-permute-start.5 = (f32[16,32,128]{2,1,0:T(8,128)S(1)}, f32[16,32,128]{2,1,0:T(8,128)S(1)}, u32[]{:S(2)}, u32[]{:S(2)}) collective-permute-start(f32[16,32,128]{2,1,0:T(8,128)S(1)} %get-tuple-element.17), channel_id=1, source_target_pairs={{0,240},{16,0},{32,16},{48,32},{64,48},{80,64},{96,80},{112,96},{1... | collective-permute-start | bytes 786440 | tf_op jit(solution)/shard_map/ppermute | solution.py:477
  46.7 0.4 fusion.8
  47.1 2.9 %collective-permute-done.5.below_ref = f32[16,32,128]{2,1,0:T(8,128)S(1)} collective-permute-done((f32[16,32,128]{2,1,0:T(8,128)S(1)}, f32[16,32,128]{2,1,0:T(8,128)S(1)}, u32[]{:S(2)}, u32[]{:S(2)}) %collective-permute-start.5) | collective-permute-done | bytes 262176 | tf_op jit(solution)/shard_map/ppermute | solution.py:477
  50.0 5.7 %collective-permute-done.4.above_ref = f32[16,32,128]{2,1,0:T(8,128)S(1)} collective-permute-done((f32[16,32,128]{2,1,0:T(8,128)S(1)}, f32[16,32,128]{2,1,0:T(8,128)S(1)}, u32[]{:S(2)}, u32[]{:S(2)}) %collective-permute-start.4) | collective-permute-done | bytes 262176 | tf_op jit(solution)/shard_map/ppermute | solution.py:476
  55.8 2.1 %collective-permute-start.6 = (f32[64,16,128]{2,1,0:T(8,128)S(1)}, f32[64,16,128]{2,1,0:T(8,128)S(1)}, u32[]{:S(2)}, u32[]{:S(2)}) collective-permute-start(f32[64,16,128]{2,1,0:T(8,128)S(1)} %get-tuple-element.11), channel_id=1, source_target_pairs={{0,1},{1,2},{2,3},{3,4},{4,5},{5,6},{6,7},{7,8},{8,9},{9,10},{10,1... | collective-permute-start | bytes 1572872 | tf_op jit(solution)/shard_map/ppermute | solution.py:479
  58.0 0.2 fusion.9
  58.3 0.4 fusion.6.other_ref
  58.7 0.9 %inner.3.inner_ref = f32[34,64,128]{2,1,0:T(8,128)S(1)} custom-call(f32[32,32,128]{2,1,0:T(8,128)S(1)} %convolve.1.own_ref, f32[16,32,128]{2,1,0:T(8,128)S(1)} %collective-permute-done.4.above_ref, f32[16,32,128]{2,1,0:T(8,128)S(1)} %collective-permute-done.5.below_ref, bf16[256,256]{1,0:T(8,128)(2,1)S(1)} %copy-done.1), custom_call_target="tpu_custom_call" | custom-call | tf_op jit(solution)/shard_map/inner/pallas_call | solution.py:429
  59.6 8.6 %collective-permute-done.6.left_ref = f32[64,16,128]{2,1,0:T(8,128)S(1)} collective-permute-done((f32[64,16,128]{2,1,0:T(8,128)S(1)}, f32[64,16,128]{2,1,0:T(8,128)S(1)}, u32[]{:S(2)}, u32[]{:S(2)}) %collective-permute-start.6) | collective-permute-done | bytes 524320 | tf_op jit(solution)/shard_map/ppermute | solution.py:479
  68.1 1.4 %collective-permute-done.7.right_ref = f32[64,16,128]{2,1,0:T(8,128)S(1)} collective-permute-done((f32[64,16,128]{2,1,0:T(8,128)S(1)}, f32[64,16,128]{2,1,0:T(8,128)S(1)}, u32[]{:S(2)}, u32[]{:S(2)}) %collective-permute-start.7) | collective-permute-done | bytes 524320 | tf_op jit(solution)/shard_map/ppermute | solution.py:480
  69.6 4.3 %correlate.1 = f32[32,32,128]{2,1,0:T(8,128)} custom-call(f32[34,64,128]{2,1,0:T(8,128)S(1)} %inner.3.inner_ref, f32[64,16,128]{2,1,0:T(8,128)S(1)} %collective-permute-done.6.left_ref, f32[64,16,128]{2,1,0:T(8,128)S(1)} %collective-permute-done.7.right_ref, f32[34,256,128]{2,1,0:T(8,128)S(1)} %transfer.1.transfer_ref, f32[32,32,128]{2,1,0:T(8,128)S(1)} %fusion.6.other_ref, ...), custom_call_target="tpu_custom_call" | custom-call | tf_op jit(solution)/shard_map/correlate/pallas_call | solution.py:445
  (30 shorter events, 0.3 us)
Async XLA Ops:
  0.0 23.8 %copy-start.7 = (bf16[256,128]{1,0:T(8,128)(2,1)S(1)}, bf16[256,128]{1,0:T(8,128)(2,1)}, u32[]{:S(2)}) copy-start(bf16[256,128]{1,0:T(8,128)(2,1)} %constant.40.clone.column_ref) | copy-start | bytes 196612
  0.0 23.8 %copy-start.8 = (f32[32,128]{1,0:T(8,128)S(1)}, f32[32,128]{1,0:T(8,128)}, u32[]{:S(2)}) copy-start(f32[32,128]{1,0:T(8,128)} %constant.39.clone.depth_ref) | copy-start | bytes 49156
  0.0 20.8 %copy-start = (f32[32,32,128]{2,1,0:T(8,128)S(1)}, f32[32,32,128]{2,1,0:T(8,128)}, u32[]{:S(2)}) copy-start(f32[32,32,128]{2,1,0:T(8,128)} %own_ref.3) | copy-start | bytes 1572868
  0.0 23.8 %copy-start.4 = (f32[32,32,32]{2,1,0:T(8,128)S(1)}, f32[32,32,32]{2,1,0:T(8,128)}, u32[]{:S(2)}) copy-start(f32[32,32,32]{2,1,0:T(8,128)} %psf_ref.1) | copy-start | bytes 393220
  1.2 14.1 %collective-permute-start.1 = (f32[16,32,128]{2,1,0:T(8,128)S(1)}, f32[16,32,128]{2,1,0:T(8,128)S(1)}, u32[]{:S(2)}, u32[]{:S(2)}) collective-permute-start(f32[16,32,128]{2,1,0:T(8,128)S(1)} %get-tuple-element.19), channel_id=1, source_target_pairs={{0,240},{16,0},{32,16},{48,32},{64,48},{80,64},{96,80},{112,96},{1... | collective-permute-start | bytes 786440 | tf_op jit(solution)/shard_map/ppermute | solution.py:477
  10.3 10.5 %collective-permute-start = (f32[16,32,128]{2,1,0:T(8,128)S(1)}, f32[16,32,128]{2,1,0:T(8,128)S(1)}, u32[]{:S(2)}, u32[]{:S(2)}) collective-permute-start(f32[16,32,128]{2,1,0:T(8,128)S(1)} %get-tuple-element.20), channel_id=1, source_target_pairs={{0,16},{16,32},{32,48},{48,64},{64,80},{80,96},{96,112},{112,128},... | collective-permute-start | bytes 786440 | tf_op jit(solution)/shard_map/ppermute | solution.py:476
  21.6 14.2 %collective-permute-start.2 = (f32[64,16,128]{2,1,0:T(8,128)}, f32[64,16,128]{2,1,0:T(8,128)S(1)}, u32[]{:S(2)}, u32[]{:S(2)}) collective-permute-start(f32[64,16,128]{2,1,0:T(8,128)} %get-tuple-element.9), channel_id=1, source_target_pairs={{0,1},{1,2},{2,3},{3,4},{4,5},{5,6},{6,7},{7,8},{8,9},{9,10},{10,1... | collective-permute-start | bytes 1572872 | tf_op jit(solution)/shard_map/ppermute | solution.py:479
  23.8 14.2 %collective-permute-start.3 = (f32[64,16,128]{2,1,0:T(8,128)S(1)}, f32[64,16,128]{2,1,0:T(8,128)S(1)}, u32[]{:S(2)}, u32[]{:S(2)}) collective-permute-start(f32[64,16,128]{2,1,0:T(8,128)S(1)} %get-tuple-element.10), channel_id=1, source_target_pairs={{0,15},{1,0},{2,1},{3,2},{4,3},{5,4},{6,5},{7,6},{8,7},{9,8},{10,9... | collective-permute-start | bytes 1572872 | tf_op jit(solution)/shard_map/ppermute | solution.py:480
  23.8 1.9 %copy-start.1 = (bf16[256,256]{1,0:T(8,128)(2,1)S(1)}, bf16[256,256]{1,0:T(8,128)(2,1)}, u32[]{:S(2)}) copy-start(bf16[256,256]{1,0:T(8,128)(2,1)} %constant.41.clone.depth_ref) | copy-start | bytes 393220
  35.9 2.1 %copy-start.2 = (bf16[256,256]{1,0:T(8,128)(2,1)S(1)}, bf16[256,256]{1,0:T(8,128)(2,1)}, u32[]{:S(2)}) copy-start(bf16[256,256]{1,0:T(8,128)(2,1)} %constant.44.clone.depth_back_ref) | copy-start | bytes 393220
  35.9 2.1 %copy-start.3 = (bf16[256,256]{1,0:T(8,128)(2,1)S(1)}, bf16[256,256]{1,0:T(8,128)(2,1)}, u32[]{:S(2)}) copy-start(bf16[256,256]{1,0:T(8,128)(2,1)} %constant.42.clone.column_ref) | copy-start | bytes 393220
  36.0 2.0 %copy-start.5 = (f32[32,32,128]{2,1,0:T(8,128)S(1)}, f32[32,32,128]{2,1,0:T(8,128)}, u32[]{:S(2)}) copy-start(f32[32,32,128]{2,1,0:T(8,128)} %other_ref.1) | copy-start | bytes 1572868
  36.0 2.0 %copy-start.6 = (bf16[128,256]{1,0:T(8,128)(2,1)S(1)}, bf16[128,256]{1,0:T(8,128)(2,1)}, u32[]{:S(2)}) copy-start(bf16[128,256]{1,0:T(8,128)(2,1)} %constant.43.clone.column_back_ref) | copy-start | bytes 196612
  41.5 8.5 %collective-permute-start.5 = (f32[16,32,128]{2,1,0:T(8,128)S(1)}, f32[16,32,128]{2,1,0:T(8,128)S(1)}, u32[]{:S(2)}, u32[]{:S(2)}) collective-permute-start(f32[16,32,128]{2,1,0:T(8,128)S(1)} %get-tuple-element.17), channel_id=1, source_target_pairs={{0,240},{16,0},{32,16},{48,32},{64,48},{80,64},{96,80},{112,96},{1... | collective-permute-start | bytes 786440 | tf_op jit(solution)/shard_map/ppermute | solution.py:477
  46.7 9.1 %collective-permute-start.4 = (f32[16,32,128]{2,1,0:T(8,128)S(1)}, f32[16,32,128]{2,1,0:T(8,128)S(1)}, u32[]{:S(2)}, u32[]{:S(2)}) collective-permute-start(f32[16,32,128]{2,1,0:T(8,128)S(1)} %get-tuple-element.18), channel_id=1, source_target_pairs={{0,16},{16,32},{32,48},{48,64},{64,80},{80,96},{96,112},{112,128},... | collective-permute-start | bytes 786440 | tf_op jit(solution)/shard_map/ppermute | solution.py:476
  55.8 12.3 %collective-permute-start.6 = (f32[64,16,128]{2,1,0:T(8,128)S(1)}, f32[64,16,128]{2,1,0:T(8,128)S(1)}, u32[]{:S(2)}, u32[]{:S(2)}) collective-permute-start(f32[64,16,128]{2,1,0:T(8,128)S(1)} %get-tuple-element.11), channel_id=1, source_target_pairs={{0,1},{1,2},{2,3},{3,4},{4,5},{5,6},{6,7},{7,8},{8,9},{9,10},{10,1... | collective-permute-start | bytes 1572872 | tf_op jit(solution)/shard_map/ppermute | solution.py:479
  58.0 11.6 %collective-permute-start.7 = (f32[64,16,128]{2,1,0:T(8,128)S(1)}, f32[64,16,128]{2,1,0:T(8,128)S(1)}, u32[]{:S(2)}, u32[]{:S(2)}) collective-permute-start(f32[64,16,128]{2,1,0:T(8,128)S(1)} %get-tuple-element.12), channel_id=1, source_target_pairs={{0,15},{1,0},{2,1},{3,2},{4,3},{5,4},{6,5},{7,6},{8,7},{9,8},{10,9... | collective-permute-start | bytes 1572872 | tf_op jit(solution)/shard_map/ppermute | solution.py:480

commit v4 on v3

--- a/solution.py
+++ b/solution.py
@@ -294,6 +294,18 @@
         starts_ref[at : at + count] = ref[:, :16, :]
 
 
+def split_kernel(block_ref, whole_ref, last_ref, first_ref, done):
+    rows = (pl.ds(16, 16), last_ref), (pl.ds(0, 16), first_ref), (pl.ds(0, 32), whole_ref)
+    copies = [
+        pltpu.make_async_copy(block_ref.at[part], ref, done.at[i])
+        for i, (part, ref) in enumerate(rows)
+    ]
+    for copy in copies:
+        copy.start()
+    for copy in copies:
+        copy.wait()
+
+
 def inner_kernel(own_ref, above_ref, below_ref, depth_ref, rows_ref, field):
     matrix = depth_ref[...]
     depth_piece(own_ref, matrix, field, 16, 0)
@@ -398,7 +410,7 @@
             pltpu.VMEM((size, size, depth), jnp.float32),
             pltpu.VMEM((PLANES, 2 * size, depth), jnp.float32),
         ],
-        compiler_params=pltpu.CompilerParams(vmem_limit_bytes=16 * 2**20),
+        compiler_params=pltpu.CompilerParams(vmem_limit_bytes=8 * 2**20),
         name="transfer",
     )(
         psf,
@@ -417,6 +429,19 @@
         compiler_params=pltpu.CompilerParams(vmem_limit_bytes=2 * 2**20),
         name="edges",
     )(own, above, below)
+
+
+def split(block):
+    shape = jax.ShapeDtypeStruct((16,) + block.shape[1:], jnp.float32)
+    return pl.pallas_call(
+        split_kernel,
+        out_shape=(jax.ShapeDtypeStruct(block.shape, jnp.float32), shape, shape),
+        in_specs=[pl.BlockSpec(memory_space=pltpu.HBM)],
+        out_specs=tuple(vmem(3)),
+        scratch_shapes=[pltpu.SemaphoreType.DMA((3,))],
+        compiler_params=pltpu.CompilerParams(vmem_limit_bytes=2**20),
+        name="split",
+    )(block)
 
 
 def convolve(pieces, transfer, other, adjoint):
@@ -432,7 +457,7 @@
         in_specs=vmem(4),
         out_specs=vmem(1)[0],
         scratch_shapes=[pltpu.VMEM((WINDOW, 32, depth), jnp.float32)],
-        compiler_params=pltpu.CompilerParams(vmem_limit_bytes=16 * 2**20),
+        compiler_params=pltpu.CompilerParams(vmem_limit_bytes=4 * 2**20),
         name="inner",
     )(own, above, below, depth_matrix)
     forward = np.concatenate(
@@ -473,8 +498,9 @@
         count = lax.axis_size(axis)
         return [(i, (i + step) % count) for i in range(count)]
 
-    above = lax.ppermute(block[16:], "px", ring("px", 1))
-    below = lax.ppermute(block[:16], "px", ring("px", -1))
+    block, last, first = split(block)
+    above = lax.ppermute(last, "px", ring("px", 1))
+    below = lax.ppermute(first, "px", ring("px", -1))
     ends, starts = edges(block, above, below)
     left = lax.ppermute(ends, "py", ring("py", 1))
     right = lax.ppermute(starts, "py", ring("py", -1))
@@ -529,7 +555,7 @@
     transfer = transfer_function(psf, estimate.shape[2])
     pieces = halos(estimate)
     quotient = convolve(pieces, transfer, observed, False)
-    scaled = estimate / (1.0 - penalty_weight * variation(pieces))
+    scaled = pieces[0] / (1.0 - penalty_weight * variation(pieces))
     return convolve(halos(quotient), transfer, scaled, True)
 
 

time: 74 us -> 72.5 us (0.980)
  waiting for transfers between devices: 40.1 us -> 39.1 us
    ppermute x4, waiting for transfers between devices: 19.1 us -> 15.8 us  [the longest x2 9.55 us: halos(): above = lax.ppermute(last, 'px', ring('px', 1))]
    ppermute x2, starting transfers between devices: 4.3 us -> 2.23 us  [halos(): left = lax.ppermute(ends, 'py', ring('py', 1))]
    slice x2 -> x0, local copies, waits for them, and re-layouts: 1.19 us -> none  [halos(): below = lax.ppermute(block[:16], 'px', ring('px', -1))]
    ppermute x2, waiting for transfers between devices: 3.21 us -> 4.37 us  [halos(): right = lax.ppermute(starts, 'py', ring('py', -1))]
    unnamed x18, local copies, waits for them, and re-layouts: 0.05 us -> 1.14 us
    ppermute x2, waiting for transfers between devices: 17.9 us -> 18.9 us  [halos(): left = lax.ppermute(ends, 'py', ring('py', 1))]
    ppermute x4, starting transfers between devices: 14.3 us -> 15.3 us  [the longest x2 10.8 us: halos(): below = lax.ppermute(first, 'px', ring('px', -1))]
where the time goes in v4:
time: 72.5 us; the launch traced here: 72.4 us
  waiting for transfers between devices  39.1 us (54%)
  starting transfers between devices  18 us (25%)
  Pallas kernels  12.4 us (17%)
  other arithmetic  1.39 us (2%)
  local copies, waits for them, and re-layouts  1.23 us (2%)
    ppermute x2, waiting for transfers between devices, halos(): left = lax.ppermute(ends, 'py', ring('py', 1))  18.9 us
    ppermute x2, starting transfers between devices, halos(): below = lax.ppermute(first, 'px', ring('px', -1))  10.8 us
    ppermute x2, waiting for transfers between devices, halos(): above = lax.ppermute(last, 'px', ring('px', 1))  9.55 us
    pallas_call x2, Pallas kernels, convolve(): pl.pallas_call(functools.partial(convolve_kernel, adjoint), out_shape=jax...  7.73 us
    ppermute x2, waiting for transfers between devices, halos(): below = lax.ppermute(first, 'px', ring('px', -1))  6.3 us
    ppermute x2, starting transfers between devices, halos(): above = lax.ppermute(last, 'px', ring('px', 1))  4.51 us
    ppermute x2, waiting for transfers between devices, halos(): right = lax.ppermute(starts, 'py', ring('py', -1))  4.37 us
    ppermute x2, starting transfers between devices, halos(): left = lax.ppermute(ends, 'py', ring('py', 1))  2.23 us
  transfers between devices with their start and end apart: 8, of which 8 were waited for; matrix products, arithmetic and copies ran while one was open for 2% of the time, Pallas kernels for 5%

profile of v4, /device:TPU:1, one launch (start us, length us, event | category | flops | bytes accessed | tf_op | source)
XLA Modules:
  0.0 72.4 jit_solution(14564192638966834446)
XLA Ops:
  0.0 1.1 %copy-done.5 = f32[32,32,128]{2,1,0:T(8,128)S(1)} copy-done((f32[32,32,128]{2,1,0:T(8,128)S(1)}, f32[32,32,128]{2,1,0:T(8,128)}, u32[]{:S(2)}) %copy-start.5) | copy-done | bytes 524312
  1.2 3.8 %collective-permute-start = (f32[16,32,128]{2,1,0:T(8,128)S(1)}, f32[16,32,128]{2,1,0:T(8,128)S(1)}, u32[]{:S(2)}, u32[]{:S(2)}) collective-permute-start(f32[16,32,128]{2,1,0:T(8,128)S(1)} %get-tuple-element.16), channel_id=1, source_target_pairs={{0,16},{16,32},{32,48},{48,64},{64,80},{80,96},{96,112},{112,128},... | collective-permute-start | bytes 786440 | tf_op jit(solution)/shard_map/ppermute | solution.py:502
  5.0 5.4 %collective-permute-start.1 = (f32[16,32,128]{2,1,0:T(8,128)S(1)}, f32[16,32,128]{2,1,0:T(8,128)S(1)}, u32[]{:S(2)}, u32[]{:S(2)}) collective-permute-start(f32[16,32,128]{2,1,0:T(8,128)S(1)} %get-tuple-element.17), channel_id=1, source_target_pairs={{0,240},{16,0},{32,16},{48,32},{64,48},{80,64},{96,80},{112,96},{1... | collective-permute-start | bytes 786440 | tf_op jit(solution)/shard_map/ppermute | solution.py:503
  10.4 6.0 %collective-permute-done.above_ref = f32[16,32,128]{2,1,0:T(8,128)S(1)} collective-permute-done((f32[16,32,128]{2,1,0:T(8,128)S(1)}, f32[16,32,128]{2,1,0:T(8,128)S(1)}, u32[]{:S(2)}, u32[]{:S(2)}) %collective-permute-start) | collective-permute-done | bytes 262176 | tf_op jit(solution)/shard_map/ppermute | solution.py:502
  16.4 2.6 %collective-permute-done.1.below_ref = f32[16,32,128]{2,1,0:T(8,128)S(1)} collective-permute-done((f32[16,32,128]{2,1,0:T(8,128)S(1)}, f32[16,32,128]{2,1,0:T(8,128)S(1)}, u32[]{:S(2)}, u32[]{:S(2)}) %collective-permute-start.1) | collective-permute-done | bytes 262176 | tf_op jit(solution)/shard_map/ppermute | solution.py:503
  19.0 0.9 %edges.2 = (f32[64,16,128]{2,1,0:T(8,128)}, f32[64,16,128]{2,1,0:T(8,128)S(1)}) custom-call(f32[32,32,128]{2,1,0:T(8,128)S(1)} %get-tuple-element.15.own_ref, f32[16,32,128]{2,1,0:T(8,128)S(1)} %collective-permute-done.above_ref, f32[16,32,128]{2,1,0:T(8,128)S(1)} %collective-permute-done.1.below_ref), custom_call_target="tpu_custom_call" | custom-call | tf_op jit(solution)/shard_map/edges/pallas_call | solution.py:424
  19.9 2.1 %collective-permute-start.2 = (f32[64,16,128]{2,1,0:T(8,128)}, f32[64,16,128]{2,1,0:T(8,128)S(1)}, u32[]{:S(2)}, u32[]{:S(2)}) collective-permute-start(f32[64,16,128]{2,1,0:T(8,128)} %get-tuple-element.18), channel_id=1, source_target_pairs={{0,1},{1,2},{2,3},{3,4},{4,5},{5,6},{6,7},{7,8},{8,9},{9,10},{10,1... | collective-permute-start | bytes 1572872 | tf_op jit(solution)/shard_map/ppermute | solution.py:505
  22.1 1.8 %transfer.1.transfer_ref = f32[34,256,128]{2,1,0:T(8,128)S(1)} custom-call(f32[32,32,32]{2,1,0:T(8,128)S(1)} %copy-done.3, f32[32,128]{1,0:T(8,128)S(1)} %copy-done.8, bf16[256,128]{1,0:T(8,128)(2,1)S(1)} %copy-done.7), custom_call_target="tpu_custom_call" | custom-call | tf_op jit(solution)/shard_map/transfer/pallas_call | solution.py:405
  23.9 0.9 %inner.2.inner_ref = f32[34,64,128]{2,1,0:T(8,128)S(1)} custom-call(f32[32,32,128]{2,1,0:T(8,128)S(1)} %get-tuple-element.15.own_ref, f32[16,32,128]{2,1,0:T(8,128)S(1)} %collective-permute-done.above_ref, f32[16,32,128]{2,1,0:T(8,128)S(1)} %collective-permute-done.1.below_ref, bf16[256,256]{1,0:T(8,128)(2,1)S(1)} %copy-done), custom_call_target="tpu_custom_call" | custom-call | tf_op jit(solution)/shard_map/inner/pallas_call | solution.py:454
  24.8 9.3 %collective-permute-done.2.left_ref = f32[64,16,128]{2,1,0:T(8,128)S(1)} collective-permute-done((f32[64,16,128]{2,1,0:T(8,128)}, f32[64,16,128]{2,1,0:T(8,128)S(1)}, u32[]{:S(2)}, u32[]{:S(2)}) %collective-permute-start.2) | collective-permute-done | bytes 524320 | tf_op jit(solution)/shard_map/ppermute | solution.py:505
  34.2 0.2 slice_subtract_fusion
  34.5 1.8 %collective-permute-done.3.right_ref = f32[64,16,128]{2,1,0:T(8,128)S(1)} collective-permute-done((f32[64,16,128]{2,1,0:T(8,128)S(1)}, f32[64,16,128]{2,1,0:T(8,128)S(1)}, u32[]{:S(2)}, u32[]{:S(2)}) %collective-permute-start.3) | collective-permute-done | bytes 524320 | tf_op jit(solution)/shard_map/ppermute | solution.py:506
  36.3 3.5 %convolve.1.block_ref = f32[32,32,128]{2,1,0:T(8,128)S(1)} custom-call(f32[34,64,128]{2,1,0:T(8,128)S(1)} %inner.2.inner_ref, f32[64,16,128]{2,1,0:T(8,128)S(1)} %collective-permute-done.2.left_ref, f32[64,16,128]{2,1,0:T(8,128)S(1)} %collective-permute-done.3.right_ref, f32[34,256,128]{2,1,0:T(8,128)S(1)} %transfer.1.transfer_ref, ...), custom_call_target="tpu_custom_call" | custom-call | tf_op jit(solution)/shard_map/convolve/pallas_call | solution.py:470
  39.9 0.7 collective-permute-start.4
  40.5 5.4 %collective-permute-start.5 = (f32[16,32,128]{2,1,0:T(8,128)S(1)}, f32[16,32,128]{2,1,0:T(8,128)S(1)}, u32[]{:S(2)}, u32[]{:S(2)}) collective-permute-start(f32[16,32,128]{2,1,0:T(8,128)S(1)} %get-tuple-element.22), channel_id=1, source_target_pairs={{0,240},{16,0},{32,16},{48,32},{64,48},{80,64},{96,80},{112,96},{1... | collective-permute-start | bytes 786440 | tf_op jit(solution)/shard_map/ppermute | solution.py:503
  45.9 0.4 fusion.8
  46.4 3.6 %collective-permute-done.4.above_ref = f32[16,32,128]{2,1,0:T(8,128)S(1)} collective-permute-done((f32[16,32,128]{2,1,0:T(8,128)S(1)}, f32[16,32,128]{2,1,0:T(8,128)S(1)}, u32[]{:S(2)}, u32[]{:S(2)}) %collective-permute-start.4) | collective-permute-done | bytes 262176 | tf_op jit(solution)/shard_map/ppermute | solution.py:502
  49.9 3.7 %collective-permute-done.5.below_ref = f32[16,32,128]{2,1,0:T(8,128)S(1)} collective-permute-done((f32[16,32,128]{2,1,0:T(8,128)S(1)}, f32[16,32,128]{2,1,0:T(8,128)S(1)}, u32[]{:S(2)}, u32[]{:S(2)}) %collective-permute-start.5) | collective-permute-done | bytes 262176 | tf_op jit(solution)/shard_map/ppermute | solution.py:503
  53.8 0.5 collective-permute-start.7
  54.6 0.4 fusion.6.other_ref
  55.0 0.9 %inner.3.inner_ref = f32[34,64,128]{2,1,0:T(8,128)S(1)} custom-call(f32[32,32,128]{2,1,0:T(8,128)S(1)} %get-tuple-element.20.own_ref, f32[16,32,128]{2,1,0:T(8,128)S(1)} %collective-permute-done.4.above_ref, f32[16,32,128]{2,1,0:T(8,128)S(1)} %collective-permute-done.5.below_ref, bf16[256,256]{1,0:T(8,128)(2,1)S(1)} %copy-done), custom_call_target="tpu_custom_call" | custom-call | tf_op jit(solution)/shard_map/inner/pallas_call | solution.py:454
  55.9 9.6 %collective-permute-done.6.left_ref = f32[64,16,128]{2,1,0:T(8,128)S(1)} collective-permute-done((f32[64,16,128]{2,1,0:T(8,128)S(1)}, f32[64,16,128]{2,1,0:T(8,128)S(1)}, u32[]{:S(2)}, u32[]{:S(2)}) %collective-permute-start.6) | collective-permute-done | bytes 524320 | tf_op jit(solution)/shard_map/ppermute | solution.py:505
  65.5 2.6 %collective-permute-done.7.right_ref = f32[64,16,128]{2,1,0:T(8,128)S(1)} collective-permute-done((f32[64,16,128]{2,1,0:T(8,128)S(1)}, f32[64,16,128]{2,1,0:T(8,128)S(1)}, u32[]{:S(2)}, u32[]{:S(2)}) %collective-permute-start.7) | collective-permute-done | bytes 524320 | tf_op jit(solution)/shard_map/ppermute | solution.py:506
  68.1 4.3 %correlate.1 = f32[32,32,128]{2,1,0:T(8,128)} custom-call(f32[34,64,128]{2,1,0:T(8,128)S(1)} %inner.3.inner_ref, f32[64,16,128]{2,1,0:T(8,128)S(1)} %collective-permute-done.6.left_ref, f32[64,16,128]{2,1,0:T(8,128)S(1)} %collective-permute-done.7.right_ref, f32[34,256,128]{2,1,0:T(8,128)S(1)} %transfer.1.transfer_ref, f32[32,32,128]{2,1,0:T(8,128)S(1)} %fusion.6.other_ref, ...), custom_call_target="tpu_custom_call" | custom-call | tf_op jit(solution)/shard_map/correlate/pallas_call | solution.py:470
  (30 shorter events, 0.8 us)
Async XLA Ops:
  0.0 22.0 %copy-start.3 = (f32[32,32,32]{2,1,0:T(8,128)S(1)}, f32[32,32,32]{2,1,0:T(8,128)}, u32[]{:S(2)}) copy-start(f32[32,32,32]{2,1,0:T(8,128)} %psf_ref.1) | copy-start | bytes 393220
  0.0 1.1 %copy-start.5 = (f32[32,32,128]{2,1,0:T(8,128)S(1)}, f32[32,32,128]{2,1,0:T(8,128)}, u32[]{:S(2)}) copy-start(f32[32,32,128]{2,1,0:T(8,128)} %block_ref.1) | copy-start | bytes 1572868
  1.1 20.9 %copy-start.7 = (bf16[256,128]{1,0:T(8,128)(2,1)S(1)}, bf16[256,128]{1,0:T(8,128)(2,1)}, u32[]{:S(2)}) copy-start(bf16[256,128]{1,0:T(8,128)(2,1)} %constant.40.clone.column_ref) | copy-start | bytes 196612
  1.1 20.9 %copy-start.8 = (f32[32,128]{1,0:T(8,128)S(1)}, f32[32,128]{1,0:T(8,128)}, u32[]{:S(2)}) copy-start(f32[32,128]{1,0:T(8,128)} %constant.39.clone.depth_ref) | copy-start | bytes 49156
  1.2 15.2 %collective-permute-start = (f32[16,32,128]{2,1,0:T(8,128)S(1)}, f32[16,32,128]{2,1,0:T(8,128)S(1)}, u32[]{:S(2)}, u32[]{:S(2)}) collective-permute-start(f32[16,32,128]{2,1,0:T(8,128)S(1)} %get-tuple-element.16), channel_id=1, source_target_pairs={{0,16},{16,32},{32,48},{48,64},{64,80},{80,96},{96,112},{112,128},... | collective-permute-start | bytes 786440 | tf_op jit(solution)/shard_map/ppermute | solution.py:502
  5.0 14.0 %collective-permute-start.1 = (f32[16,32,128]{2,1,0:T(8,128)S(1)}, f32[16,32,128]{2,1,0:T(8,128)S(1)}, u32[]{:S(2)}, u32[]{:S(2)}) collective-permute-start(f32[16,32,128]{2,1,0:T(8,128)S(1)} %get-tuple-element.17), channel_id=1, source_target_pairs={{0,240},{16,0},{32,16},{48,32},{64,48},{80,64},{96,80},{112,96},{1... | collective-permute-start | bytes 786440 | tf_op jit(solution)/shard_map/ppermute | solution.py:503
  19.9 14.2 %collective-permute-start.2 = (f32[64,16,128]{2,1,0:T(8,128)}, f32[64,16,128]{2,1,0:T(8,128)S(1)}, u32[]{:S(2)}, u32[]{:S(2)}) collective-permute-start(f32[64,16,128]{2,1,0:T(8,128)} %get-tuple-element.18), channel_id=1, source_target_pairs={{0,1},{1,2},{2,3},{3,4},{4,5},{5,6},{6,7},{7,8},{8,9},{9,10},{10,1... | collective-permute-start | bytes 1572872 | tf_op jit(solution)/shard_map/ppermute | solution.py:505
  22.0 14.2 %collective-permute-start.3 = (f32[64,16,128]{2,1,0:T(8,128)S(1)}, f32[64,16,128]{2,1,0:T(8,128)S(1)}, u32[]{:S(2)}, u32[]{:S(2)}) collective-permute-start(f32[64,16,128]{2,1,0:T(8,128)S(1)} %get-tuple-element.19), channel_id=1, source_target_pairs={{0,15},{1,0},{2,1},{3,2},{4,3},{5,4},{6,5},{7,6},{8,7},{9,8},{10,9... | collective-permute-start | bytes 1572872 | tf_op jit(solution)/shard_map/ppermute | solution.py:506
  22.0 1.9 %copy-start = (bf16[256,256]{1,0:T(8,128)(2,1)S(1)}, bf16[256,256]{1,0:T(8,128)(2,1)}, u32[]{:S(2)}) copy-start(bf16[256,256]{1,0:T(8,128)(2,1)} %constant.41.clone.depth_ref) | copy-start | bytes 393220
  34.2 2.1 %copy-start.1 = (bf16[256,256]{1,0:T(8,128)(2,1)S(1)}, bf16[256,256]{1,0:T(8,128)(2,1)}, u32[]{:S(2)}) copy-start(bf16[256,256]{1,0:T(8,128)(2,1)} %constant.44.clone.depth_back_ref) | copy-start | bytes 393220
  34.2 2.1 %copy-start.2 = (bf16[256,256]{1,0:T(8,128)(2,1)S(1)}, bf16[256,256]{1,0:T(8,128)(2,1)}, u32[]{:S(2)}) copy-start(bf16[256,256]{1,0:T(8,128)(2,1)} %constant.42.clone.column_ref) | copy-start | bytes 393220
  34.2 2.0 %copy-start.4 = (f32[32,32,128]{2,1,0:T(8,128)S(1)}, f32[32,32,128]{2,1,0:T(8,128)}, u32[]{:S(2)}) copy-start(f32[32,32,128]{2,1,0:T(8,128)} %other_ref.1) | copy-start | bytes 1572868
  34.2 2.0 %copy-start.6 = (bf16[128,256]{1,0:T(8,128)(2,1)S(1)}, bf16[128,256]{1,0:T(8,128)(2,1)}, u32[]{:S(2)}) copy-start(bf16[128,256]{1,0:T(8,128)(2,1)} %constant.43.clone.column_back_ref) | copy-start | bytes 196612
  39.9 10.1 %collective-permute-start.4 = (f32[16,32,128]{2,1,0:T(8,128)S(1)}, f32[16,32,128]{2,1,0:T(8,128)S(1)}, u32[]{:S(2)}, u32[]{:S(2)}) collective-permute-start(f32[16,32,128]{2,1,0:T(8,128)S(1)} %get-tuple-element.21), channel_id=1, source_target_pairs={{0,16},{16,32},{32,48},{48,64},{64,80},{80,96},{96,112},{112,128},... | collective-permute-start | bytes 786440 | tf_op jit(solution)/shard_map/ppermute | solution.py:502
  40.5 13.1 %collective-permute-start.5 = (f32[16,32,128]{2,1,0:T(8,128)S(1)}, f32[16,32,128]{2,1,0:T(8,128)S(1)}, u32[]{:S(2)}, u32[]{:S(2)}) collective-permute-start(f32[16,32,128]{2,1,0:T(8,128)S(1)} %get-tuple-element.22), channel_id=1, source_target_pairs={{0,240},{16,0},{32,16},{48,32},{64,48},{80,64},{96,80},{112,96},{1... | collective-permute-start | bytes 786440 | tf_op jit(solution)/shard_map/ppermute | solution.py:503
  53.7 11.8 %collective-permute-start.6 = (f32[64,16,128]{2,1,0:T(8,128)S(1)}, f32[64,16,128]{2,1,0:T(8,128)S(1)}, u32[]{:S(2)}, u32[]{:S(2)}) collective-permute-start(f32[64,16,128]{2,1,0:T(8,128)S(1)} %get-tuple-element.23), channel_id=1, source_target_pairs={{0,1},{1,2},{2,3},{3,4},{4,5},{5,6},{6,7},{7,8},{8,9},{9,10},{10,1... | collective-permute-start | bytes 1572872 | tf_op jit(solution)/shard_map/ppermute | solution.py:505
  53.8 14.3 %collective-permute-start.7 = (f32[64,16,128]{2,1,0:T(8,128)S(1)}, f32[64,16,128]{2,1,0:T(8,128)S(1)}, u32[]{:S(2)}, u32[]{:S(2)}) collective-permute-start(f32[64,16,128]{2,1,0:T(8,128)S(1)} %get-tuple-element.24), channel_id=1, source_target_pairs={{0,15},{1,0},{2,1},{3,2},{4,3},{5,4},{6,5},{7,6},{8,7},{9,8},{10,9... | collective-permute-start | bytes 1572872 | tf_op jit(solution)/shard_map/ppermute | solution.py:506

commit v5 on v4

--- a/solution.py
+++ b/solution.py
@@ -287,18 +287,16 @@
     lax.fori_loop(0, width // 8, chunk, 0)
 
 
-def edges_kernel(own_ref, above_ref, below_ref, ends_ref, starts_ref):
-    for ref, at in ((above_ref, 0), (own_ref, 16), (below_ref, 48)):
-        count = ref.shape[0]
-        ends_ref[at : at + count] = ref[:, 16:, :]
-        starts_ref[at : at + count] = ref[:, :16, :]
-
-
-def split_kernel(block_ref, whole_ref, last_ref, first_ref, done):
-    rows = (pl.ds(16, 16), last_ref), (pl.ds(0, 16), first_ref), (pl.ds(0, 32), whole_ref)
+def edges_kernel(first_ref, last_ref, above_ref, below_ref, ends_ref, starts_ref):
+    for i, ref in enumerate((above_ref, first_ref, last_ref, below_ref)):
+        ends_ref[16 * i : 16 * i + 16] = ref[:, 16:, :]
+        starts_ref[16 * i : 16 * i + 16] = ref[:, :16, :]
+
+
+def split_kernel(block_ref, first_ref, last_ref, done):
     copies = [
-        pltpu.make_async_copy(block_ref.at[part], ref, done.at[i])
-        for i, (part, ref) in enumerate(rows)
+        pltpu.make_async_copy(block_ref.at[pl.ds(16 * i, 16)], ref, done.at[i])
+        for i, ref in enumerate((first_ref, last_ref))
     ]
     for copy in copies:
         copy.start()
@@ -306,12 +304,14 @@
         copy.wait()
 
 
-def inner_kernel(own_ref, above_ref, below_ref, depth_ref, rows_ref, field):
+def columns_kernel(count, *refs):
+    pieces, (depth_ref, rows_ref, field) = refs[:count], refs[count:]
     matrix = depth_ref[...]
-    depth_piece(own_ref, matrix, field, 16, 0)
-    depth_piece(above_ref, matrix, field, 0, 0)
-    depth_piece(below_ref, matrix, field, 48, 0)
-    row_transforms(field, rows_ref, 32)
+    at = 0
+    for ref in pieces:
+        depth_piece(ref, matrix, field, at, 0)
+        at += ref.shape[0]
+    row_transforms(field, rows_ref, field.shape[1])
 
 
 def convolve_kernel(
@@ -325,24 +325,19 @@
     column_ref,
     column_back_ref,
     depth_back_ref,
-    out_ref,
-    field,
-    rows,
-    spectra,
-    back,
+    *out_refs_and_scratch,
 ):
-    depth_matrix = depth_ref[...]
-    depth_piece(left_ref, depth_matrix, field, 0, 0)
-    depth_piece(right_ref, depth_matrix, field, 0, 16)
-    row_transforms(field, rows, 32)
+    *out_refs, right_field, rows, spectra, back, field = out_refs_and_scratch
+    depth_piece(right_ref, depth_ref[...], right_field, 0, 0)
+    row_transforms(right_field, rows, 16)
 
     for p in range(0, PLANES, 2):
         spectrum = along_columns(
             column_ref[...],
             jnp.concatenate(
                 [
-                    jnp.concatenate([inner_ref[p], rows[p]], 0),
-                    jnp.concatenate([inner_ref[p + 1], rows[p + 1]], 0),
+                    jnp.concatenate([inner_ref[k], left_ref[k], rows[k]], 0)
+                    for k in (p, p + 1)
                 ],
                 1,
             ),
@@ -378,7 +373,7 @@
             return back[plane, here, :], back[plane, there, :]
 
         def store(x, value):
-            field[x, here, :] = value
+            field[x - 16, here, :] = value
 
         rows_inverse(load, store)
         return carry
@@ -387,12 +382,12 @@
 
     matrix = depth_back_ref[...]
     for x in range(0, 32, 16):
-        values = field[16 + x : 32 + x].reshape(512, 128)
+        values = field[x : 16 + x].reshape(512, 128)
         result = along_depth(values, matrix).reshape(16, 32, 128)
         if adjoint:
-            out_ref[x : x + 16] = other_ref[x : x + 16] * result
+            out_refs[0][x : x + 16] = other_ref[x : x + 16] * result
         else:
-            out_ref[x : x + 16] = other_ref[x : x + 16] / result
+            out_refs[x // 16][...] = other_ref[x : x + 16] / result
 
 
 def vmem(count):
@@ -419,64 +414,73 @@
     )
 
 
-def edges(own, above, below):
-    shape = jax.ShapeDtypeStruct((WINDOW, 16, own.shape[2]), jnp.float32)
+def edges(first, last, above, below):
+    shape = jax.ShapeDtypeStruct((WINDOW, 16, first.shape[2]), jnp.float32)
     return pl.pallas_call(
         edges_kernel,
         out_shape=(shape, shape),
-        in_specs=vmem(3),
+        in_specs=vmem(4),
         out_specs=tuple(vmem(2)),
         compiler_params=pltpu.CompilerParams(vmem_limit_bytes=2 * 2**20),
         name="edges",
-    )(own, above, below)
+    )(first, last, above, below)
 
 
 def split(block):
     shape = jax.ShapeDtypeStruct((16,) + block.shape[1:], jnp.float32)
     return pl.pallas_call(
         split_kernel,
-        out_shape=(jax.ShapeDtypeStruct(block.shape, jnp.float32), shape, shape),
+        out_shape=(shape, shape),
         in_specs=[pl.BlockSpec(memory_space=pltpu.HBM)],
-        out_specs=tuple(vmem(3)),
-        scratch_shapes=[pltpu.SemaphoreType.DMA((3,))],
+        out_specs=tuple(vmem(2)),
+        scratch_shapes=[pltpu.SemaphoreType.DMA((2,))],
         compiler_params=pltpu.CompilerParams(vmem_limit_bytes=2**20),
         name="split",
     )(block)
 
 
+def columns(pieces, depth_matrix, name):
+    _, width, depth = pieces[0].shape
+    return pl.pallas_call(
+        functools.partial(columns_kernel, len(pieces)),
+        out_shape=jax.ShapeDtypeStruct((PLANES, 2 * width, depth), jnp.float32),
+        in_specs=vmem(len(pieces) + 1),
+        out_specs=vmem(1)[0],
+        scratch_shapes=[pltpu.VMEM((WINDOW, width, depth), jnp.float32)],
+        compiler_params=pltpu.CompilerParams(vmem_limit_bytes=8 * 2**20),
+        name=name,
+    )(*pieces, depth_matrix)
+
+
 def convolve(pieces, transfer, other, adjoint):
-    own, above, below, left, right = pieces
+    first, last, above, below, left, right = pieces
     depth = other.shape[2]
     positions = np.arange(WINDOW)
     scale = 1.0 / (WINDOW * WINDOW * depth)
     depth_matrix = right_operand(depth_forward(np.arange(depth), depth))
-    half_rows = (PLANES, WINDOW, depth)
-    inner = pl.pallas_call(
-        inner_kernel,
-        out_shape=jax.ShapeDtypeStruct(half_rows, jnp.float32),
-        in_specs=vmem(4),
-        out_specs=vmem(1)[0],
-        scratch_shapes=[pltpu.VMEM((WINDOW, 32, depth), jnp.float32)],
-        compiler_params=pltpu.CompilerParams(vmem_limit_bytes=4 * 2**20),
-        name="inner",
-    )(own, above, below, depth_matrix)
+    inner = columns((above, first, last, below), depth_matrix, "inner")
+    left = columns((left,), depth_matrix, "left")
     forward = np.concatenate(
         [
             column_forward(positions[16:48]),
-            column_forward(np.concatenate([positions[:16], positions[48:]])),
+            column_forward(positions[:16]),
+            column_forward(positions[48:]),
         ],
         1,
     )
+    whole = jax.ShapeDtypeStruct(other.shape, jnp.float32)
+    half = jax.ShapeDtypeStruct((16,) + other.shape[1:], jnp.float32)
     return pl.pallas_call(
         functools.partial(convolve_kernel, adjoint),
-        out_shape=jax.ShapeDtypeStruct(other.shape, jnp.float32),
+        out_shape=whole if adjoint else (half, half),
         in_specs=vmem(9),
-        out_specs=vmem(1)[0],
+        out_specs=vmem(1)[0] if adjoint else tuple(vmem(2)),
         scratch_shapes=[
-            pltpu.VMEM((WINDOW, 32, depth), jnp.float32),
-            pltpu.VMEM(half_rows, jnp.float32),
+            pltpu.VMEM((WINDOW, 16, depth), jnp.float32),
+            pltpu.VMEM((PLANES, 32, depth), jnp.float32),
             pltpu.VMEM((PLANES, 2 * WINDOW, depth), jnp.float32),
-            pltpu.VMEM(half_rows, jnp.float32),
+            pltpu.VMEM((PLANES, WINDOW, depth), jnp.float32),
+            pltpu.VMEM((32, 32, depth), jnp.float32),
         ],
         compiler_params=pltpu.CompilerParams(vmem_limit_bytes=20 * 2**20),
         name="correlate" if adjoint else "convolve",
@@ -493,22 +497,21 @@
     )
 
 
-def halos(block):
+def halos(first, last):
     def ring(axis, step):
         count = lax.axis_size(axis)
         return [(i, (i + step) % count) for i in range(count)]
 
-    block, last, first = split(block)
     above = lax.ppermute(last, "px", ring("px", 1))
     below = lax.ppermute(first, "px", ring("px", -1))
-    ends, starts = edges(block, above, below)
+    ends, starts = edges(first, last, above, below)
     left = lax.ppermute(ends, "py", ring("py", 1))
     right = lax.ppermute(starts, "py", ring("py", -1))
-    return block, above, below, left, right
-
-
-def variation(pieces):
-    volume, above, below, left, right = pieces
+    return first, last, above, below, left, right
+
+
+def variation(volume, pieces):
+    _, _, above, below, left, right = pieces
     row_count, col_count, _ = volume.shape
     row_whole = row_count * lax.axis_size("px")
     col_whole = col_count * lax.axis_size("py")
@@ -553,10 +556,10 @@
 
 def shards(estimate, observed, psf):
     transfer = transfer_function(psf, estimate.shape[2])
-    pieces = halos(estimate)
+    pieces = halos(*split(estimate))
     quotient = convolve(pieces, transfer, observed, False)
-    scaled = pieces[0] / (1.0 - penalty_weight * variation(pieces))
-    return convolve(halos(quotient), transfer, scaled, True)
+    scaled = estimate / (1.0 - penalty_weight * variation(estimate, pieces))
+    return convolve(halos(*quotient), transfer, scaled, True)
 
 
 def solution(mesh):

time: 72.5 us -> 72.2 us (level)
    ppermute x2, waiting for transfers between devices: 4.37 us -> 3.51 us  [halos(): right = lax.ppermute(starts, 'py', ring('py', -1))]
    pallas_call x8 -> x9, Pallas kernels: 10.6 us -> 10.7 us  [the longest x2 6.94 us: convolve(): pl.pallas_call(functools.partial(convolve_kernel, adjoint), out_shape=who...]
  transfers between devices with their start and end apart: 8 -> 8, of which waited for: 8 -> 8; matrix products, arithmetic and copies ran while one was open for 2% -> 2% of each run, Pallas kernels for 5% -> 6%
where the time goes in v5:
time: 72.2 us; the launch traced here: 72 us
  waiting for transfers between devices  38.8 us (54%)
  starting transfers between devices  18 us (25%)
  Pallas kernels  12.5 us (17%)
  other arithmetic  1.36 us (2%)
  local copies, waits for them, and re-layouts  1.18 us (2%)
    ppermute x2, waiting for transfers between devices, halos(): left = lax.ppermute(ends, 'py', ring('py', 1))  18.9 us
    ppermute x2, starting transfers between devices, halos(): below = lax.ppermute(first, 'px', ring('px', -1))  10.8 us
    ppermute x2, waiting for transfers between devices, halos(): above = lax.ppermute(last, 'px', ring('px', 1))  10 us
    pallas_call x2, Pallas kernels, convolve(): pl.pallas_call(functools.partial(convolve_kernel, adjoint), out_shape=who...  6.94 us
    ppermute x2, waiting for transfers between devices, halos(): below = lax.ppermute(first, 'px', ring('px', -1))  6.3 us
    ppermute x2, starting transfers between devices, halos(): above = lax.ppermute(last, 'px', ring('px', 1))  4.51 us
    ppermute x2, waiting for transfers between devices, halos(): right = lax.ppermute(starts, 'py', ring('py', -1))  3.51 us
    pallas_call x4, Pallas kernels, columns(): pl.pallas_call(functools.partial(columns_kernel, len(pieces)), out_shape=...  2.74 us
  transfers between devices with their start and end apart: 8, of which 8 were waited for; matrix products, arithmetic and copies ran while one was open for 2% of the time, Pallas kernels for 6%

profile of v5, /device:TPU:1, one launch (start us, length us, event | category | flops | bytes accessed | tf_op | source)
XLA Modules:
  0.0 72.0 jit_solution(1226105506572175768)
XLA Ops:
  0.0 1.0 %copy-done = f32[32,32,128]{2,1,0:T(8,128)S(1)} copy-done((f32[32,32,128]{2,1,0:T(8,128)S(1)}, f32[32,32,128]{2,1,0:T(8,128)}, u32[]{:S(2)}) %copy-start) | copy-done | bytes 524312
  1.1 3.8 %collective-permute-start = (f32[16,32,128]{2,1,0:T(8,128)S(1)}, f32[16,32,128]{2,1,0:T(8,128)S(1)}, u32[]{:S(2)}, u32[]{:S(2)}) collective-permute-start(f32[16,32,128]{2,1,0:T(8,128)S(1)} %get-tuple-element.13.refs_2_.last_ref), channel_id=1, source_target_pairs={{0,16},{16,32},{32,48},{48,64},{64,80},{80,96},{96,112},{112,128},... | collective-permute-start | bytes 786440 | tf_op jit(solution)/shard_map/ppermute | solution.py:505
  4.9 5.4 %collective-permute-start.1 = (f32[16,32,128]{2,1,0:T(8,128)S(1)}, f32[16,32,128]{2,1,0:T(8,128)S(1)}, u32[]{:S(2)}, u32[]{:S(2)}) collective-permute-start(f32[16,32,128]{2,1,0:T(8,128)S(1)} %get-tuple-element.14.refs_1_.first_ref), channel_id=1, source_target_pairs={{0,240},{16,0},{32,16},{48,32},{64,48},{80,64},{96,80},{112,96},{1... | collective-permute-start | bytes 786440 | tf_op jit(solution)/shard_map/ppermute | solution.py:506
  10.3 6.0 %collective-permute-done.refs_0_.above_ref = f32[16,32,128]{2,1,0:T(8,128)S(1)} collective-permute-done((f32[16,32,128]{2,1,0:T(8,128)S(1)}, f32[16,32,128]{2,1,0:T(8,128)S(1)}, u32[]{:S(2)}, u32[]{:S(2)}) %collective-permute-start) | collective-permute-done | bytes 262176 | tf_op jit(solution)/shard_map/ppermute | solution.py:505
  16.3 2.6 %collective-permute-done.1.refs_3_.below_ref = f32[16,32,128]{2,1,0:T(8,128)S(1)} collective-permute-done((f32[16,32,128]{2,1,0:T(8,128)S(1)}, f32[16,32,128]{2,1,0:T(8,128)S(1)}, u32[]{:S(2)}, u32[]{:S(2)}) %collective-permute-start.1) | collective-permute-done | bytes 262176 | tf_op jit(solution)/shard_map/ppermute | solution.py:506
  18.9 0.9 %edges.2 = (f32[64,16,128]{2,1,0:T(8,128)}, f32[64,16,128]{2,1,0:T(8,128)S(1)}) custom-call(f32[16,32,128]{2,1,0:T(8,128)S(1)} %get-tuple-element.14.refs_1_.first_ref, f32[16,32,128]{2,1,0:T(8,128)S(1)} %get-tuple-element.13.refs_2_.last_ref, f32[16,32,128]{2,1,0:T(8,128)S(1)} %collective-permute-done.refs_0_.above_ref, ...), custom_call_target="tpu_custom_call" | custom-call | tf_op jit(solution)/shard_map/edges/pallas_call | solution.py:419
  19.8 2.1 %collective-permute-start.2 = (f32[64,16,128]{2,1,0:T(8,128)}, f32[64,16,128]{2,1,0:T(8,128)S(1)}, u32[]{:S(2)}, u32[]{:S(2)}) collective-permute-start(f32[64,16,128]{2,1,0:T(8,128)} %get-tuple-element.15), channel_id=1, source_target_pairs={{0,1},{1,2},{2,3},{3,4},{4,5},{5,6},{6,7},{7,8},{8,9},{9,10},{10,1... | collective-permute-start | bytes 1572872 | tf_op jit(solution)/shard_map/ppermute | solution.py:508
  22.0 1.8 %transfer.1.transfer_ref = f32[34,256,128]{2,1,0:T(8,128)S(1)} custom-call(f32[32,32,32]{2,1,0:T(8,128)S(1)} %copy-done.3, f32[32,128]{1,0:T(8,128)S(1)} %copy-done.9, bf16[256,128]{1,0:T(8,128)(2,1)S(1)} %copy-done.8), custom_call_target="tpu_custom_call" | custom-call | tf_op jit(solution)/shard_map/transfer/pallas_call | solution.py:400
  23.8 0.9 %inner.2.inner_ref = f32[34,64,128]{2,1,0:T(8,128)S(1)} custom-call(f32[16,32,128]{2,1,0:T(8,128)S(1)} %collective-permute-done.refs_0_.above_ref, f32[16,32,128]{2,1,0:T(8,128)S(1)} %get-tuple-element.14.refs_1_.first_ref, f32[16,32,128]{2,1,0:T(8,128)S(1)} %get-tuple-element.13.refs_2_.last_ref, ...), custom_call_target="tpu_custom_call" | custom-call | tf_op jit(solution)/shard_map/inner/pallas_call | solution.py:444
  24.7 9.3 %collective-permute-done.2.refs_0_ = f32[64,16,128]{2,1,0:T(8,128)S(1)} collective-permute-done((f32[64,16,128]{2,1,0:T(8,128)}, f32[64,16,128]{2,1,0:T(8,128)S(1)}, u32[]{:S(2)}, u32[]{:S(2)}) %collective-permute-start.2) | collective-permute-done | bytes 524320 | tf_op jit(solution)/shard_map/ppermute | solution.py:508
  34.0 0.5 left.2.left_ref
  34.9 1.3 %collective-permute-done.3.right_ref = f32[64,16,128]{2,1,0:T(8,128)S(1)} collective-permute-done((f32[64,16,128]{2,1,0:T(8,128)S(1)}, f32[64,16,128]{2,1,0:T(8,128)S(1)}, u32[]{:S(2)}, u32[]{:S(2)}) %collective-permute-start.3) | collective-permute-done | bytes 524320 | tf_op jit(solution)/shard_map/ppermute | solution.py:509
  36.2 3.1 %convolve.1 = (f32[16,32,128]{2,1,0:T(8,128)S(1)}, f32[16,32,128]{2,1,0:T(8,128)S(1)}) custom-call(f32[34,64,128]{2,1,0:T(8,128)S(1)} %inner.2.inner_ref, f32[34,32,128]{2,1,0:T(8,128)S(1)} %left.2.left_ref, f32[64,16,128]{2,1,0:T(8,128)S(1)} %collective-permute-done.3.right_ref, f32[34,256,128]{2,1,0:T(8,128)S(1)} %transfer.1.transfer_ref, ...), custom_call_target="tpu_custom_call" | custom-call | tf_op jit(solution)/shard_map/convolve/pallas_call | solution.py:473
  39.2 0.7 collective-permute-start.4
  39.9 5.4 %collective-permute-start.5 = (f32[16,32,128]{2,1,0:T(8,128)S(1)}, f32[16,32,128]{2,1,0:T(8,128)S(1)}, u32[]{:S(2)}, u32[]{:S(2)}) collective-permute-start(f32[16,32,128]{2,1,0:T(8,128)S(1)} %get-tuple-element.18.refs_1_.first_ref), channel_id=1, source_target_pairs={{0,240},{16,0},{32,16},{48,32},{64,48},{80,64},{96,80},{112,96},{1... | collective-permute-start | bytes 786440 | tf_op jit(solution)/shard_map/ppermute | solution.py:506
  45.3 0.4 fusion.8
  45.8 4.1 %collective-permute-done.4.refs_0_.above_ref = f32[16,32,128]{2,1,0:T(8,128)S(1)} collective-permute-done((f32[16,32,128]{2,1,0:T(8,128)S(1)}, f32[16,32,128]{2,1,0:T(8,128)S(1)}, u32[]{:S(2)}, u32[]{:S(2)}) %collective-permute-start.4) | collective-permute-done | bytes 262176 | tf_op jit(solution)/shard_map/ppermute | solution.py:505
  49.8 3.7 %collective-permute-done.5.refs_3_.below_ref = f32[16,32,128]{2,1,0:T(8,128)S(1)} collective-permute-done((f32[16,32,128]{2,1,0:T(8,128)S(1)}, f32[16,32,128]{2,1,0:T(8,128)S(1)}, u32[]{:S(2)}, u32[]{:S(2)}) %collective-permute-start.5) | collective-permute-done | bytes 262176 | tf_op jit(solution)/shard_map/ppermute | solution.py:506
  53.7 0.5 collective-permute-start.7
  54.9 0.9 %inner.3.inner_ref = f32[34,64,128]{2,1,0:T(8,128)S(1)} custom-call(f32[16,32,128]{2,1,0:T(8,128)S(1)} %collective-permute-done.4.refs_0_.above_ref, f32[16,32,128]{2,1,0:T(8,128)S(1)} %get-tuple-element.18.refs_1_.first_ref, f32[16,32,128]{2,1,0:T(8,128)S(1)} %get-tuple-element.17.refs_2_.last_ref, ...), custom_call_target="tpu_custom_call" | custom-call | tf_op jit(solution)/shard_map/inner/pallas_call | solution.py:444
  55.8 9.7 %collective-permute-done.6.refs_0_ = f32[64,16,128]{2,1,0:T(8,128)S(1)} collective-permute-done((f32[64,16,128]{2,1,0:T(8,128)S(1)}, f32[64,16,128]{2,1,0:T(8,128)S(1)}, u32[]{:S(2)}, u32[]{:S(2)}) %collective-permute-start.6) | collective-permute-done | bytes 524320 | tf_op jit(solution)/shard_map/ppermute | solution.py:508
  65.4 0.5 left.3.left_ref
  65.9 2.3 %collective-permute-done.7.right_ref = f32[64,16,128]{2,1,0:T(8,128)S(1)} collective-permute-done((f32[64,16,128]{2,1,0:T(8,128)S(1)}, f32[64,16,128]{2,1,0:T(8,128)S(1)}, u32[]{:S(2)}, u32[]{:S(2)}) %collective-permute-start.7) | collective-permute-done | bytes 524320 | tf_op jit(solution)/shard_map/ppermute | solution.py:509
  68.2 3.9 %correlate.1 = f32[32,32,128]{2,1,0:T(8,128)} custom-call(f32[34,64,128]{2,1,0:T(8,128)S(1)} %inner.3.inner_ref, f32[34,32,128]{2,1,0:T(8,128)S(1)} %left.3.left_ref, f32[64,16,128]{2,1,0:T(8,128)S(1)} %collective-permute-done.7.right_ref, f32[34,256,128]{2,1,0:T(8,128)S(1)} %transfer.1.transfer_ref, f32[32,32,128]{2,1,0:T(8,128)S(1)} %fusion.6.other_ref, ...), custom_call_target="tpu_custom_call" | custom-call | tf_op jit(solution)/shard_map/correlate/pallas_call | solution.py:473
  (33 shorter events, 1.3 us)
Async XLA Ops:
  0.0 1.0 %copy-start = (f32[32,32,128]{2,1,0:T(8,128)S(1)}, f32[32,32,128]{2,1,0:T(8,128)}, u32[]{:S(2)}) copy-start(f32[32,32,128]{2,1,0:T(8,128)} %block_ref.1) | copy-start | bytes 1572868
  1.0 20.9 %copy-start.3 = (f32[32,32,32]{2,1,0:T(8,128)S(1)}, f32[32,32,32]{2,1,0:T(8,128)}, u32[]{:S(2)}) copy-start(f32[32,32,32]{2,1,0:T(8,128)} %psf_ref.1) | copy-start | bytes 393220
  1.0 20.9 %copy-start.8 = (bf16[256,128]{1,0:T(8,128)(2,1)S(1)}, bf16[256,128]{1,0:T(8,128)(2,1)}, u32[]{:S(2)}) copy-start(bf16[256,128]{1,0:T(8,128)(2,1)} %constant.40.clone.column_ref) | copy-start | bytes 196612
  1.0 20.9 %copy-start.9 = (f32[32,128]{1,0:T(8,128)S(1)}, f32[32,128]{1,0:T(8,128)}, u32[]{:S(2)}) copy-start(f32[32,128]{1,0:T(8,128)} %constant.39.clone.depth_ref) | copy-start | bytes 49156
  1.1 15.2 %collective-permute-start = (f32[16,32,128]{2,1,0:T(8,128)S(1)}, f32[16,32,128]{2,1,0:T(8,128)S(1)}, u32[]{:S(2)}, u32[]{:S(2)}) collective-permute-start(f32[16,32,128]{2,1,0:T(8,128)S(1)} %get-tuple-element.13.refs_2_.last_ref), channel_id=1, source_target_pairs={{0,16},{16,32},{32,48},{48,64},{64,80},{80,96},{96,112},{112,128},... | collective-permute-start | bytes 786440 | tf_op jit(solution)/shard_map/ppermute | solution.py:505
  4.9 14.0 %collective-permute-start.1 = (f32[16,32,128]{2,1,0:T(8,128)S(1)}, f32[16,32,128]{2,1,0:T(8,128)S(1)}, u32[]{:S(2)}, u32[]{:S(2)}) collective-permute-start(f32[16,32,128]{2,1,0:T(8,128)S(1)} %get-tuple-element.14.refs_1_.first_ref), channel_id=1, source_target_pairs={{0,240},{16,0},{32,16},{48,32},{64,48},{80,64},{96,80},{112,96},{1... | collective-permute-start | bytes 786440 | tf_op jit(solution)/shard_map/ppermute | solution.py:506
  19.8 14.2 %collective-permute-start.2 = (f32[64,16,128]{2,1,0:T(8,128)}, f32[64,16,128]{2,1,0:T(8,128)S(1)}, u32[]{:S(2)}, u32[]{:S(2)}) collective-permute-start(f32[64,16,128]{2,1,0:T(8,128)} %get-tuple-element.15), channel_id=1, source_target_pairs={{0,1},{1,2},{2,3},{3,4},{4,5},{5,6},{6,7},{7,8},{8,9},{9,10},{10,1... | collective-permute-start | bytes 1572872 | tf_op jit(solution)/shard_map/ppermute | solution.py:508
  21.9 14.2 %collective-permute-start.3 = (f32[64,16,128]{2,1,0:T(8,128)S(1)}, f32[64,16,128]{2,1,0:T(8,128)S(1)}, u32[]{:S(2)}, u32[]{:S(2)}) collective-permute-start(f32[64,16,128]{2,1,0:T(8,128)S(1)} %get-tuple-element.16), channel_id=1, source_target_pairs={{0,15},{1,0},{2,1},{3,2},{4,3},{5,4},{6,5},{7,6},{8,7},{9,8},{10,9... | collective-permute-start | bytes 1572872 | tf_op jit(solution)/shard_map/ppermute | solution.py:509
  21.9 1.9 %copy-start.2 = (bf16[256,256]{1,0:T(8,128)(2,1)S(1)}, bf16[256,256]{1,0:T(8,128)(2,1)}, u32[]{:S(2)}) copy-start(bf16[256,256]{1,0:T(8,128)(2,1)} %constant.41.clone.refs_4_.refs_1_.depth_ref) | copy-start | bytes 393220
  24.7 9.8 %copy-start.1 = (f32[32,32,128]{2,1,0:T(8,128)S(1)}, f32[32,32,128]{2,1,0:T(8,128)}, u32[]{:S(2)}) copy-start(f32[32,32,128]{2,1,0:T(8,128)} %block_ref.1) | copy-start | bytes 1572868
  34.6 1.6 %copy-start.4 = (bf16[256,256]{1,0:T(8,128)(2,1)S(1)}, bf16[256,256]{1,0:T(8,128)(2,1)}, u32[]{:S(2)}) copy-start(bf16[256,256]{1,0:T(8,128)(2,1)} %constant.44.clone.depth_back_ref) | copy-start | bytes 393220
  34.6 1.6 %copy-start.5 = (bf16[256,256]{1,0:T(8,128)(2,1)S(1)}, bf16[256,256]{1,0:T(8,128)(2,1)}, u32[]{:S(2)}) copy-start(bf16[256,256]{1,0:T(8,128)(2,1)} %constant.42.clone.column_ref) | copy-start | bytes 393220
  34.6 1.5 %copy-start.6 = (f32[32,32,128]{2,1,0:T(8,128)S(1)}, f32[32,32,128]{2,1,0:T(8,128)}, u32[]{:S(2)}) copy-start(f32[32,32,128]{2,1,0:T(8,128)} %other_ref.1) | copy-start | bytes 1572868
  34.6 1.5 %copy-start.7 = (bf16[128,256]{1,0:T(8,128)(2,1)S(1)}, bf16[128,256]{1,0:T(8,128)(2,1)}, u32[]{:S(2)}) copy-start(bf16[128,256]{1,0:T(8,128)(2,1)} %constant.43.clone.column_back_ref) | copy-start | bytes 196612
  39.2 10.6 %collective-permute-start.4 = (f32[16,32,128]{2,1,0:T(8,128)S(1)}, f32[16,32,128]{2,1,0:T(8,128)S(1)}, u32[]{:S(2)}, u32[]{:S(2)}) collective-permute-start(f32[16,32,128]{2,1,0:T(8,128)S(1)} %get-tuple-element.17.refs_2_.last_ref), channel_id=1, source_target_pairs={{0,16},{16,32},{32,48},{48,64},{64,80},{80,96},{96,112},{112,128},... | collective-permute-start | bytes 786440 | tf_op jit(solution)/shard_map/ppermute | solution.py:505
  39.9 13.6 %collective-permute-start.5 = (f32[16,32,128]{2,1,0:T(8,128)S(1)}, f32[16,32,128]{2,1,0:T(8,128)S(1)}, u32[]{:S(2)}, u32[]{:S(2)}) collective-permute-start(f32[16,32,128]{2,1,0:T(8,128)S(1)} %get-tuple-element.18.refs_1_.first_ref), channel_id=1, source_target_pairs={{0,240},{16,0},{32,16},{48,32},{64,48},{80,64},{96,80},{112,96},{1... | collective-permute-start | bytes 786440 | tf_op jit(solution)/shard_map/ppermute | solution.py:506
  53.6 11.8 %collective-permute-start.6 = (f32[64,16,128]{2,1,0:T(8,128)S(1)}, f32[64,16,128]{2,1,0:T(8,128)S(1)}, u32[]{:S(2)}, u32[]{:S(2)}) collective-permute-start(f32[64,16,128]{2,1,0:T(8,128)S(1)} %get-tuple-element.19), channel_id=1, source_target_pairs={{0,1},{1,2},{2,3},{3,4},{4,5},{5,6},{6,7},{7,8},{8,9},{9,10},{10,1... | collective-permute-start | bytes 1572872 | tf_op jit(solution)/shard_map/ppermute | solution.py:508
  53.7 14.5 %collective-permute-start.7 = (f32[64,16,128]{2,1,0:T(8,128)S(1)}, f32[64,16,128]{2,1,0:T(8,128)S(1)}, u32[]{:S(2)}, u32[]{:S(2)}) collective-permute-start(f32[64,16,128]{2,1,0:T(8,128)S(1)} %get-tuple-element.20), channel_id=1, source_target_pairs={{0,15},{1,0},{2,1},{3,2},{4,3},{5,4},{6,5},{7,6},{8,7},{9,8},{10,9... | collective-permute-start | bytes 1572872 | tf_op jit(solution)/shard_map/ppermute | solution.py:509

commit v6 on v5

--- a/solution.py
+++ b/solution.py
@@ -558,7 +558,8 @@
     transfer = transfer_function(psf, estimate.shape[2])
     pieces = halos(*split(estimate))
     quotient = convolve(pieces, transfer, observed, False)
-    scaled = estimate / (1.0 - penalty_weight * variation(estimate, pieces))
+    around, quotient = lax.optimization_barrier((pieces[2:], quotient))
+    scaled = estimate / (1.0 - penalty_weight * variation(estimate, pieces[:2] + around))
     return convolve(halos(*quotient), transfer, scaled, True)
 
 

time: 72.2 us -> 71.5 us (level)
  waiting for transfers between devices: 38.8 us -> 37.8 us
    ppermute x2, waiting for transfers between devices: 10 us -> 9.23 us  [halos(): above = lax.ppermute(last, 'px', ring('px', 1))]
where the time goes in v6:
time: 71.5 us; the launch traced here: 71.1 us
  waiting for transfers between devices  37.8 us (53%)
  starting transfers between devices  18 us (25%)
  Pallas kernels  12.5 us (17%)
  other arithmetic  1.36 us (2%)
  local copies, waits for them, and re-layouts  1.18 us (2%)
    ppermute x2, waiting for transfers between devices, halos(): left = lax.ppermute(ends, 'py', ring('py', 1))  19.2 us
    ppermute x2, starting transfers between devices, halos(): below = lax.ppermute(first, 'px', ring('px', -1))  10.8 us
    ppermute x2, waiting for transfers between devices, halos(): above = lax.ppermute(last, 'px', ring('px', 1))  9.23 us
    pallas_call x2, Pallas kernels, convolve(): pl.pallas_call(functools.partial(convolve_kernel, adjoint), out_shape=who...  6.95 us
    ppermute x2, waiting for transfers between devices, halos(): below = lax.ppermute(first, 'px', ring('px', -1))  5.9 us
    ppermute x2, starting transfers between devices, halos(): above = lax.ppermute(last, 'px', ring('px', 1))  4.51 us
    ppermute x2, waiting for transfers between devices, halos(): right = lax.ppermute(starts, 'py', ring('py', -1))  3.51 us
    pallas_call x4, Pallas kernels, columns(): pl.pallas_call(functools.partial(columns_kernel, len(pieces)), out_shape=...  2.75 us
  transfers between devices with their start and end apart: 8, of which 8 were waited for; matrix products, arithmetic and copies ran while one was open for 2% of the time, Pallas kernels for 6%

profile of v6, /device:TPU:1, one launch (start us, length us, event | category | flops | bytes accessed | tf_op | source)
XLA Modules:
  0.0 71.1 jit_solution(1757127679079277850)
XLA Ops:
  0.0 1.0 %copy-done = f32[32,32,128]{2,1,0:T(8,128)S(1)} copy-done((f32[32,32,128]{2,1,0:T(8,128)S(1)}, f32[32,32,128]{2,1,0:T(8,128)}, u32[]{:S(2)}) %copy-start) | copy-done | bytes 524312
  1.1 3.8 %collective-permute-start = (f32[16,32,128]{2,1,0:T(8,128)S(1)}, f32[16,32,128]{2,1,0:T(8,128)S(1)}, u32[]{:S(2)}, u32[]{:S(2)}) collective-permute-start(f32[16,32,128]{2,1,0:T(8,128)S(1)} %get-tuple-element.19.last_ref.refs_2_), channel_id=1, source_target_pairs={{0,16},{16,32},{32,48},{48,64},{64,80},{80,96},{96,112},{112,128},... | collective-permute-start | bytes 786440 | tf_op jit(solution)/shard_map/ppermute | solution.py:505
  4.9 5.4 %collective-permute-start.1 = (f32[16,32,128]{2,1,0:T(8,128)S(1)}, f32[16,32,128]{2,1,0:T(8,128)S(1)}, u32[]{:S(2)}, u32[]{:S(2)}) collective-permute-start(f32[16,32,128]{2,1,0:T(8,128)S(1)} %get-tuple-element.20.first_ref.refs_1_), channel_id=1, source_target_pairs={{0,240},{16,0},{32,16},{48,32},{64,48},{80,64},{96,80},{112,96},{1... | collective-permute-start | bytes 786440 | tf_op jit(solution)/shard_map/ppermute | solution.py:506
  10.3 6.0 %collective-permute-done.above_ref.refs_0_ = f32[16,32,128]{2,1,0:T(8,128)S(1)} collective-permute-done((f32[16,32,128]{2,1,0:T(8,128)S(1)}, f32[16,32,128]{2,1,0:T(8,128)S(1)}, u32[]{:S(2)}, u32[]{:S(2)}) %collective-permute-start) | collective-permute-done | bytes 262176 | tf_op jit(solution)/shard_map/ppermute | solution.py:505
  16.3 2.6 %collective-permute-done.1.below_ref.refs_3_ = f32[16,32,128]{2,1,0:T(8,128)S(1)} collective-permute-done((f32[16,32,128]{2,1,0:T(8,128)S(1)}, f32[16,32,128]{2,1,0:T(8,128)S(1)}, u32[]{:S(2)}, u32[]{:S(2)}) %collective-permute-start.1) | collective-permute-done | bytes 262176 | tf_op jit(solution)/shard_map/ppermute | solution.py:506
  18.9 0.9 %edges.2 = (f32[64,16,128]{2,1,0:T(8,128)}, f32[64,16,128]{2,1,0:T(8,128)S(1)}) custom-call(f32[16,32,128]{2,1,0:T(8,128)S(1)} %get-tuple-element.20.first_ref.refs_1_, f32[16,32,128]{2,1,0:T(8,128)S(1)} %get-tuple-element.19.last_ref.refs_2_, f32[16,32,128]{2,1,0:T(8,128)S(1)} %collective-permute-done.above_ref.refs_0_, ...), custom_call_target="tpu_custom_call" | custom-call | tf_op jit(solution)/shard_map/edges/pallas_call | solution.py:419
  19.8 2.1 %collective-permute-start.2 = (f32[64,16,128]{2,1,0:T(8,128)}, f32[64,16,128]{2,1,0:T(8,128)S(1)}, u32[]{:S(2)}, u32[]{:S(2)}) collective-permute-start(f32[64,16,128]{2,1,0:T(8,128)} %get-tuple-element.21), channel_id=1, source_target_pairs={{0,1},{1,2},{2,3},{3,4},{4,5},{5,6},{6,7},{7,8},{8,9},{9,10},{10,1... | collective-permute-start | bytes 1572872 | tf_op jit(solution)/shard_map/ppermute | solution.py:508
  22.0 1.8 %transfer.1.transfer_ref = f32[34,256,128]{2,1,0:T(8,128)S(1)} custom-call(f32[32,32,32]{2,1,0:T(8,128)S(1)} %copy-done.3, f32[32,128]{1,0:T(8,128)S(1)} %copy-done.9, bf16[256,128]{1,0:T(8,128)(2,1)S(1)} %copy-done.8), custom_call_target="tpu_custom_call" | custom-call | tf_op jit(solution)/shard_map/transfer/pallas_call | solution.py:400
  23.8 0.9 %inner.2.inner_ref = f32[34,64,128]{2,1,0:T(8,128)S(1)} custom-call(f32[16,32,128]{2,1,0:T(8,128)S(1)} %collective-permute-done.above_ref.refs_0_, f32[16,32,128]{2,1,0:T(8,128)S(1)} %get-tuple-element.20.first_ref.refs_1_, f32[16,32,128]{2,1,0:T(8,128)S(1)} %get-tuple-element.19.last_ref.refs_2_, ...), custom_call_target="tpu_custom_call" | custom-call | tf_op jit(solution)/shard_map/inner/pallas_call | solution.py:444
  24.7 9.3 %collective-permute-done.2.refs_0_ = f32[64,16,128]{2,1,0:T(8,128)S(1)} collective-permute-done((f32[64,16,128]{2,1,0:T(8,128)}, f32[64,16,128]{2,1,0:T(8,128)S(1)}, u32[]{:S(2)}, u32[]{:S(2)}) %collective-permute-start.2) | collective-permute-done | bytes 524320 | tf_op jit(solution)/shard_map/ppermute | solution.py:508
  34.0 0.5 left.2.left_ref
  34.5 1.7 %collective-permute-done.3.right_ref = f32[64,16,128]{2,1,0:T(8,128)S(1)} collective-permute-done((f32[64,16,128]{2,1,0:T(8,128)S(1)}, f32[64,16,128]{2,1,0:T(8,128)S(1)}, u32[]{:S(2)}, u32[]{:S(2)}) %collective-permute-start.3) | collective-permute-done | bytes 524320 | tf_op jit(solution)/shard_map/ppermute | solution.py:509
  36.2 3.1 %convolve.1 = (f32[16,32,128]{2,1,0:T(8,128)S(1)}, f32[16,32,128]{2,1,0:T(8,128)S(1)}) custom-call(f32[34,64,128]{2,1,0:T(8,128)S(1)} %inner.2.inner_ref, f32[34,32,128]{2,1,0:T(8,128)S(1)} %left.2.left_ref, f32[64,16,128]{2,1,0:T(8,128)S(1)} %collective-permute-done.3.right_ref, f32[34,256,128]{2,1,0:T(8,128)S(1)} %transfer.1.transfer_ref, ...), custom_call_target="tpu_custom_call" | custom-call | tf_op jit(solution)/shard_map/convolve/pallas_call | solution.py:473
  39.6 0.7 collective-permute-start.4
  40.3 5.4 %collective-permute-start.5 = (f32[16,32,128]{2,1,0:T(8,128)S(1)}, f32[16,32,128]{2,1,0:T(8,128)S(1)}, u32[]{:S(2)}, u32[]{:S(2)}) collective-permute-start(f32[16,32,128]{2,1,0:T(8,128)S(1)} %get-tuple-element.26.refs_1_.first_ref), channel_id=1, source_target_pairs={{0,240},{16,0},{32,16},{48,32},{64,48},{80,64},{96,80},{112,96},{1... | collective-permute-start | bytes 786440 | tf_op jit(solution)/shard_map/ppermute | solution.py:506
  45.7 0.4 fusion.8
  46.1 3.2 %collective-permute-done.4.refs_0_.above_ref = f32[16,32,128]{2,1,0:T(8,128)S(1)} collective-permute-done((f32[16,32,128]{2,1,0:T(8,128)S(1)}, f32[16,32,128]{2,1,0:T(8,128)S(1)}, u32[]{:S(2)}, u32[]{:S(2)}) %collective-permute-start.4) | collective-permute-done | bytes 262176 | tf_op jit(solution)/shard_map/ppermute | solution.py:505
  49.4 3.3 %collective-permute-done.5.refs_3_.below_ref = f32[16,32,128]{2,1,0:T(8,128)S(1)} collective-permute-done((f32[16,32,128]{2,1,0:T(8,128)S(1)}, f32[16,32,128]{2,1,0:T(8,128)S(1)}, u32[]{:S(2)}, u32[]{:S(2)}) %collective-permute-start.5) | collective-permute-done | bytes 262176 | tf_op jit(solution)/shard_map/ppermute | solution.py:506
  53.7 0.3 fusion.6.other_ref
  54.0 0.9 %inner.3.inner_ref = f32[34,64,128]{2,1,0:T(8,128)S(1)} custom-call(f32[16,32,128]{2,1,0:T(8,128)S(1)} %collective-permute-done.4.refs_0_.above_ref, f32[16,32,128]{2,1,0:T(8,128)S(1)} %get-tuple-element.26.refs_1_.first_ref, f32[16,32,128]{2,1,0:T(8,128)S(1)} %get-tuple-element.25.refs_2_.last_ref, ...), custom_call_target="tpu_custom_call" | custom-call | tf_op jit(solution)/shard_map/inner/pallas_call | solution.py:444
  54.9 9.9 %collective-permute-done.6.refs_0_ = f32[64,16,128]{2,1,0:T(8,128)S(1)} collective-permute-done((f32[64,16,128]{2,1,0:T(8,128)S(1)}, f32[64,16,128]{2,1,0:T(8,128)S(1)}, u32[]{:S(2)}, u32[]{:S(2)}) %collective-permute-start.6) | collective-permute-done | bytes 524320 | tf_op jit(solution)/shard_map/ppermute | solution.py:508
  64.8 0.5 left.3.left_ref
  65.3 1.9 %collective-permute-done.7.right_ref = f32[64,16,128]{2,1,0:T(8,128)S(1)} collective-permute-done((f32[64,16,128]{2,1,0:T(8,128)S(1)}, f32[64,16,128]{2,1,0:T(8,128)S(1)}, u32[]{:S(2)}, u32[]{:S(2)}) %collective-permute-start.7) | collective-permute-done | bytes 524320 | tf_op jit(solution)/shard_map/ppermute | solution.py:509
  67.2 3.9 %correlate.1 = f32[32,32,128]{2,1,0:T(8,128)} custom-call(f32[34,64,128]{2,1,0:T(8,128)S(1)} %inner.3.inner_ref, f32[34,32,128]{2,1,0:T(8,128)S(1)} %left.3.left_ref, f32[64,16,128]{2,1,0:T(8,128)S(1)} %collective-permute-done.7.right_ref, f32[34,256,128]{2,1,0:T(8,128)S(1)} %transfer.1.transfer_ref, f32[32,32,128]{2,1,0:T(8,128)S(1)} %fusion.6.other_ref, ...), custom_call_target="tpu_custom_call" | custom-call | tf_op jit(solution)/shard_map/correlate/pallas_call | solution.py:473
  (33 shorter events, 1.4 us)
Async XLA Ops:
  0.0 1.0 %copy-start = (f32[32,32,128]{2,1,0:T(8,128)S(1)}, f32[32,32,128]{2,1,0:T(8,128)}, u32[]{:S(2)}) copy-start(f32[32,32,128]{2,1,0:T(8,128)} %block_ref.1) | copy-start | bytes 1572868
  1.0 20.9 %copy-start.3 = (f32[32,32,32]{2,1,0:T(8,128)S(1)}, f32[32,32,32]{2,1,0:T(8,128)}, u32[]{:S(2)}) copy-start(f32[32,32,32]{2,1,0:T(8,128)} %psf_ref.1) | copy-start | bytes 393220
  1.0 20.9 %copy-start.8 = (bf16[256,128]{1,0:T(8,128)(2,1)S(1)}, bf16[256,128]{1,0:T(8,128)(2,1)}, u32[]{:S(2)}) copy-start(bf16[256,128]{1,0:T(8,128)(2,1)} %constant.40.clone.column_ref) | copy-start | bytes 196612
  1.0 20.9 %copy-start.9 = (f32[32,128]{1,0:T(8,128)S(1)}, f32[32,128]{1,0:T(8,128)}, u32[]{:S(2)}) copy-start(f32[32,128]{1,0:T(8,128)} %constant.39.clone.depth_ref) | copy-start | bytes 49156
  1.1 15.2 %collective-permute-start = (f32[16,32,128]{2,1,0:T(8,128)S(1)}, f32[16,32,128]{2,1,0:T(8,128)S(1)}, u32[]{:S(2)}, u32[]{:S(2)}) collective-permute-start(f32[16,32,128]{2,1,0:T(8,128)S(1)} %get-tuple-element.19.last_ref.refs_2_), channel_id=1, source_target_pairs={{0,16},{16,32},{32,48},{48,64},{64,80},{80,96},{96,112},{112,128},... | collective-permute-start | bytes 786440 | tf_op jit(solution)/shard_map/ppermute | solution.py:505
  4.9 14.0 %collective-permute-start.1 = (f32[16,32,128]{2,1,0:T(8,128)S(1)}, f32[16,32,128]{2,1,0:T(8,128)S(1)}, u32[]{:S(2)}, u32[]{:S(2)}) collective-permute-start(f32[16,32,128]{2,1,0:T(8,128)S(1)} %get-tuple-element.20.first_ref.refs_1_), channel_id=1, source_target_pairs={{0,240},{16,0},{32,16},{48,32},{64,48},{80,64},{96,80},{112,96},{1... | collective-permute-start | bytes 786440 | tf_op jit(solution)/shard_map/ppermute | solution.py:506
  19.8 14.2 %collective-permute-start.2 = (f32[64,16,128]{2,1,0:T(8,128)}, f32[64,16,128]{2,1,0:T(8,128)S(1)}, u32[]{:S(2)}, u32[]{:S(2)}) collective-permute-start(f32[64,16,128]{2,1,0:T(8,128)} %get-tuple-element.21), channel_id=1, source_target_pairs={{0,1},{1,2},{2,3},{3,4},{4,5},{5,6},{6,7},{7,8},{8,9},{9,10},{10,1... | collective-permute-start | bytes 1572872 | tf_op jit(solution)/shard_map/ppermute | solution.py:508
  21.9 14.2 %collective-permute-start.3 = (f32[64,16,128]{2,1,0:T(8,128)S(1)}, f32[64,16,128]{2,1,0:T(8,128)S(1)}, u32[]{:S(2)}, u32[]{:S(2)}) collective-permute-start(f32[64,16,128]{2,1,0:T(8,128)S(1)} %get-tuple-element.22), channel_id=1, source_target_pairs={{0,15},{1,0},{2,1},{3,2},{4,3},{5,4},{6,5},{7,6},{8,7},{9,8},{10,9... | collective-permute-start | bytes 1572872 | tf_op jit(solution)/shard_map/ppermute | solution.py:509
  21.9 1.8 %copy-start.2 = (bf16[256,256]{1,0:T(8,128)(2,1)S(1)}, bf16[256,256]{1,0:T(8,128)(2,1)}, u32[]{:S(2)}) copy-start(bf16[256,256]{1,0:T(8,128)(2,1)} %constant.41.clone.refs_4_.refs_1_.depth_ref) | copy-start | bytes 393220
  24.7 11.5 %copy-start.4 = (bf16[256,256]{1,0:T(8,128)(2,1)S(1)}, bf16[256,256]{1,0:T(8,128)(2,1)}, u32[]{:S(2)}) copy-start(bf16[256,256]{1,0:T(8,128)(2,1)} %constant.42.clone.column_ref) | copy-start | bytes 393220
  24.7 11.5 %copy-start.5 = (bf16[256,256]{1,0:T(8,128)(2,1)S(1)}, bf16[256,256]{1,0:T(8,128)(2,1)}, u32[]{:S(2)}) copy-start(bf16[256,256]{1,0:T(8,128)(2,1)} %constant.44.clone.depth_back_ref) | copy-start | bytes 393220
  24.7 11.4 %copy-start.6 = (f32[32,32,128]{2,1,0:T(8,128)S(1)}, f32[32,32,128]{2,1,0:T(8,128)}, u32[]{:S(2)}) copy-start(f32[32,32,128]{2,1,0:T(8,128)} %other_ref.1) | copy-start | bytes 1572868
  24.7 11.4 %copy-start.7 = (bf16[128,256]{1,0:T(8,128)(2,1)S(1)}, bf16[128,256]{1,0:T(8,128)(2,1)}, u32[]{:S(2)}) copy-start(bf16[128,256]{1,0:T(8,128)(2,1)} %constant.43.clone.column_back_ref) | copy-start | bytes 196612
  34.5 4.8 %copy-start.1 = (f32[32,32,128]{2,1,0:T(8,128)S(1)}, f32[32,32,128]{2,1,0:T(8,128)}, u32[]{:S(2)}) copy-start(f32[32,32,128]{2,1,0:T(8,128)} %block_ref.1) | copy-start | bytes 1572868
  39.6 9.7 %collective-permute-start.4 = (f32[16,32,128]{2,1,0:T(8,128)S(1)}, f32[16,32,128]{2,1,0:T(8,128)S(1)}, u32[]{:S(2)}, u32[]{:S(2)}) collective-permute-start(f32[16,32,128]{2,1,0:T(8,128)S(1)} %get-tuple-element.25.refs_2_.last_ref), channel_id=1, source_target_pairs={{0,16},{16,32},{32,48},{48,64},{64,80},{80,96},{96,112},{112,128},... | collective-permute-start | bytes 786440 | tf_op jit(solution)/shard_map/ppermute | solution.py:505
  40.3 12.4 %collective-permute-start.5 = (f32[16,32,128]{2,1,0:T(8,128)S(1)}, f32[16,32,128]{2,1,0:T(8,128)S(1)}, u32[]{:S(2)}, u32[]{:S(2)}) collective-permute-start(f32[16,32,128]{2,1,0:T(8,128)S(1)} %get-tuple-element.26.refs_1_.first_ref), channel_id=1, source_target_pairs={{0,240},{16,0},{32,16},{48,32},{64,48},{80,64},{96,80},{112,96},{1... | collective-permute-start | bytes 786440 | tf_op jit(solution)/shard_map/ppermute | solution.py:506
  52.8 12.1 %collective-permute-start.6 = (f32[64,16,128]{2,1,0:T(8,128)S(1)}, f32[64,16,128]{2,1,0:T(8,128)S(1)}, u32[]{:S(2)}, u32[]{:S(2)}) collective-permute-start(f32[64,16,128]{2,1,0:T(8,128)S(1)} %get-tuple-element.27), channel_id=1, source_target_pairs={{0,1},{1,2},{2,3},{3,4},{4,5},{5,6},{6,7},{7,8},{8,9},{9,10},{10,1... | collective-permute-start | bytes 1572872 | tf_op jit(solution)/shard_map/ppermute | solution.py:508
  53.1 14.1 %collective-permute-start.7 = (f32[64,16,128]{2,1,0:T(8,128)S(1)}, f32[64,16,128]{2,1,0:T(8,128)S(1)}, u32[]{:S(2)}, u32[]{:S(2)}) collective-permute-start(f32[64,16,128]{2,1,0:T(8,128)S(1)} %get-tuple-element.28), channel_id=1, source_target_pairs={{0,15},{1,0},{2,1},{3,2},{4,3},{5,4},{6,5},{7,6},{8,7},{9,8},{10,9... | collective-permute-start | bytes 1572872 | tf_op jit(solution)/shard_map/ppermute | solution.py:509

commit v7 on v6

--- a/solution.py
+++ b/solution.py
@@ -260,10 +260,11 @@
     count, width, lanes = ref.shape
     step = 512 // width
     for x in range(0, count, step):
-        values = ref[x : x + step].reshape(step * width, lanes)
-        field[x_from + x : x_from + x + step, y_from : y_from + width, :] = along_depth(
+        size = min(step, count - x)
+        values = ref[x : x + size].reshape(size * width, lanes)
+        field[x_from + x : x_from + x + size, y_from : y_from + width, :] = along_depth(
             values, matrix
-        ).reshape(step, width, lanes)
+        ).reshape(size, width, lanes)
 
 
 def row_transforms(field, rows, width):
@@ -287,10 +288,14 @@
     lax.fori_loop(0, width // 8, chunk, 0)
 
 
-def edges_kernel(first_ref, last_ref, above_ref, below_ref, ends_ref, starts_ref):
-    for i, ref in enumerate((above_ref, first_ref, last_ref, below_ref)):
-        ends_ref[16 * i : 16 * i + 16] = ref[:, 16:, :]
-        starts_ref[16 * i : 16 * i + 16] = ref[:, :16, :]
+def edge_kernel(side, first_ref, last_ref, above_ref, below_ref, out_ref):
+    at = 0
+    for ref in (above_ref, first_ref, last_ref, below_ref):
+        count = ref.shape[0]
+        out_ref[at : at + count] = ref[:, side : side + 16, :]
+        at += count
+    if at < WINDOW:
+        out_ref[at] = jnp.zeros_like(out_ref[0])
 
 
 def split_kernel(block_ref, first_ref, last_ref, done):
@@ -311,6 +316,8 @@
     for ref in pieces:
         depth_piece(ref, matrix, field, at, 0)
         at += ref.shape[0]
+    if at < WINDOW:
+        field[at] = jnp.zeros_like(field[0])
     row_transforms(field, rows_ref, field.shape[1])
 
 
@@ -387,7 +394,10 @@
         if adjoint:
             out_refs[0][x : x + 16] = other_ref[x : x + 16] * result
         else:
-            out_refs[x // 16][...] = other_ref[x : x + 16] / result
+            quotient = other_ref[x : x + 16] / result
+            out_refs[x // 16][...] = quotient
+            if x == 0:
+                out_refs[2][...] = quotient[:15]
 
 
 def vmem(count):
@@ -414,15 +424,14 @@
     )
 
 
-def edges(first, last, above, below):
-    shape = jax.ShapeDtypeStruct((WINDOW, 16, first.shape[2]), jnp.float32)
+def edge(side, first, last, above, below):
     return pl.pallas_call(
-        edges_kernel,
-        out_shape=(shape, shape),
+        functools.partial(edge_kernel, side),
+        out_shape=jax.ShapeDtypeStruct((WINDOW, 16, first.shape[2]), jnp.float32),
         in_specs=vmem(4),
-        out_specs=tuple(vmem(2)),
-        compiler_params=pltpu.CompilerParams(vmem_limit_bytes=2 * 2**20),
-        name="edges",
+        out_specs=vmem(1)[0],
+        compiler_params=pltpu.CompilerParams(vmem_limit_bytes=2**20),
+        name="edge",
     )(first, last, above, below)
 
 
@@ -469,12 +478,12 @@
         1,
     )
     whole = jax.ShapeDtypeStruct(other.shape, jnp.float32)
-    half = jax.ShapeDtypeStruct((16,) + other.shape[1:], jnp.float32)
+    parts = [jax.ShapeDtypeStruct((rows,) + other.shape[1:], jnp.float32) for rows in (16, 16, 15)]
     return pl.pallas_call(
         functools.partial(convolve_kernel, adjoint),
-        out_shape=whole if adjoint else (half, half),
+        out_shape=whole if adjoint else tuple(parts),
         in_specs=vmem(9),
-        out_specs=vmem(1)[0] if adjoint else tuple(vmem(2)),
+        out_specs=vmem(1)[0] if adjoint else tuple(vmem(3)),
         scratch_shapes=[
             pltpu.VMEM((WINDOW, 16, depth), jnp.float32),
             pltpu.VMEM((PLANES, 32, depth), jnp.float32),
@@ -497,16 +506,15 @@
     )
 
 
-def halos(first, last):
+def halos(first, last, down):
     def ring(axis, step):
         count = lax.axis_size(axis)
         return [(i, (i + step) % count) for i in range(count)]
 
     above = lax.ppermute(last, "px", ring("px", 1))
-    below = lax.ppermute(first, "px", ring("px", -1))
-    ends, starts = edges(first, last, above, below)
-    left = lax.ppermute(ends, "py", ring("py", 1))
-    right = lax.ppermute(starts, "py", ring("py", -1))
+    below = lax.ppermute(down, "px", ring("px", -1))
+    left = lax.ppermute(edge(16, first, last, above, below), "py", ring("py", 1))
+    right = lax.ppermute(edge(0, first, last, above, below), "py", ring("py", -1))
     return first, last, above, below, left, right
 
 
@@ -556,7 +564,8 @@
 
 def shards(estimate, observed, psf):
     transfer = transfer_function(psf, estimate.shape[2])
-    pieces = halos(*split(estimate))
+    first, last = split(estimate)
+    pieces = halos(first, last, first)
     quotient = convolve(pieces, transfer, observed, False)
     around, quotient = lax.optimization_barrier((pieces[2:], quotient))
     scaled = estimate / (1.0 - penalty_weight * variation(estimate, pieces[:2] + around))

time: 71.5 us -> 70.1 us (0.980)
  waiting for transfers between devices: 37.8 us -> 35.6 us
  starting transfers between devices: 18 us -> 19.1 us
    ppermute x2, waiting for transfers between devices: 9.23 us -> 5.99 us  [halos(): above = lax.ppermute(last, 'px', ring('px', 1))]
    ppermute x6, starting transfers between devices: 13.5 us -> 15.1 us  [the longest x2 10.8 us: halos(): below = lax.ppermute(down, 'px', ring('px', -1))]
    ppermute x6, waiting for transfers between devices: 28.6 us -> 29.6 us  [the longest x2 16.3 us: halos(): lax.ppermute(edge(16, first, last, above, below), 'py', ring('py', 1))]
  transfers between devices with their start and end apart: 8 -> 8, of which waited for: 8 -> 7; matrix products, arithmetic and copies ran while one was open for 2% -> 2% of each run, Pallas kernels for 6% -> 8%
where the time goes in v7:
time: 70.1 us; the launch traced here: 70 us
  waiting for transfers between devices  35.6 us (51%)
  starting transfers between devices  19.1 us (27%)
  Pallas kernels  12.5 us (18%)
  other arithmetic  1.38 us (2%)
  local copies, waits for them, and re-layouts  1.19 us (2%)
    ppermute x2, waiting for transfers between devices, halos(): lax.ppermute(edge(16, first, last, above, below), 'py', ring('py', 1))  16.3 us
    ppermute x2, starting transfers between devices, halos(): below = lax.ppermute(down, 'px', ring('px', -1))  10.8 us
    ppermute x2, waiting for transfers between devices, halos(): below = lax.ppermute(down, 'px', ring('px', -1))  8.42 us
    pallas_call x2, Pallas kernels, convolve(): pl.pallas_call(functools.partial(convolve_kernel, adjoint), out_shape=who...  6.94 us
    ppermute x2, waiting for transfers between devices, halos(): above = lax.ppermute(last, 'px', ring('px', 1))  5.99 us
    ppermute x2, waiting for transfers between devices, halos(): lax.ppermute(edge(0, first, last, above, below), 'py', ring('py', -1))  4.87 us
    ppermute x2, starting transfers between devices, halos(): lax.ppermute(edge(16, first, last, above, below), 'py', ring('py', 1))  4.21 us
    ppermute x2, starting transfers between devices, halos(): above = lax.ppermute(last, 'px', ring('px', 1))  4 us
  transfers between devices with their start and end apart: 8, of which 7 were waited for; matrix products, arithmetic and copies ran while one was open for 2% of the time, Pallas kernels for 8%

profile of v7, /device:TPU:1, one launch (start us, length us, event | category | flops | bytes accessed | tf_op | source)
XLA Modules:
  0.0 70.0 jit_solution(11078370225457772005)
XLA Ops:
  0.0 1.0 %copy-done = f32[32,32,128]{2,1,0:T(8,128)S(1)} copy-done((f32[32,32,128]{2,1,0:T(8,128)S(1)}, f32[32,32,128]{2,1,0:T(8,128)}, u32[]{:S(2)}) %copy-start) | copy-done | bytes 524312
  1.1 3.8 %collective-permute-start = (f32[16,32,128]{2,1,0:T(8,128)S(1)}, f32[16,32,128]{2,1,0:T(8,128)S(1)}, u32[]{:S(2)}, u32[]{:S(2)}) collective-permute-start(f32[16,32,128]{2,1,0:T(8,128)S(1)} %get-tuple-element.17.last_ref.refs_2_), channel_id=1, source_target_pairs={{0,16},{16,32},{32,48},{48,64},{64,80},{80,96},{96,112},{112,128},... | collective-permute-start | bytes 786440 | tf_op jit(solution)/shard_map/ppermute | solution.py:514
  4.9 5.4 %collective-permute-start.1 = (f32[16,32,128]{2,1,0:T(8,128)S(1)}, f32[16,32,128]{2,1,0:T(8,128)S(1)}, u32[]{:S(2)}, u32[]{:S(2)}) collective-permute-start(f32[16,32,128]{2,1,0:T(8,128)S(1)} %get-tuple-element.18.first_ref.refs_1_), channel_id=1, source_target_pairs={{0,240},{16,0},{32,16},{48,32},{64,48},{80,64},{96,80},{112,96},{1... | collective-permute-start | bytes 786440 | tf_op jit(solution)/shard_map/ppermute | solution.py:515
  10.3 6.0 %collective-permute-done.above_ref.refs_0_ = f32[16,32,128]{2,1,0:T(8,128)S(1)} collective-permute-done((f32[16,32,128]{2,1,0:T(8,128)S(1)}, f32[16,32,128]{2,1,0:T(8,128)S(1)}, u32[]{:S(2)}, u32[]{:S(2)}) %collective-permute-start) | collective-permute-done | bytes 262176 | tf_op jit(solution)/shard_map/ppermute | solution.py:514
  16.3 2.6 %collective-permute-done.1.below_ref.refs_3_ = f32[16,32,128]{2,1,0:T(8,128)S(1)} collective-permute-done((f32[16,32,128]{2,1,0:T(8,128)S(1)}, f32[16,32,128]{2,1,0:T(8,128)S(1)}, u32[]{:S(2)}, u32[]{:S(2)}) %collective-permute-start.1) | collective-permute-done | bytes 262176 | tf_op jit(solution)/shard_map/ppermute | solution.py:515
  19.0 2.2 %collective-permute-start.2 = (f32[64,16,128]{2,1,0:T(8,128)S(1)}, f32[64,16,128]{2,1,0:T(8,128)S(1)}, u32[]{:S(2)}, u32[]{:S(2)}) collective-permute-start(f32[64,16,128]{2,1,0:T(8,128)S(1)} %edge.4), channel_id=1, source_target_pairs={{0,1},{1,2},{2,3},{3,4},{4,5},{5,6},{6,7},{7,8},{8,9},{9,10},{10,1... | collective-permute-start | bytes 1572872 | tf_op jit(solution)/shard_map/ppermute | solution.py:516
  21.2 0.8 %edge.5 = f32[64,16,128]{2,1,0:T(8,128)} custom-call(f32[16,32,128]{2,1,0:T(8,128)S(1)} %get-tuple-element.18.first_ref.refs_1_, f32[16,32,128]{2,1,0:T(8,128)S(1)} %get-tuple-element.17.last_ref.refs_2_, f32[16,32,128]{2,1,0:T(8,128)S(1)} %collective-permute-done.above_ref.refs_0_, f32[16,32,128]{2,1,0:T(8,128)S(1)} %collective-permute-done.1.below_ref.refs_3_), custom_call_target="tpu_custom_call" | custom-call | tf_op jit(solution)/shard_map/edge/pallas_call | solution.py:428
  22.1 1.8 %transfer.1.transfer_ref = f32[34,256,128]{2,1,0:T(8,128)S(1)} custom-call(f32[32,32,32]{2,1,0:T(8,128)S(1)} %copy-done.3, f32[32,128]{1,0:T(8,128)S(1)} %copy-done.9, bf16[256,128]{1,0:T(8,128)(2,1)S(1)} %copy-done.8), custom_call_target="tpu_custom_call" | custom-call | tf_op jit(solution)/shard_map/transfer/pallas_call | solution.py:410
  23.9 0.9 %inner.2.inner_ref = f32[34,64,128]{2,1,0:T(8,128)S(1)} custom-call(f32[16,32,128]{2,1,0:T(8,128)S(1)} %collective-permute-done.above_ref.refs_0_, f32[16,32,128]{2,1,0:T(8,128)S(1)} %get-tuple-element.18.first_ref.refs_1_, f32[16,32,128]{2,1,0:T(8,128)S(1)} %get-tuple-element.17.last_ref.refs_2_, ...), custom_call_target="tpu_custom_call" | custom-call | tf_op jit(solution)/shard_map/inner/pallas_call | solution.py:453
  24.9 8.1 %collective-permute-done.2.refs_0_ = f32[64,16,128]{2,1,0:T(8,128)S(1)} collective-permute-done((f32[64,16,128]{2,1,0:T(8,128)S(1)}, f32[64,16,128]{2,1,0:T(8,128)S(1)}, u32[]{:S(2)}, u32[]{:S(2)}) %collective-permute-start.2) | collective-permute-done | bytes 524320 | tf_op jit(solution)/shard_map/ppermute | solution.py:516
  33.0 0.5 left.2.left_ref
  33.5 3.0 %collective-permute-done.3.right_ref = f32[64,16,128]{2,1,0:T(8,128)S(1)} collective-permute-done((f32[64,16,128]{2,1,0:T(8,128)}, f32[64,16,128]{2,1,0:T(8,128)S(1)}, u32[]{:S(2)}, u32[]{:S(2)}) %collective-permute-start.3) | collective-permute-done | bytes 524320 | tf_op jit(solution)/shard_map/ppermute | solution.py:517
  36.5 3.1 %convolve.1 = (f32[16,32,128]{2,1,0:T(8,128)S(1)}, f32[16,32,128]{2,1,0:T(8,128)S(1)}, f32[15,32,128]{2,1,0:T(8,128)S(1)}) custom-call(f32[34,64,128]{2,1,0:T(8,128)S(1)} %inner.2.inner_ref, f32[34,32,128]{2,1,0:T(8,128)S(1)} %left.2.left_ref, f32[64,16,128]{2,1,0:T(8,128)S(1)} %collective-permute-done.3.right_ref, ...), custom_call_target="tpu_custom_call" | custom-call | tf_op jit(solution)/shard_map/convolve/pallas_call | solution.py:482
  40.1 5.4 %collective-permute-start.5 = (f32[15,32,128]{2,1,0:T(8,128)S(1)}, f32[15,32,128]{2,1,0:T(8,128)S(1)}, u32[]{:S(2)}, u32[]{:S(2)}) collective-permute-start(f32[15,32,128]{2,1,0:T(8,128)S(1)} %get-tuple-element.24), channel_id=1, source_target_pairs={{0,240},{16,0},{32,16},{48,32},{64,48},{80,64},{96,80},{112,96},{1... | collective-permute-start | bytes 737288 | tf_op jit(solution)/shard_map/ppermute | solution.py:515
  45.5 0.4 fusion.8
  46.0 5.8 %collective-permute-done.5.refs_3_.below_ref = f32[15,32,128]{2,1,0:T(8,128)S(1)} collective-permute-done((f32[15,32,128]{2,1,0:T(8,128)S(1)}, f32[15,32,128]{2,1,0:T(8,128)S(1)}, u32[]{:S(2)}, u32[]{:S(2)}) %collective-permute-start.5) | collective-permute-done | bytes 245792 | tf_op jit(solution)/shard_map/ppermute | solution.py:515
  52.0 2.0 %collective-permute-start.6 = (f32[64,16,128]{2,1,0:T(8,128)S(1)}, f32[64,16,128]{2,1,0:T(8,128)S(1)}, u32[]{:S(2)}, u32[]{:S(2)}) collective-permute-start(f32[64,16,128]{2,1,0:T(8,128)S(1)} %edge.6), channel_id=1, source_target_pairs={{0,1},{1,2},{2,3},{3,4},{4,5},{5,6},{6,7},{7,8},{8,9},{9,10},{10,1... | collective-permute-start | bytes 1572872 | tf_op jit(solution)/shard_map/ppermute | solution.py:516
  53.9 0.3 fusion.9
  54.3 0.4 fusion.6.other_ref
  54.6 0.9 %inner.3.inner_ref = f32[34,64,128]{2,1,0:T(8,128)S(1)} custom-call(f32[16,32,128]{2,1,0:T(8,128)S(1)} %collective-permute-done.4.refs_0_.above_ref, f32[16,32,128]{2,1,0:T(8,128)S(1)} %get-tuple-element.23.refs_1_.first_ref, f32[16,32,128]{2,1,0:T(8,128)S(1)} %get-tuple-element.22.refs_2_.last_ref, ...), custom_call_target="tpu_custom_call" | custom-call | tf_op jit(solution)/shard_map/inner/pallas_call | solution.py:453
  55.5 8.2 %collective-permute-done.6.refs_0_ = f32[64,16,128]{2,1,0:T(8,128)S(1)} collective-permute-done((f32[64,16,128]{2,1,0:T(8,128)S(1)}, f32[64,16,128]{2,1,0:T(8,128)S(1)}, u32[]{:S(2)}, u32[]{:S(2)}) %collective-permute-start.6) | collective-permute-done | bytes 524320 | tf_op jit(solution)/shard_map/ppermute | solution.py:516
  63.8 0.5 left.3.left_ref
  64.3 1.9 %collective-permute-done.7.right_ref = f32[64,16,128]{2,1,0:T(8,128)S(1)} collective-permute-done((f32[64,16,128]{2,1,0:T(8,128)S(1)}, f32[64,16,128]{2,1,0:T(8,128)S(1)}, u32[]{:S(2)}, u32[]{:S(2)}) %collective-permute-start.7) | collective-permute-done | bytes 524320 | tf_op jit(solution)/shard_map/ppermute | solution.py:517
  66.1 3.9 %correlate.1 = f32[32,32,128]{2,1,0:T(8,128)} custom-call(f32[34,64,128]{2,1,0:T(8,128)S(1)} %inner.3.inner_ref, f32[34,32,128]{2,1,0:T(8,128)S(1)} %left.3.left_ref, f32[64,16,128]{2,1,0:T(8,128)S(1)} %collective-permute-done.7.right_ref, f32[34,256,128]{2,1,0:T(8,128)S(1)} %transfer.1.transfer_ref, f32[32,32,128]{2,1,0:T(8,128)S(1)} %fusion.6.other_ref, ...), custom_call_target="tpu_custom_call" | custom-call | tf_op jit(solution)/shard_map/correlate/pallas_call | solution.py:482
  (35 shorter events, 0.9 us)
Async XLA Ops:
  0.0 1.0 %copy-start = (f32[32,32,128]{2,1,0:T(8,128)S(1)}, f32[32,32,128]{2,1,0:T(8,128)}, u32[]{:S(2)}) copy-start(f32[32,32,128]{2,1,0:T(8,128)} %block_ref.1) | copy-start | bytes 1572868
  1.1 15.2 %collective-permute-start = (f32[16,32,128]{2,1,0:T(8,128)S(1)}, f32[16,32,128]{2,1,0:T(8,128)S(1)}, u32[]{:S(2)}, u32[]{:S(2)}) collective-permute-start(f32[16,32,128]{2,1,0:T(8,128)S(1)} %get-tuple-element.17.last_ref.refs_2_), channel_id=1, source_target_pairs={{0,16},{16,32},{32,48},{48,64},{64,80},{80,96},{96,112},{112,128},... | collective-permute-start | bytes 786440 | tf_op jit(solution)/shard_map/ppermute | solution.py:514
  4.9 14.0 %collective-permute-start.1 = (f32[16,32,128]{2,1,0:T(8,128)S(1)}, f32[16,32,128]{2,1,0:T(8,128)S(1)}, u32[]{:S(2)}, u32[]{:S(2)}) collective-permute-start(f32[16,32,128]{2,1,0:T(8,128)S(1)} %get-tuple-element.18.first_ref.refs_1_), channel_id=1, source_target_pairs={{0,240},{16,0},{32,16},{48,32},{64,48},{80,64},{96,80},{112,96},{1... | collective-permute-start | bytes 786440 | tf_op jit(solution)/shard_map/ppermute | solution.py:515
  18.9 3.1 %copy-start.3 = (f32[32,32,32]{2,1,0:T(8,128)S(1)}, f32[32,32,32]{2,1,0:T(8,128)}, u32[]{:S(2)}) copy-start(f32[32,32,32]{2,1,0:T(8,128)} %psf_ref.1) | copy-start | bytes 393220
  19.0 3.1 %copy-start.8 = (bf16[256,128]{1,0:T(8,128)(2,1)S(1)}, bf16[256,128]{1,0:T(8,128)(2,1)}, u32[]{:S(2)}) copy-start(bf16[256,128]{1,0:T(8,128)(2,1)} %constant.40.clone.column_ref) | copy-start | bytes 196612
  19.0 3.1 %copy-start.9 = (f32[32,128]{1,0:T(8,128)S(1)}, f32[32,128]{1,0:T(8,128)}, u32[]{:S(2)}) copy-start(f32[32,128]{1,0:T(8,128)} %constant.39.clone.depth_ref) | copy-start | bytes 49156
  19.0 14.0 %collective-permute-start.2 = (f32[64,16,128]{2,1,0:T(8,128)S(1)}, f32[64,16,128]{2,1,0:T(8,128)S(1)}, u32[]{:S(2)}, u32[]{:S(2)}) collective-permute-start(f32[64,16,128]{2,1,0:T(8,128)S(1)} %edge.4), channel_id=1, source_target_pairs={{0,1},{1,2},{2,3},{3,4},{4,5},{5,6},{6,7},{7,8},{8,9},{9,10},{10,1... | collective-permute-start | bytes 1572872 | tf_op jit(solution)/shard_map/ppermute | solution.py:516
  22.0 14.4 %collective-permute-start.3 = (f32[64,16,128]{2,1,0:T(8,128)}, f32[64,16,128]{2,1,0:T(8,128)S(1)}, u32[]{:S(2)}, u32[]{:S(2)}) collective-permute-start(f32[64,16,128]{2,1,0:T(8,128)} %edge.5), channel_id=1, source_target_pairs={{0,15},{1,0},{2,1},{3,2},{4,3},{5,4},{6,5},{7,6},{8,7},{9,8},{10,9... | collective-permute-start | bytes 1572872 | tf_op jit(solution)/shard_map/ppermute | solution.py:517
  22.1 1.8 %copy-start.2 = (bf16[256,256]{1,0:T(8,128)(2,1)S(1)}, bf16[256,256]{1,0:T(8,128)(2,1)}, u32[]{:S(2)}) copy-start(bf16[256,256]{1,0:T(8,128)(2,1)} %constant.41.clone.refs_4_.refs_1_.depth_ref) | copy-start | bytes 393220
  24.8 11.7 %copy-start.4 = (bf16[256,256]{1,0:T(8,128)(2,1)S(1)}, bf16[256,256]{1,0:T(8,128)(2,1)}, u32[]{:S(2)}) copy-start(bf16[256,256]{1,0:T(8,128)(2,1)} %constant.42.clone.column_ref) | copy-start | bytes 393220
  24.8 11.7 %copy-start.5 = (bf16[256,256]{1,0:T(8,128)(2,1)S(1)}, bf16[256,256]{1,0:T(8,128)(2,1)}, u32[]{:S(2)}) copy-start(bf16[256,256]{1,0:T(8,128)(2,1)} %constant.44.clone.depth_back_ref) | copy-start | bytes 393220
  24.8 11.7 %copy-start.6 = (f32[32,32,128]{2,1,0:T(8,128)S(1)}, f32[32,32,128]{2,1,0:T(8,128)}, u32[]{:S(2)}) copy-start(f32[32,32,128]{2,1,0:T(8,128)} %other_ref.1) | copy-start | bytes 1572868
  24.8 11.6 %copy-start.7 = (bf16[128,256]{1,0:T(8,128)(2,1)S(1)}, bf16[128,256]{1,0:T(8,128)(2,1)}, u32[]{:S(2)}) copy-start(bf16[128,256]{1,0:T(8,128)(2,1)} %constant.43.clone.column_back_ref) | copy-start | bytes 196612
  33.4 6.2 %copy-start.1 = (f32[32,32,128]{2,1,0:T(8,128)S(1)}, f32[32,32,128]{2,1,0:T(8,128)}, u32[]{:S(2)}) copy-start(f32[32,32,128]{2,1,0:T(8,128)} %block_ref.1) | copy-start | bytes 1572868
  40.0 11.8 %collective-permute-start.4 = (f32[16,32,128]{2,1,0:T(8,128)S(1)}, f32[16,32,128]{2,1,0:T(8,128)S(1)}, u32[]{:S(2)}, u32[]{:S(2)}) collective-permute-start(f32[16,32,128]{2,1,0:T(8,128)S(1)} %get-tuple-element.22.refs_2_.last_ref), channel_id=1, source_target_pairs={{0,16},{16,32},{32,48},{48,64},{64,80},{80,96},{96,112},{112,128},... | collective-permute-start | bytes 786440 | tf_op jit(solution)/shard_map/ppermute | solution.py:514
  40.1 11.6 %collective-permute-start.5 = (f32[15,32,128]{2,1,0:T(8,128)S(1)}, f32[15,32,128]{2,1,0:T(8,128)S(1)}, u32[]{:S(2)}, u32[]{:S(2)}) collective-permute-start(f32[15,32,128]{2,1,0:T(8,128)S(1)} %get-tuple-element.24), channel_id=1, source_target_pairs={{0,240},{16,0},{32,16},{48,32},{64,48},{80,64},{96,80},{112,96},{1... | collective-permute-start | bytes 737288 | tf_op jit(solution)/shard_map/ppermute | solution.py:515
  51.8 14.3 %collective-permute-start.7 = (f32[64,16,128]{2,1,0:T(8,128)S(1)}, f32[64,16,128]{2,1,0:T(8,128)S(1)}, u32[]{:S(2)}, u32[]{:S(2)}) collective-permute-start(f32[64,16,128]{2,1,0:T(8,128)S(1)} %edge.7), channel_id=1, source_target_pairs={{0,15},{1,0},{2,1},{3,2},{4,3},{5,4},{6,5},{7,6},{8,7},{9,8},{10,9... | collective-permute-start | bytes 1572872 | tf_op jit(solution)/shard_map/ppermute | solution.py:517
  52.0 11.8 %collective-permute-start.6 = (f32[64,16,128]{2,1,0:T(8,128)S(1)}, f32[64,16,128]{2,1,0:T(8,128)S(1)}, u32[]{:S(2)}, u32[]{:S(2)}) collective-permute-start(f32[64,16,128]{2,1,0:T(8,128)S(1)} %edge.6), channel_id=1, source_target_pairs={{0,1},{1,2},{2,3},{3,4},{4,5},{5,6},{6,7},{7,8},{8,9},{9,10},{10,1... | collective-permute-start | bytes 1572872 | tf_op jit(solution)/shard_map/ppermute | solution.py:516

commit v8 on v7

--- a/solution.py
+++ b/solution.py
@@ -285,7 +285,7 @@
         rows_forward(load, store, zero)
         return carry
 
-    lax.fori_loop(0, width // 8, chunk, 0)
+    lax.fori_loop(0, width // 8, chunk, 0, unroll=2)
 
 
 def edge_kernel(side, first_ref, last_ref, above_ref, below_ref, out_ref):
@@ -385,7 +385,7 @@
         rows_inverse(load, store)
         return carry
 
-    lax.fori_loop(0, 4, chunk_back, 0)
+    lax.fori_loop(0, 4, chunk_back, 0, unroll=2)
 
     matrix = depth_back_ref[...]
     for x in range(0, 32, 16):

time: 70.1 us -> 69.8 us (level)
  no operation moved by 1% of the time
where the time goes in v8:
time: 69.8 us; the launch traced here: 69.7 us
  waiting for transfers between devices  35.8 us (51%)
  starting transfers between devices  19.1 us (27%)
  Pallas kernels  12 us (17%)
  other arithmetic  1.38 us (2%)
  local copies, waits for them, and re-layouts  1.19 us (2%)
    ppermute x2, waiting for transfers between devices, halos(): lax.ppermute(edge(16, first, last, above, below), 'py', ring('py', 1))  16.4 us
    ppermute x2, starting transfers between devices, halos(): below = lax.ppermute(down, 'px', ring('px', -1))  10.8 us
    ppermute x2, waiting for transfers between devices, halos(): below = lax.ppermute(down, 'px', ring('px', -1))  8.42 us
    pallas_call x2, Pallas kernels, convolve(): pl.pallas_call(functools.partial(convolve_kernel, adjoint), out_shape=who...  6.66 us
    ppermute x2, waiting for transfers between devices, halos(): above = lax.ppermute(last, 'px', ring('px', 1))  5.99 us
    ppermute x2, waiting for transfers between devices, halos(): lax.ppermute(edge(0, first, last, above, below), 'py', ring('py', -1))  4.98 us
    ppermute x2, starting transfers between devices, halos(): lax.ppermute(edge(16, first, last, above, below), 'py', ring('py', 1))  4.21 us
    ppermute x2, starting transfers between devices, halos(): above = lax.ppermute(last, 'px', ring('px', 1))  4 us
  transfers between devices with their start and end apart: 8, of which 7 were waited for; matrix products, arithmetic and copies ran while one was open for 2% of the time, Pallas kernels for 8%

profile of v8, /device:TPU:1, one launch (start us, length us, event | category | flops | bytes accessed | tf_op | source)
XLA Modules:
  0.0 69.7 jit_solution(1159034953124991829)
XLA Ops:
  0.0 1.0 %copy-done = f32[32,32,128]{2,1,0:T(8,128)S(1)} copy-done((f32[32,32,128]{2,1,0:T(8,128)S(1)}, f32[32,32,128]{2,1,0:T(8,128)}, u32[]{:S(2)}) %copy-start) | copy-done | bytes 524312
  1.1 3.8 %collective-permute-start = (f32[16,32,128]{2,1,0:T(8,128)S(1)}, f32[16,32,128]{2,1,0:T(8,128)S(1)}, u32[]{:S(2)}, u32[]{:S(2)}) collective-permute-start(f32[16,32,128]{2,1,0:T(8,128)S(1)} %get-tuple-element.17.last_ref.refs_2_), channel_id=1, source_target_pairs={{0,16},{16,32},{32,48},{48,64},{64,80},{80,96},{96,112},{112,128},... | collective-permute-start | bytes 786440 | tf_op jit(solution)/shard_map/ppermute | solution.py:514
  4.9 5.4 %collective-permute-start.1 = (f32[16,32,128]{2,1,0:T(8,128)S(1)}, f32[16,32,128]{2,1,0:T(8,128)S(1)}, u32[]{:S(2)}, u32[]{:S(2)}) collective-permute-start(f32[16,32,128]{2,1,0:T(8,128)S(1)} %get-tuple-element.18.first_ref.refs_1_), channel_id=1, source_target_pairs={{0,240},{16,0},{32,16},{48,32},{64,48},{80,64},{96,80},{112,96},{1... | collective-permute-start | bytes 786440 | tf_op jit(solution)/shard_map/ppermute | solution.py:515
  10.3 6.0 %collective-permute-done.above_ref.refs_0_ = f32[16,32,128]{2,1,0:T(8,128)S(1)} collective-permute-done((f32[16,32,128]{2,1,0:T(8,128)S(1)}, f32[16,32,128]{2,1,0:T(8,128)S(1)}, u32[]{:S(2)}, u32[]{:S(2)}) %collective-permute-start) | collective-permute-done | bytes 262176 | tf_op jit(solution)/shard_map/ppermute | solution.py:514
  16.3 2.6 %collective-permute-done.1.below_ref.refs_3_ = f32[16,32,128]{2,1,0:T(8,128)S(1)} collective-permute-done((f32[16,32,128]{2,1,0:T(8,128)S(1)}, f32[16,32,128]{2,1,0:T(8,128)S(1)}, u32[]{:S(2)}, u32[]{:S(2)}) %collective-permute-start.1) | collective-permute-done | bytes 262176 | tf_op jit(solution)/shard_map/ppermute | solution.py:515
  19.0 2.2 %collective-permute-start.2 = (f32[64,16,128]{2,1,0:T(8,128)S(1)}, f32[64,16,128]{2,1,0:T(8,128)S(1)}, u32[]{:S(2)}, u32[]{:S(2)}) collective-permute-start(f32[64,16,128]{2,1,0:T(8,128)S(1)} %edge.4), channel_id=1, source_target_pairs={{0,1},{1,2},{2,3},{3,4},{4,5},{5,6},{6,7},{7,8},{8,9},{9,10},{10,1... | collective-permute-start | bytes 1572872 | tf_op jit(solution)/shard_map/ppermute | solution.py:516
  21.2 0.8 %edge.5 = f32[64,16,128]{2,1,0:T(8,128)} custom-call(f32[16,32,128]{2,1,0:T(8,128)S(1)} %get-tuple-element.18.first_ref.refs_1_, f32[16,32,128]{2,1,0:T(8,128)S(1)} %get-tuple-element.17.last_ref.refs_2_, f32[16,32,128]{2,1,0:T(8,128)S(1)} %collective-permute-done.above_ref.refs_0_, f32[16,32,128]{2,1,0:T(8,128)S(1)} %collective-permute-done.1.below_ref.refs_3_), custom_call_target="tpu_custom_call" | custom-call | tf_op jit(solution)/shard_map/edge/pallas_call | solution.py:428
  22.1 1.8 %transfer.1.transfer_ref = f32[34,256,128]{2,1,0:T(8,128)S(1)} custom-call(f32[32,32,32]{2,1,0:T(8,128)S(1)} %copy-done.3, f32[32,128]{1,0:T(8,128)S(1)} %copy-done.9, bf16[256,128]{1,0:T(8,128)(2,1)S(1)} %copy-done.8), custom_call_target="tpu_custom_call" | custom-call | tf_op jit(solution)/shard_map/transfer/pallas_call | solution.py:410
  23.9 0.9 %inner.2.inner_ref = f32[34,64,128]{2,1,0:T(8,128)S(1)} custom-call(f32[16,32,128]{2,1,0:T(8,128)S(1)} %collective-permute-done.above_ref.refs_0_, f32[16,32,128]{2,1,0:T(8,128)S(1)} %get-tuple-element.18.first_ref.refs_1_, f32[16,32,128]{2,1,0:T(8,128)S(1)} %get-tuple-element.17.last_ref.refs_2_, ...), custom_call_target="tpu_custom_call" | custom-call | tf_op jit(solution)/shard_map/inner/pallas_call | solution.py:453
  24.8 8.1 %collective-permute-done.2.refs_0_ = f32[64,16,128]{2,1,0:T(8,128)S(1)} collective-permute-done((f32[64,16,128]{2,1,0:T(8,128)S(1)}, f32[64,16,128]{2,1,0:T(8,128)S(1)}, u32[]{:S(2)}, u32[]{:S(2)}) %collective-permute-start.2) | collective-permute-done | bytes 524320 | tf_op jit(solution)/shard_map/ppermute | solution.py:516
  33.0 0.4 left.2.left_ref
  33.4 3.1 %collective-permute-done.3.right_ref = f32[64,16,128]{2,1,0:T(8,128)S(1)} collective-permute-done((f32[64,16,128]{2,1,0:T(8,128)}, f32[64,16,128]{2,1,0:T(8,128)S(1)}, u32[]{:S(2)}, u32[]{:S(2)}) %collective-permute-start.3) | collective-permute-done | bytes 524320 | tf_op jit(solution)/shard_map/ppermute | solution.py:517
  36.5 2.9 %convolve.1 = (f32[16,32,128]{2,1,0:T(8,128)S(1)}, f32[16,32,128]{2,1,0:T(8,128)S(1)}, f32[15,32,128]{2,1,0:T(8,128)S(1)}) custom-call(f32[34,64,128]{2,1,0:T(8,128)S(1)} %inner.2.inner_ref, f32[34,32,128]{2,1,0:T(8,128)S(1)} %left.2.left_ref, f32[64,16,128]{2,1,0:T(8,128)S(1)} %collective-permute-done.3.right_ref, ...), custom_call_target="tpu_custom_call" | custom-call | tf_op jit(solution)/shard_map/convolve/pallas_call | solution.py:482
  40.0 5.4 %collective-permute-start.5 = (f32[15,32,128]{2,1,0:T(8,128)S(1)}, f32[15,32,128]{2,1,0:T(8,128)S(1)}, u32[]{:S(2)}, u32[]{:S(2)}) collective-permute-start(f32[15,32,128]{2,1,0:T(8,128)S(1)} %get-tuple-element.24), channel_id=1, source_target_pairs={{0,240},{16,0},{32,16},{48,32},{64,48},{80,64},{96,80},{112,96},{1... | collective-permute-start | bytes 737288 | tf_op jit(solution)/shard_map/ppermute | solution.py:515
  45.4 0.4 fusion.8
  45.8 5.8 %collective-permute-done.5.refs_3_.below_ref = f32[15,32,128]{2,1,0:T(8,128)S(1)} collective-permute-done((f32[15,32,128]{2,1,0:T(8,128)S(1)}, f32[15,32,128]{2,1,0:T(8,128)S(1)}, u32[]{:S(2)}, u32[]{:S(2)}) %collective-permute-start.5) | collective-permute-done | bytes 245792 | tf_op jit(solution)/shard_map/ppermute | solution.py:515
  51.8 2.0 %collective-permute-start.6 = (f32[64,16,128]{2,1,0:T(8,128)S(1)}, f32[64,16,128]{2,1,0:T(8,128)S(1)}, u32[]{:S(2)}, u32[]{:S(2)}) collective-permute-start(f32[64,16,128]{2,1,0:T(8,128)S(1)} %edge.6), channel_id=1, source_target_pairs={{0,1},{1,2},{2,3},{3,4},{4,5},{5,6},{6,7},{7,8},{8,9},{9,10},{10,1... | collective-permute-start | bytes 1572872 | tf_op jit(solution)/shard_map/ppermute | solution.py:516
  53.8 0.3 fusion.9
  54.1 0.4 fusion.6.other_ref
  54.5 0.9 %inner.3.inner_ref = f32[34,64,128]{2,1,0:T(8,128)S(1)} custom-call(f32[16,32,128]{2,1,0:T(8,128)S(1)} %collective-permute-done.4.refs_0_.above_ref, f32[16,32,128]{2,1,0:T(8,128)S(1)} %get-tuple-element.23.refs_1_.first_ref, f32[16,32,128]{2,1,0:T(8,128)S(1)} %get-tuple-element.22.refs_2_.last_ref, ...), custom_call_target="tpu_custom_call" | custom-call | tf_op jit(solution)/shard_map/inner/pallas_call | solution.py:453
  55.4 8.3 %collective-permute-done.6.refs_0_ = f32[64,16,128]{2,1,0:T(8,128)S(1)} collective-permute-done((f32[64,16,128]{2,1,0:T(8,128)S(1)}, f32[64,16,128]{2,1,0:T(8,128)S(1)}, u32[]{:S(2)}, u32[]{:S(2)}) %collective-permute-start.6) | collective-permute-done | bytes 524320 | tf_op jit(solution)/shard_map/ppermute | solution.py:516
  63.6 0.4 left.3.left_ref
  64.1 1.9 %collective-permute-done.7.right_ref = f32[64,16,128]{2,1,0:T(8,128)S(1)} collective-permute-done((f32[64,16,128]{2,1,0:T(8,128)S(1)}, f32[64,16,128]{2,1,0:T(8,128)S(1)}, u32[]{:S(2)}, u32[]{:S(2)}) %collective-permute-start.7) | collective-permute-done | bytes 524320 | tf_op jit(solution)/shard_map/ppermute | solution.py:517
  66.0 3.7 %correlate.1 = f32[32,32,128]{2,1,0:T(8,128)} custom-call(f32[34,64,128]{2,1,0:T(8,128)S(1)} %inner.3.inner_ref, f32[34,32,128]{2,1,0:T(8,128)S(1)} %left.3.left_ref, f32[64,16,128]{2,1,0:T(8,128)S(1)} %collective-permute-done.7.right_ref, f32[34,256,128]{2,1,0:T(8,128)S(1)} %transfer.1.transfer_ref, f32[32,32,128]{2,1,0:T(8,128)S(1)} %fusion.6.other_ref, ...), custom_call_target="tpu_custom_call" | custom-call | tf_op jit(solution)/shard_map/correlate/pallas_call | solution.py:482
  (35 shorter events, 0.9 us)
Async XLA Ops:
  0.0 1.0 %copy-start = (f32[32,32,128]{2,1,0:T(8,128)S(1)}, f32[32,32,128]{2,1,0:T(8,128)}, u32[]{:S(2)}) copy-start(f32[32,32,128]{2,1,0:T(8,128)} %block_ref.1) | copy-start | bytes 1572868
  1.1 15.2 %collective-permute-start = (f32[16,32,128]{2,1,0:T(8,128)S(1)}, f32[16,32,128]{2,1,0:T(8,128)S(1)}, u32[]{:S(2)}, u32[]{:S(2)}) collective-permute-start(f32[16,32,128]{2,1,0:T(8,128)S(1)} %get-tuple-element.17.last_ref.refs_2_), channel_id=1, source_target_pairs={{0,16},{16,32},{32,48},{48,64},{64,80},{80,96},{96,112},{112,128},... | collective-permute-start | bytes 786440 | tf_op jit(solution)/shard_map/ppermute | solution.py:514
  4.9 14.0 %collective-permute-start.1 = (f32[16,32,128]{2,1,0:T(8,128)S(1)}, f32[16,32,128]{2,1,0:T(8,128)S(1)}, u32[]{:S(2)}, u32[]{:S(2)}) collective-permute-start(f32[16,32,128]{2,1,0:T(8,128)S(1)} %get-tuple-element.18.first_ref.refs_1_), channel_id=1, source_target_pairs={{0,240},{16,0},{32,16},{48,32},{64,48},{80,64},{96,80},{112,96},{1... | collective-permute-start | bytes 786440 | tf_op jit(solution)/shard_map/ppermute | solution.py:515
  18.9 3.1 %copy-start.3 = (f32[32,32,32]{2,1,0:T(8,128)S(1)}, f32[32,32,32]{2,1,0:T(8,128)}, u32[]{:S(2)}) copy-start(f32[32,32,32]{2,1,0:T(8,128)} %psf_ref.1) | copy-start | bytes 393220
  19.0 3.1 %copy-start.8 = (bf16[256,128]{1,0:T(8,128)(2,1)S(1)}, bf16[256,128]{1,0:T(8,128)(2,1)}, u32[]{:S(2)}) copy-start(bf16[256,128]{1,0:T(8,128)(2,1)} %constant.40.clone.column_ref) | copy-start | bytes 196612
  19.0 3.1 %copy-start.9 = (f32[32,128]{1,0:T(8,128)S(1)}, f32[32,128]{1,0:T(8,128)}, u32[]{:S(2)}) copy-start(f32[32,128]{1,0:T(8,128)} %constant.39.clone.depth_ref) | copy-start | bytes 49156
  19.0 14.0 %collective-permute-start.2 = (f32[64,16,128]{2,1,0:T(8,128)S(1)}, f32[64,16,128]{2,1,0:T(8,128)S(1)}, u32[]{:S(2)}, u32[]{:S(2)}) collective-permute-start(f32[64,16,128]{2,1,0:T(8,128)S(1)} %edge.4), channel_id=1, source_target_pairs={{0,1},{1,2},{2,3},{3,4},{4,5},{5,6},{6,7},{7,8},{8,9},{9,10},{10,1... | collective-permute-start | bytes 1572872 | tf_op jit(solution)/shard_map/ppermute | solution.py:516
  22.0 14.4 %collective-permute-start.3 = (f32[64,16,128]{2,1,0:T(8,128)}, f32[64,16,128]{2,1,0:T(8,128)S(1)}, u32[]{:S(2)}, u32[]{:S(2)}) collective-permute-start(f32[64,16,128]{2,1,0:T(8,128)} %edge.5), channel_id=1, source_target_pairs={{0,15},{1,0},{2,1},{3,2},{4,3},{5,4},{6,5},{7,6},{8,7},{9,8},{10,9... | collective-permute-start | bytes 1572872 | tf_op jit(solution)/shard_map/ppermute | solution.py:517
  22.1 1.8 %copy-start.2 = (bf16[256,256]{1,0:T(8,128)(2,1)S(1)}, bf16[256,256]{1,0:T(8,128)(2,1)}, u32[]{:S(2)}) copy-start(bf16[256,256]{1,0:T(8,128)(2,1)} %constant.41.clone.refs_4_.refs_1_.depth_ref) | copy-start | bytes 393220
  24.8 11.7 %copy-start.4 = (bf16[256,256]{1,0:T(8,128)(2,1)S(1)}, bf16[256,256]{1,0:T(8,128)(2,1)}, u32[]{:S(2)}) copy-start(bf16[256,256]{1,0:T(8,128)(2,1)} %constant.42.clone.column_ref) | copy-start | bytes 393220
  24.8 11.7 %copy-start.5 = (bf16[256,256]{1,0:T(8,128)(2,1)S(1)}, bf16[256,256]{1,0:T(8,128)(2,1)}, u32[]{:S(2)}) copy-start(bf16[256,256]{1,0:T(8,128)(2,1)} %constant.44.clone.depth_back_ref) | copy-start | bytes 393220
  24.8 11.7 %copy-start.6 = (f32[32,32,128]{2,1,0:T(8,128)S(1)}, f32[32,32,128]{2,1,0:T(8,128)}, u32[]{:S(2)}) copy-start(f32[32,32,128]{2,1,0:T(8,128)} %other_ref.1) | copy-start | bytes 1572868
  24.8 11.7 %copy-start.7 = (bf16[128,256]{1,0:T(8,128)(2,1)S(1)}, bf16[128,256]{1,0:T(8,128)(2,1)}, u32[]{:S(2)}) copy-start(bf16[128,256]{1,0:T(8,128)(2,1)} %constant.43.clone.column_back_ref) | copy-start | bytes 196612
  33.4 6.1 %copy-start.1 = (f32[32,32,128]{2,1,0:T(8,128)S(1)}, f32[32,32,128]{2,1,0:T(8,128)}, u32[]{:S(2)}) copy-start(f32[32,32,128]{2,1,0:T(8,128)} %block_ref.1) | copy-start | bytes 1572868
  39.8 11.8 %collective-permute-start.4 = (f32[16,32,128]{2,1,0:T(8,128)S(1)}, f32[16,32,128]{2,1,0:T(8,128)S(1)}, u32[]{:S(2)}, u32[]{:S(2)}) collective-permute-start(f32[16,32,128]{2,1,0:T(8,128)S(1)} %get-tuple-element.22.refs_2_.last_ref), channel_id=1, source_target_pairs={{0,16},{16,32},{32,48},{48,64},{64,80},{80,96},{96,112},{112,128},... | collective-permute-start | bytes 786440 | tf_op jit(solution)/shard_map/ppermute | solution.py:514
  40.0 11.6 %collective-permute-start.5 = (f32[15,32,128]{2,1,0:T(8,128)S(1)}, f32[15,32,128]{2,1,0:T(8,128)S(1)}, u32[]{:S(2)}, u32[]{:S(2)}) collective-permute-start(f32[15,32,128]{2,1,0:T(8,128)S(1)} %get-tuple-element.24), channel_id=1, source_target_pairs={{0,240},{16,0},{32,16},{48,32},{64,48},{80,64},{96,80},{112,96},{1... | collective-permute-start | bytes 737288 | tf_op jit(solution)/shard_map/ppermute | solution.py:515
  51.7 14.3 %collective-permute-start.7 = (f32[64,16,128]{2,1,0:T(8,128)S(1)}, f32[64,16,128]{2,1,0:T(8,128)S(1)}, u32[]{:S(2)}, u32[]{:S(2)}) collective-permute-start(f32[64,16,128]{2,1,0:T(8,128)S(1)} %edge.7), channel_id=1, source_target_pairs={{0,15},{1,0},{2,1},{3,2},{4,3},{5,4},{6,5},{7,6},{8,7},{9,8},{10,9... | collective-permute-start | bytes 1572872 | tf_op jit(solution)/shard_map/ppermute | solution.py:517
  51.8 11.8 %collective-permute-start.6 = (f32[64,16,128]{2,1,0:T(8,128)S(1)}, f32[64,16,128]{2,1,0:T(8,128)S(1)}, u32[]{:S(2)}, u32[]{:S(2)}) collective-permute-start(f32[64,16,128]{2,1,0:T(8,128)S(1)} %edge.6), channel_id=1, source_target_pairs={{0,1},{1,2},{2,3},{3,4},{4,5},{5,6},{6,7},{7,8},{8,9},{9,10},{10,1... | collective-permute-start | bytes 1572872 | tf_op jit(solution)/shard_map/ppermute | solution.py:516
